TPU v7x, 512 devices: a whole 4x4x16 slice. The times are simulated.
512 devices in a mesh: section: 2 (over x_lo), dom: 32 (over z, core), slab: 8 (over x_hi, y).
Axes of the slice: x: 4 (x_hi: 2, x_lo: 2; x = x_hi * 2 + x_lo), y: 4, z: 16, core: 2. Of those that a mesh axis runs over, the one named last changes fastest.
Arguments:
- residual: float32 [8, 1048576], P(None, ('section', 'dom', 'slab')), may hold values from -6 to 6
- coupling_tiles: float32 [8, 128, 128], replicated, may hold values from -0.1875 to 0.1875
- inverse_tiles: float32 [8, 128, 128], replicated, may hold values from -0.5 to 0.5
- diag_kind: int32 [8192], P(('section', 'dom', 'slab')), may hold values from 0 to 7
- diag_coeff: float32 [8192], P(('section', 'dom', 'slab')), may hold values from 0.5 to 4
- tile_cols: int32 [8, 8192], P(None, ('section', 'dom', 'slab')), may hold values from 0 to 19, as said below
- tile_kinds: int32 [8, 8192], P(None, ('section', 'dom', 'slab')), may hold values from 0 to 7
- tile_coeff: float32 [8, 8192], P(None, ('section', 'dom', 'slab')), may hold values from 0.25 to 2
- halo_rows: int32 [1024], P(('section', 'dom', 'slab')), may hold values from 0 to 15, as said below
- tile_owner: int32 [8192, 1], P(('section', 'dom', 'slab')), may hold values from 0 to 63; in each aligned block of 16 rows (0 to 15, 16 to 31, ...) at most 2 rows name the same one
- node_slot: int32 [8192], P(('section', 'dom', 'slab')), may hold values from 0 to 1
- edge_nodes: int32 [2, 1048576], P(None, ('section', 'dom', 'slab')), may hold values from 0 to 127, as said below
- tangents: float32 [3, 1048576], P(None, ('section', 'dom', 'slab')), may hold values from -5 to 5
- grad_blocks: float32 [1024, 128, 128], P(('section', 'dom', 'slab')), may hold values from -0.09375 to 0.09375
- vec_blocks: float32 [1024, 128, 128], P(('section', 'dom', 'slab')), may hold values from -0.1875 to 0.1875
Outputs:
- preconditioned: float32 [8, 1048576], P(None, ('section', 'dom', 'slab'))
Inputs may be any that keep to these rules, and one draw needn't show every extreme that they name: `tile_cols`: within each device's 16 tiles (local number t): row 0 names 16 + h and row 1 names 18 + h, each h < 2 named exactly 16 // 2 times in each of these rows; rows 2 to 7 name a local tile other than t. `halo_rows`: each device's 2 entries are distinct local tile numbers. `edge_nodes`: an edge's two ends differ. `tile_owner`: among the 16 tiles of one device no owner is named more than 2 times, and 2 is reached.
All inputs are finite; a program needn't handle non-finite values.
Results may differ from a plain program's by a relative error of at most 0.0001.
Values sent between devices are 32-bit elements; how exact they have to be, the bound alone decides.
No kernel may reach another device: no remote copies, remote signals or barrier semaphores. Data moves between devices by JAX's collectives and lax.ppermute only.
A program may use at most 64 MiB of HBM per device.

v0:
```python
import math

import jax
import jax.numpy as jnp
from jax import lax
from jax.sharding import PartitionSpec as P

HIGHEST = lax.Precision.HIGHEST
DAMPING = 0.7


def padded(block, sides, width):
    for axis, dim in sides:
        count = lax.axis_size(axis)
        forward = [(i, i + 1) for i in range(count - 1)]
        backward = [(target, source) for source, target in forward]
        low = lax.ppermute(
            lax.slice_in_dim(block, block.shape[dim] - width, None, axis=dim), axis, forward
        )
        high = lax.ppermute(lax.slice_in_dim(block, 0, width, axis=dim), axis, backward)
        block = jnp.concatenate([low, block, high], axis=dim)
    return block


def inverse_apply(inputs, kind_index, scales, inverse_tiles):
    matrices = jnp.take(inverse_tiles, kind_index, axis=0)
    products = jnp.einsum("ktj,tij->kti", inputs, matrices, precision=HIGHEST)
    return products / scales[None, :, None]


def nodal_solve(gathered, grad_blocks, vec_blocks):
    grad_part = jnp.einsum("nij,nkj->nki", grad_blocks, gathered[:, 0], precision=HIGHEST)
    vec_part = jnp.einsum("nij,nckj->ncki", vec_blocks, gathered[:, 1:], precision=HIGHEST)
    return jnp.concatenate([grad_part[:, None], vec_part], axis=1)


def in_blocks(func, count, arrays):
    width = math.gcd(count, 8)
    shaped = tuple((item.reshape((count // width, width) + item.shape[1:]) for item in arrays))
    result = lax.map(lambda pieces: func(*pieces), shaped)
    return result.reshape((count,) + result.shape[2:])


def end_table(ends):
    nodes = jnp.arange(ends.shape[1], dtype=jnp.int32)
    return (ends[:, :, None] == nodes[None, None, :]).astype(jnp.float32)


def to_nodes(ends_first, ends_second, weight_first, weight_second, rows):
    data_first = weight_first[:, :, None, :] * rows[:, None]
    data_second = weight_second[:, :, None, :] * rows[:, None]
    total = jnp.einsum("tbn,tckb->tckn", end_table(ends_first), data_first, precision=HIGHEST)
    return total + jnp.einsum(
        "tbn,tckb->tckn", end_table(ends_second), data_second, precision=HIGHEST
    )


def from_nodes(ends_first, ends_second, weight_first, weight_second, values):
    at_first = jnp.einsum("tbn,tckn->tckb", end_table(ends_first), values, precision=HIGHEST)
    at_second = jnp.einsum("tbn,tckn->tckb", end_table(ends_second), values, precision=HIGHEST)
    return jnp.sum(
        weight_first[:, :, None, :] * at_first + weight_second[:, :, None, :] * at_second, axis=1
    )


def body(
    residual,
    coupling_tiles,
    inverse_tiles,
    diag_kind,
    diag_coeff,
    tile_cols,
    tile_kinds,
    tile_coeff,
    halo_rows,
    tile_owner,
    node_slot,
    edge_nodes,
    tangents,
    grad_blocks,
    vec_blocks,
):
    cases = residual.shape[0]
    tile_width = coupling_tiles.shape[1]
    kind_count = coupling_tiles.shape[0]
    local_tiles = diag_kind.shape[0]
    node_tiles = grad_blocks.shape[0]
    edge_rows = residual.reshape(cases, local_tiles, tile_width)
    positions = jnp.arange(local_tiles, dtype=jnp.int32)
    smoothed = inverse_apply(edge_rows, diag_kind, diag_coeff, inverse_tiles)
    rim_values = jnp.take(smoothed, halo_rows, axis=1)[None]
    near_values = padded(rim_values, (("slab", 0),), 1)
    from_lower, from_upper = (near_values[0], near_values[2])
    sources = jnp.concatenate([smoothed, from_lower, from_upper], axis=1)
    source_count = sources.shape[1]
    coupled = jnp.einsum("ksj,qij->qski", sources, coupling_tiles, precision=HIGHEST).reshape(
        kind_count * source_count, cases, tile_width
    )
    diagonal_part = (
        jnp.take(coupled, diag_kind * source_count + positions, axis=0) * diag_coeff[:, None, None]
    )
    beside = jnp.take(coupled, (tile_kinds * source_count + tile_cols).reshape(-1), axis=0).reshape(
        tile_cols.shape[0], local_tiles, cases, tile_width
    )
    applied = diagonal_part + jnp.sum(beside * tile_coeff[:, :, None, None], axis=0)
    smoothed_twice = smoothed + DAMPING * inverse_apply(
        edge_rows - applied.transpose(1, 0, 2), diag_kind, diag_coeff, inverse_tiles
    )
    owners = lax.axis_size(("section", "dom"))
    capacity = max(2, 3 * local_tiles // (2 * owners))
    slots_total = owners * capacity
    owner_of = tile_owner[:, 0]
    owner_hot = (owner_of[:, None] == jnp.arange(owners, dtype=jnp.int32)[None, :]).astype(
        jnp.int32
    )
    ranks = jnp.sum(jnp.cumsum(owner_hot, axis=0) * owner_hot, axis=1) - 1
    places = owner_of * capacity + ranks
    slot_tile = jax.ops.segment_sum(positions + 1, places, slots_total) - 1
    slot_filled = (slot_tile >= 0).astype(jnp.float32)
    slot_source = jnp.maximum(slot_tile, 0)
    ends_first = edge_nodes[0].reshape(local_tiles, tile_width)
    ends_second = edge_nodes[1].reshape(local_tiles, tile_width)
    halves = 0.5 * tangents.reshape(3, local_tiles, tile_width).transpose(1, 0, 2)
    unit_row = jnp.ones((local_tiles, 1, tile_width), jnp.float32)
    weight_first = jnp.concatenate([-unit_row, halves], axis=1)
    weight_second = jnp.concatenate([unit_row, halves], axis=1)
    tile_major = edge_rows.transpose(1, 0, 2)
    partials = in_blocks(
        to_nodes, local_tiles, (ends_first, ends_second, weight_first, weight_second, tile_major)
    )
    outgoing = (jnp.take(partials, slot_source, axis=0) * slot_filled[:, None, None, None]).reshape(
        owners, capacity, 4, cases, tile_width
    )
    outgoing_slot = (jnp.take(node_slot, slot_source).astype(jnp.float32) * slot_filled).reshape(
        owners, capacity
    )
    arrived, arrived_slot = (
        lax.all_to_all(outgoing, ("section", "dom"), split_axis=0, concat_axis=0, tiled=True),
        lax.all_to_all(outgoing_slot, ("section", "dom"), split_axis=0, concat_axis=0, tiled=True),
    )
    slot_hot = (
        arrived_slot.reshape(-1)[:, None] == jnp.arange(node_tiles, dtype=jnp.float32)[None, :]
    ).astype(jnp.float32)
    gathered = jnp.einsum(
        "sn,sckb->nckb",
        slot_hot,
        arrived.reshape(slots_total, 4, cases, tile_width),
        precision=HIGHEST,
    )
    solved = nodal_solve(gathered, grad_blocks, vec_blocks)
    returning = jnp.einsum("sn,nckb->sckb", slot_hot, solved, precision=HIGHEST).reshape(
        owners, capacity, 4, cases, tile_width
    )
    returned = lax.all_to_all(
        returning, ("section", "dom"), split_axis=0, concat_axis=0, tiled=True
    )
    at_tiles = jnp.take(returned.reshape(slots_total, 4, cases, tile_width), places, axis=0)
    back_tiles = in_blocks(
        from_nodes, local_tiles, (ends_first, ends_second, weight_first, weight_second, at_tiles)
    )
    correction = back_tiles.transpose(1, 0, 2)
    return (smoothed_twice + correction).reshape(cases, local_tiles * tile_width)


def solution(mesh):
    placed = (
        P(None, ("section", "dom", "slab")),
        P(),
        P(),
        P(("section", "dom", "slab")),
        P(("section", "dom", "slab")),
        P(None, ("section", "dom", "slab")),
        P(None, ("section", "dom", "slab")),
        P(None, ("section", "dom", "slab")),
        P(("section", "dom", "slab")),
        P(("section", "dom", "slab"), None),
        P(("section", "dom", "slab")),
        P(None, ("section", "dom", "slab")),
        P(None, ("section", "dom", "slab")),
        P(("section", "dom", "slab"), None, None),
        P(("section", "dom", "slab"), None, None),
    )
    return jax.shard_map(
        body,
        mesh=mesh,
        in_specs=placed,
        out_specs=P(None, ("section", "dom", "slab")),
        check_vma=False,
    )
```

profile of v0, /device:TPU:24, one launch (start us, length us, event | category | flops | bytes accessed | tf_op | source)
XLA Modules:
  0.0 274.7 jit_solution(3632772431733349455)
XLA Ops:
  0.0 2.0 fusion.72
  2.7 0.8 select_reduce_fusion
  4.9 10.0 %compare_select_fusion.21 = f32[128]{0:T(128)S(1)} fusion(s32[128]{0:T(128)S(1)} %scatter_custom_fusion, s32[]{:T(128)} %bitcast.55, s32[]{:T(128)} %bitcast.40, s32[]{:T(128)} %bitcast.41, s32[]{:T(128)} %bitcast.42, s32[]{:T(128)} %bitcast.43, s32[]{:T(128)} %bitcast.44, s32[]{:T(128)} %bitcast.45, s32[]{:T(128)} %bitcast.46, s32[]{:T(128)} %bitcast.47, ...), kind=kLoop, calls=%fused_computation.130 | loop fusion | flops 4608 | bytes 1088 | tf_op jit(solution)/shard_map/mul | solution.py:134
  15.7 17.0 %all-to-all-start = ((f32[64,1,2]{2,1,0:T(1,128)}), f32[64,1,2]{2,1,0:T(1,128)S(1)}, u32[]{:S(2)}, u32[]{:S(2)}) async-start(f32[64,1,2]{2,1,0:T(1,128)} %bitcast.56), calls=%async_computation | async-start | bytes 65536 | tf_op jit(solution)/shard_map/all_to_all | solution.py:139
  33.6 0.8 fusion.71
  34.4 3.5 %while.20 = (s32[]{:T(128)}, f32[2,8,4,8,128]{4,3,2,1,0:T(8,128)S(1)}, f32[2,8,4,128]{3,2,1,0:T(4,128)S(1)}, f32[2,8,8,128]{3,2,1,0:T(8,128)}, s32[2,8,128]{2,1,...) while((s32[]{:T(128)}, f32[2,8,4,8,128]{4,3,2,1,0:T(8,128)S(1)}, ...), condition=%wide.region_5.7_spmd, body=%wide.region_4.6_spmd.sunk | while | flops 101023744 | bytes 647269 | solution.py:40
  38.2 0.8 gather_fusion.3
  39.3 3.2 %copy.43 = f32[64,2,4,8,128]{4,1,3,2,0:T(2,128)} copy(f32[64,2,4,8,128]{4,3,2,1,0:T(8,128)S(1)} %select_multiply_fusion) | data formatting | bytes 4194304 | tf_op jit(solution)/shard_map/mul | solution.py:131
  42.5 3.5 %all-to-all-done = f32[64,1,2]{2,1,0:T(1,128)S(1)} async-done(((f32[64,1,2]{2,1,0:T(1,128)}), f32[64,1,2]{2,1,0:T(1,128)S(1)}, u32[]{:S(2)}, u32[]{:S(2)}) %all-to-all-start) | async-done | bytes 544 | tf_op jit(solution)/shard_map/all_to_all | solution.py:139
  46.0 10.2 %all-to-all-start.1 = ((f32[64,2,4,8,128]{4,1,3,2,0:T(2,128)}), f32[64,2,4,8,128]{4,1,3,2,0:T(2,128)S(1)}, u32[]{:S(2)}, u32[]{:S(2)}) async-start(f32[64,2,4,8,128]{4,1,3,2,0:T(2,128)} %copy.43), calls=%async_computation.1 | async-start | bytes 4194304 | tf_op jit(solution)/shard_map/all_to_all | solution.py:138
  57.6 95.3 %all-to-all-done.1 = f32[64,2,4,8,128]{4,1,3,2,0:T(2,128)S(1)} async-done(((f32[64,2,4,8,128]{4,1,3,2,0:T(2,128)}), f32[64,2,4,8,128]{4,1,3,2,0:T(2,128)S(1)}, u32[]{:S(2)}, u32[]{:S(2)}) %all-to-all-start.1) | async-done | bytes 2097184 | tf_op jit(solution)/shard_map/all_to_all | solution.py:138
  152.9 1.1 copy.44
  155.6 1.1 fusion.50
  156.7 2.5 copy.49
  159.2 8.8 %all-to-all-start.2 = ((f32[64,2,4,8,128]{4,1,3,2,0:T(2,128)}), f32[64,2,4,8,128]{4,1,3,2,0:T(2,128)}, u32[]{:S(2)}, u32[]{:S(2)}) async-start(f32[64,2,4,8,128]{4,1,3,2,0:T(2,128)} %copy.49), calls=%async_computation.2 | async-start | bytes 4194304 | tf_op jit(solution)/shard_map/all_to_all | solution.py:154
  168.9 1.8 fusion.32
  171.3 4.3 %collective-permute-start = (f32[1,8,2,128]{3,1,2,0:T(8,128)S(1)}, f32[1,8,2,128]{3,1,2,0:T(8,128)S(1)}, u32[]{:S(2)}, u32[]{:S(2)}) collective-permute-start(f32[1,8,2,128]{3,1,2,0:T(8,128)S(1)} %bitcast_select_fusion), channel_id=1, source_target_pairs={{0,1},{1,2},{2,3},{3,4},{4,5},{5,6},{6,7},{8,9},{9,10},{10,11},{11... | collective-permute-start | bytes 24584 | tf_op jit(solution)/shard_map/ppermute | solution.py:17
  175.6 1.9 collective-permute-start.1
  177.8 7.0 %collective-permute-done.1 = f32[1,8,2,128]{3,1,2,0:T(8,128)S(1)} collective-permute-done((f32[1,8,2,128]{3,1,2,0:T(8,128)S(1)}, f32[1,8,2,128]{3,1,2,0:T(8,128)S(1)}, u32[]{:S(2)}, u32[]{:S(2)}) %collective-permute-start.1) | collective-permute-done | bytes 8224 | tf_op jit(solution)/shard_map/ppermute | solution.py:20
  187.7 76.6 %all-to-all-done.2 = f32[64,2,4,8,128]{4,1,3,2,0:T(2,128)} async-done(((f32[64,2,4,8,128]{4,1,3,2,0:T(2,128)}), f32[64,2,4,8,128]{4,1,3,2,0:T(2,128)}, u32[]{:S(2)}, u32[]{:S(2)}) %all-to-all-start.2) | async-done | bytes 2097184 | tf_op jit(solution)/shard_map/all_to_all | solution.py:154
  264.3 3.2 %copy.50 = f32[64,2,4,8,128]{4,3,2,1,0:T(8,128)} copy(f32[64,2,4,8,128]{4,1,3,2,0:T(2,128)} %all-to-all-done.2) | data formatting | bytes 4194304 | tf_op jit(solution)/shard_map/all_to_all | solution.py:154
  267.5 2.2 gather_fusion.4
  269.7 2.5 while.21
  272.3 2.4 fusion.34
  (92 shorter events, 17.6 us)
Async XLA Ops:
  0.0 168.1 %copy-start = (f32[8,128,128]{2,1,0:T(8,128)S(1)}, f32[8,128,128]{2,1,0:T(8,128)}, u32[]{:S(2)}) copy-start(f32[8,128,128]{2,1,0:T(8,128)} %param.23) | copy-start | bytes 1572868
  15.7 30.4 %all-to-all-start = ((f32[64,1,2]{2,1,0:T(1,128)}), f32[64,1,2]{2,1,0:T(1,128)S(1)}, u32[]{:S(2)}, u32[]{:S(2)}) async-start(f32[64,1,2]{2,1,0:T(1,128)} %bitcast.56), calls=%async_computation | async-start | bytes 65536 | tf_op jit(solution)/shard_map/all_to_all | solution.py:139
  46.0 106.9 %all-to-all-start.1 = ((f32[64,2,4,8,128]{4,1,3,2,0:T(2,128)}), f32[64,2,4,8,128]{4,1,3,2,0:T(2,128)S(1)}, u32[]{:S(2)}, u32[]{:S(2)}) async-start(f32[64,2,4,8,128]{4,1,3,2,0:T(2,128)} %copy.43), calls=%async_computation.1 | async-start | bytes 4194304 | tf_op jit(solution)/shard_map/all_to_all | solution.py:138
  154.1 0.9 copy-start.4
  154.1 1.2 copy-start.3
  159.2 8.8 %copy-start.9 = (s32[16]{0:T(128)S(1)}, s32[16]{0:T(128)}, u32[]{:S(2)}) copy-start(s32[16]{0:T(128)} %param.24) | copy-start | bytes 196
  159.2 105.1 %all-to-all-start.2 = ((f32[64,2,4,8,128]{4,1,3,2,0:T(2,128)}), f32[64,2,4,8,128]{4,1,3,2,0:T(2,128)}, u32[]{:S(2)}, u32[]{:S(2)}) async-start(f32[64,2,4,8,128]{4,1,3,2,0:T(2,128)} %copy.49), calls=%async_computation.2 | async-start | bytes 4194304 | tf_op jit(solution)/shard_map/all_to_all | solution.py:154
  168.0 0.7 copy-start.10
  168.0 0.8 copy-start.1
  168.0 0.8 copy-start.8
  168.1 9.5 %copy-start.6 = (s32[8,16]{1,0:T(8,128)S(1)}, s32[8,16]{1,0:T(8,128)}, u32[]{:S(2)}) copy-start(s32[8,16]{1,0:T(8,128)} %param.26) | copy-start | bytes 1540
  168.1 9.5 %copy-start.7 = (s32[8,16]{1,0:T(8,128)S(1)}, s32[8,16]{1,0:T(8,128)}, u32[]{:S(2)}) copy-start(s32[8,16]{1,0:T(8,128)} %param.27) | copy-start | bytes 1540
  168.1 16.7 %copy-start.2 = (f32[8,128,128]{2,1,0:T(8,128)S(1)}, f32[8,128,128]{2,1,0:T(8,128)}, u32[]{:S(2)}) copy-start(f32[8,128,128]{2,1,0:T(8,128)} %param.22) | copy-start | bytes 1572868
  171.3 6.5 %collective-permute-start = (f32[1,8,2,128]{3,1,2,0:T(8,128)S(1)}, f32[1,8,2,128]{3,1,2,0:T(8,128)S(1)}, u32[]{:S(2)}, u32[]{:S(2)}) collective-permute-start(f32[1,8,2,128]{3,1,2,0:T(8,128)S(1)} %bitcast_select_fusion), channel_id=1, source_target_pairs={{0,1},{1,2},{2,3},{3,4},{4,5},{5,6},{6,7},{8,9},{9,10},{10,11},{11... | collective-permute-start | bytes 24584 | tf_op jit(solution)/shard_map/ppermute | solution.py:17
  175.6 9.2 %collective-permute-start.1 = (f32[1,8,2,128]{3,1,2,0:T(8,128)S(1)}, f32[1,8,2,128]{3,1,2,0:T(8,128)S(1)}, u32[]{:S(2)}, u32[]{:S(2)}) collective-permute-start(f32[1,8,2,128]{3,1,2,0:T(8,128)S(1)} %bitcast_select_fusion), channel_id=1, source_target_pairs={{1,0},{2,1},{3,2},{4,3},{5,4},{6,5},{7,6},{9,8},{10,9},{11,10},{12... | collective-permute-start | bytes 24584 | tf_op jit(solution)/shard_map/ppermute | solution.py:20
  184.8 2.5 copy-start.5
where the time goes:
time: 277 us; the launch traced here: 275 us
  waiting for transfers between devices  182 us (66%)
  starting transfers between devices  42.2 us (15%)
  local copies, waits for them, and re-layouts  22.4 us (8%)
  other arithmetic  15.4 us (6%)
  matrix products  11.7 us (4%)
    all_to_all x1, waiting for transfers between devices, body(): lax.all_to_all(outgoing, ('section', 'dom'), split_axis=0, concat_axis=0,...  95.3 us
    all_to_all x1, waiting for transfers between devices, body(): lax.all_to_all(returning, ('section', 'dom'), split_axis=0, concat_axis=0...  76.6 us
    all_to_all x1, starting transfers between devices, body(): lax.all_to_all(outgoing_slot, ('section', 'dom'), split_axis=0, concat_ax...  17 us
    all_to_all x1, starting transfers between devices, body(): lax.all_to_all(outgoing, ('section', 'dom'), split_axis=0, concat_axis=0,...  10.2 us
    mul x1, other arithmetic, body(): jnp.take(node_slot, slot_source).astype(jnp.float32) * slot_filled  10 us
    all_to_all x1, starting transfers between devices, body(): lax.all_to_all(returning, ('section', 'dom'), split_axis=0, concat_axis=0...  8.82 us
    ppermute x1, waiting for transfers between devices, padded(): lax.ppermute(lax.slice_in_dim(block, 0, width, axis=dim), axis, backward)  6.96 us
  transfers between devices with their start and end apart: 5, of which 4 were waited for; matrix products, arithmetic and copies ran while one was open for 6% of the time, Pallas kernels for 0%

commit v1 on v0

v1 whole, which is shorter than its diff:
```python
import functools

import jax
import jax.numpy as jnp
from jax import lax
from jax.experimental import pallas as pl
from jax.experimental.pallas import tpu as pltpu
from jax.sharding import Mesh, PartitionSpec as P

DAMPING = 0.7
CORES = 2
F32 = jnp.float32
BF16 = jnp.bfloat16
SMEM = pltpu.SMEM
VMEM = pltpu.VMEM

vmem_spec = pl.BlockSpec(memory_space=VMEM)
smem_spec = pl.BlockSpec(memory_space=SMEM)
any_spec = pl.BlockSpec(memory_space=pl.ANY)


def split(x):
    high = x.astype(BF16)
    low = (x - high.astype(F32)).astype(BF16)
    return high, low


def dot_nt(a, b):
    return lax.dot_general(a, b, (((1,), (1,)), ((), ())), preferred_element_type=F32)


def product_nt(parts, matrix):
    count = parts.shape[0] // 2
    high, low = split(matrix)
    both = dot_nt(parts, high)
    return both[:count] + both[count:] + dot_nt(parts[:count], low)


def stacked(rows):
    high, low = split(rows)
    return jnp.concatenate([high, low], axis=0)


def pack_kernel(owner, slot, residual, tangents, ends, out):
    tiles, width = out.shape[0], out.shape[2]
    lanes = lax.broadcasted_iota(jnp.int32, (1, width), 1)
    row = jnp.zeros((1, width), jnp.int32)
    for t in range(tiles):
        row = jnp.where(lanes == t, owner[t] * 2 + slot[t], row)
    for t in range(tiles):
        part = slice(t * width, (t + 1) * width)
        out[t, 0:8, :] = residual[:, part]
        out[t, 8:11, :] = tangents[:, part]
        out[t, 11:13, :] = ends[:, part].astype(F32)
        out[t, 13:14, :] = row.astype(F32)


def pack(owner, slot, residual, tangents, ends):
    tiles = owner.shape[0]
    width = residual.shape[1] // tiles
    return pl.pallas_call(
        pack_kernel,
        out_shape=jax.ShapeDtypeStruct((tiles, 16, width), F32),
        in_specs=[smem_spec, smem_spec, vmem_spec, vmem_spec, vmem_spec],
        out_specs=vmem_spec,
        name="pack",
    )(owner, slot, residual, tangents, ends)


def sums_kernel(
    where, own, first, second, third, sums, chosen, buf, meta, sems, msems, *, sections_stride, tiles, group
):
    sources = (own, first, second, third)
    copies = []
    for q, src in enumerate(sources):
        copies.append(
            pltpu.make_async_copy(src.at[0, pl.ds(8, 8), :], meta.at[q], msems.at[q])
        )
        copies[-1].start()
    data = []
    for q, src in enumerate(sources):
        data.append(pltpu.make_async_copy(src, buf.at[pl.ds(q * tiles, tiles)], sems.at[q]))
        data[-1].start()
    trash = sums.shape[0] - 1
    sums[...] = jnp.zeros_like(sums)
    for copy in copies:
        copy.wait()
    my_section, my_core = where[0], where[1]

    count = jnp.int32(0)
    for q in range(4):
        for t in range(tiles):
            dst = meta[q, 5, t].astype(jnp.int32)
            owner = dst // 2
            mine = (owner // sections_stride == my_section) & (owner % CORES == my_core)
            local = ((owner % sections_stride) // CORES) * 2 + dst % 2
            chosen[0, count + 1] = q * tiles + t
            chosen[1, count + 1] = local
            count = jnp.where(mine, count + 1, count)
    chosen[0, 0] = count
    for extra in range(group):
        chosen[0, count + 1 + extra] = 0
        chosen[1, count + 1 + extra] = trash
    for copy in data:
        copy.wait()
    width = buf.shape[2]
    nodes = lax.broadcasted_iota(jnp.int32, (width, width), 0).astype(F32)

    def step(i, carry):
        for j in range(group):
            at = i * group + j + 1
            tile, local = chosen[0, at], chosen[1, at]
            rows = buf[tile, 0:8, :]
            halves = 0.5 * buf[tile, 8:11, :]
            at_a = (nodes == buf[tile, 11:12, :]).astype(F32)
            at_b = (nodes == buf[tile, 12:13, :]).astype(F32)
            plus = (at_a + at_b).astype(BF16)
            minus = (at_b - at_a).astype(BF16)
            vec = jnp.concatenate([halves[c : c + 1] * rows for c in range(3)], axis=0)
            total_vec = dot_nt(stacked(vec), plus)
            total_grad = dot_nt(stacked(rows), minus)
            sums[local, 0:8, :] += total_grad[:8] + total_grad[8:]
            sums[local, 8:32, :] += total_vec[:24] + total_vec[24:]
        return carry

    lax.fori_loop(0, (count + group - 1) // group, step, 0)


def node_sums(where, payloads, places, sections_stride):
    tiles, _, width = payloads[0].shape
    group = 4
    return pl.pallas_call(
        functools.partial(
            sums_kernel, sections_stride=sections_stride, tiles=tiles, group=group
        ),
        out_shape=(
            jax.ShapeDtypeStruct((places + 1, 32, width), F32),
            jax.ShapeDtypeStruct((2, 4 * tiles + 1 + group), jnp.int32),
        ),
        in_specs=[smem_spec] + [any_spec] * 4,
        out_specs=(vmem_spec, smem_spec),
        scratch_shapes=[
            VMEM((4 * tiles, 16, width), F32),
            SMEM((4, 8, width), F32),
            pltpu.SemaphoreType.DMA((4,)),
            pltpu.SemaphoreType.DMA((4,)),
        ],
        name="node_sums",
    )(where, *payloads)


def solve_kernel(arrived, grad, vec, out):
    count = arrived.shape[0]
    for n in range(grad.shape[0]):
        rows = arrived[0, n]
        for z in range(1, count):
            rows = rows + arrived[z, n]
        out[n, 0:8, :] = product_nt(stacked(rows[:8]), grad[n])
        out[n, 8:32, :] = product_nt(stacked(rows[8:]), vec[n])


def solve(arrived, grad, vec):
    return pl.pallas_call(
        solve_kernel,
        out_shape=jax.ShapeDtypeStruct(arrived.shape[1:], F32),
        in_specs=[vmem_spec] * 3,
        out_specs=vmem_spec,
        name="solve",
    )(arrived, grad, vec)


def back_kernel(chosen, own, first, second, third, values, out, buf, sems, *, tiles):
    data = []
    for q, src in enumerate((own, first, second, third)):
        data.append(
            pltpu.make_async_copy(
                src.at[:, pl.ds(8, 8), :], buf.at[pl.ds(q * tiles, tiles)], sems.at[q]
            )
        )
        data[-1].start()
    out[...] = jnp.zeros_like(out)
    for copy in data:
        copy.wait()
    width = buf.shape[2]

    def pick(rows, index):
        return jnp.take_along_axis(rows, index, axis=1)

    def step(i, carry):
        tile, local = chosen[0, i + 1], chosen[1, i + 1]
        index_a = jnp.broadcast_to(buf[tile, 3:4, :].astype(jnp.int32), (8, width))
        index_b = jnp.broadcast_to(buf[tile, 4:5, :].astype(jnp.int32), (8, width))
        grad = values[local, 0:8, :]
        total = pick(grad, index_b) - pick(grad, index_a)
        for c in range(3):
            rows = values[local, 8 + 8 * c : 16 + 8 * c, :]
            half = 0.5 * buf[tile, c : c + 1, :]
            total = total + half * (pick(rows, index_a) + pick(rows, index_b))
        out[tile] = total
        return carry

    lax.fori_loop(0, chosen[0, 0], step, 0)


def back(chosen, payloads, values):
    tiles, _, width = payloads[0].shape
    return pl.pallas_call(
        functools.partial(back_kernel, tiles=tiles),
        out_shape=jax.ShapeDtypeStruct((4 * tiles, 8, width), F32),
        in_specs=[smem_spec] + [any_spec] * 4 + [vmem_spec],
        out_specs=vmem_spec,
        scratch_shapes=[VMEM((4 * tiles, 8, width), F32), pltpu.SemaphoreType.DMA((4,))],
        name="back",
    )(chosen, *payloads, values)


def by_tile(ref, tiles, width):
    return jnp.concatenate([ref[:, t * width : (t + 1) * width] for t in range(tiles)], axis=0)


def smooth_kernel(kind, coeff, halo, residual, inverse, out, rim, work):
    tiles, _, width = out.shape
    parts = stacked(by_tile(residual, tiles, width))
    for k in range(inverse.shape[0]):
        work[k] = product_nt(parts, inverse[k]).reshape(tiles, 8, width)
    for t in range(tiles):
        out[t] = work[kind[t], t] / coeff[t]
    for h in range(rim.shape[0]):
        rim[h] = out[halo[h]]


def smooth(kind, coeff, halo, residual, inverse):
    tiles = kind.shape[0]
    kinds, width, _ = inverse.shape
    return pl.pallas_call(
        smooth_kernel,
        out_shape=(
            jax.ShapeDtypeStruct((tiles, 8, width), F32),
            jax.ShapeDtypeStruct((halo.shape[0], 8, width), F32),
        ),
        in_specs=[smem_spec] * 3 + [vmem_spec] * 2,
        out_specs=(vmem_spec, vmem_spec),
        scratch_shapes=[VMEM((kinds, tiles, 8, width), F32)],
        name="smooth_once",
    )(kind, coeff, halo, residual, inverse)


def again_kernel(
    kind, coeff, cols, kinds, coeffs, smoothed, low, high, residual, coupling, inverse, out, work, rest
):
    tiles, _, width = smoothed.shape
    sources = jnp.concatenate(
        [
            smoothed[...].reshape(tiles * 8, width),
            low[...].reshape(low.shape[0] * 8, width),
            high[...].reshape(high.shape[0] * 8, width),
        ],
        axis=0,
    )
    parts = stacked(sources)
    count = sources.shape[0] // 8
    for k in range(coupling.shape[0]):
        work[k] = product_nt(parts, coupling[k]).reshape(count, 8, width)
    for t in range(tiles):
        total = coeff[t] * work[kind[t], t]
        for m in range(cols.shape[0]):
            total = total + coeffs[m, t] * work[kinds[m, t], cols[m, t]]
        rest[t] = residual[:, t * width : (t + 1) * width] - total
    parts = stacked(rest[...].reshape(tiles * 8, width))
    for k in range(inverse.shape[0]):
        work[k, 0:tiles] = product_nt(parts, inverse[k]).reshape(tiles, 8, width)
    for t in range(tiles):
        out[t] = smoothed[t] + DAMPING * (work[kind[t], t] / coeff[t])


def smooth_again(kind, coeff, cols, kinds, coeffs, smoothed, low, high, residual, coupling, inverse):
    tiles, _, width = smoothed.shape
    count = tiles + low.shape[0] + high.shape[0]
    return pl.pallas_call(
        again_kernel,
        out_shape=jax.ShapeDtypeStruct((tiles, 8, width), F32),
        in_specs=[smem_spec] * 5 + [vmem_spec] * 6,
        out_specs=vmem_spec,
        scratch_shapes=[
            VMEM((coupling.shape[0], count, 8, width), F32),
            VMEM((tiles, 8, width), F32),
        ],
        name="smooth_again",
    )(kind, coeff, cols, kinds, coeffs, smoothed, low, high, residual, coupling, inverse)


def finish_kernel(smoothed, own, first, second, third, out):
    tiles, _, width = smoothed.shape
    for t in range(tiles):
        out[:, t * width : (t + 1) * width] = smoothed[t] + (
            (own[t] + first[t]) + (second[t] + third[t])
        )


def finish(smoothed, pieces):
    tiles, cases, width = smoothed.shape
    return pl.pallas_call(
        finish_kernel,
        out_shape=jax.ShapeDtypeStruct((cases, tiles * width), F32),
        in_specs=[vmem_spec] * 5,
        out_specs=vmem_spec,
        name="finish",
    )(smoothed, *pieces)


def swap(x, which):
    return lax.ppermute(x, ("section", "core"), [(i, i ^ which) for i in range(4)])


def body(
    residual,
    coupling_tiles,
    inverse_tiles,
    diag_kind,
    diag_coeff,
    tile_cols,
    tile_kinds,
    tile_coeff,
    halo_rows,
    tile_owner,
    node_slot,
    edge_nodes,
    tangents,
    grad_blocks,
    vec_blocks,
):
    heights = lax.axis_size("z")
    node_tiles = grad_blocks.shape[0]
    tiles = diag_kind.shape[0]
    width = coupling_tiles.shape[1]
    where = jnp.stack([lax.axis_index("section"), lax.axis_index("core")]).astype(jnp.int32)
    own = pack(tile_owner[:, 0], node_slot, residual, tangents, edge_nodes)
    payloads = [own] + [swap(own, which) for which in (1, 2, 3)]

    smoothed, rim = smooth(diag_kind, diag_coeff, halo_rows, residual, inverse_tiles)
    slabs = lax.axis_size("slab")
    low = lax.ppermute(rim, "slab", [(i, i + 1) for i in range(slabs - 1)])
    high = lax.ppermute(rim, "slab", [(i + 1, i) for i in range(slabs - 1)])

    sums, chosen = node_sums(where, payloads, heights * node_tiles, heights * CORES)
    sums = sums[: heights * node_tiles].reshape(heights, node_tiles * 32, width)
    arrived = lax.all_to_all(sums, "z", split_axis=0, concat_axis=0, tiled=True)

    smoothed_twice = smooth_again(
        diag_kind, diag_coeff, tile_cols, tile_kinds, tile_coeff,
        smoothed, low, high, residual, coupling_tiles, inverse_tiles,
    )

    solved = solve(arrived.reshape(heights, node_tiles, 32, width), grad_blocks, vec_blocks)
    values = lax.all_gather(solved, "z", tiled=True)
    corrections = back(chosen, payloads, values).reshape(4, tiles, 8, width)
    pieces = [corrections[0]] + [swap(corrections[which], which) for which in (1, 2, 3)]
    return finish(smoothed_twice, pieces)


def solution(mesh):
    names = ("section", "z", "core", "slab")
    sections, doms, slabs = (mesh.shape[name] for name in ("section", "dom", "slab"))
    inner = Mesh(mesh.devices.reshape(sections, doms // CORES, CORES, slabs), names)
    rows, cols = P(names), P(None, names)
    placed = (
        cols, P(), P(), rows, rows, cols, cols, cols, rows, rows, rows, cols, cols, rows, rows,
    )
    return jax.shard_map(
        body, mesh=inner, in_specs=placed, out_specs=cols, check_vma=False
    )
```

time: 277 us -> 140 us (0.51)
  waiting for transfers between devices: 182 us -> 12.1 us
  blocking collectives: 0 us -> 80.3 us
  starting transfers between devices: 42.2 us -> 21.8 us
  Pallas kernels: 0 us -> 19.5 us
  local copies, waits for them, and re-layouts: 22.4 us -> 4.54 us
  other arithmetic: 15.4 us -> 0.61 us
  matrix products: 11.7 us -> 0 us
    all_to_all x3 -> x0, waiting for transfers between devices: 175 us -> none  [the longest x1 95.3 us: body(): lax.all_to_all(outgoing, ('section', 'dom'), split_axis=0, concat_axis=0,...]
    all_to_all x0 -> x1, blocking collectives: none -> 44.3 us  [body(): arrived = lax.all_to_all(sums, 'z', split_axis=0, concat_axis=0, tiled=True)]
    all_gather x0 -> x1, blocking collectives: none -> 36.1 us  [body(): values = lax.all_gather(solved, 'z', tiled=True)]
    all_to_all x3 -> x0, starting transfers between devices: 36 us -> none  [the longest x1 17 us: body(): lax.all_to_all(outgoing_slot, ('section', 'dom'), split_axis=0, concat_ax...]
    pallas_call x0 -> x7, Pallas kernels: none -> 19.5 us  [the longest x1 5.19 us: node_sums(): pl.pallas_call(functools.partial(sums_kernel, sections_stride=sections_st...]
    ppermute x2 -> x8, starting transfers between devices: 6.21 us -> 21.8 us  [the longest x6 16 us: swap(): lax.ppermute(x, ('section', 'core'), [(i, i ^ which) for i in range(4)])]
    dot_general x15 -> x0, matrix products: 11.7 us -> none  [the longest x2 4.25 us: inverse_apply(): products = jnp.einsum('ktj,tij->kti', inputs, matrices, precision=HIGHEST)]
    mul x3 -> x0, other arithmetic: 11.1 us -> none  [the longest x1 10 us: body(): jnp.take(node_slot, slot_source).astype(jnp.float32) * slot_filled]
  transfers between devices with their start and end apart: 5 -> 8, of which waited for: 4 -> 3; matrix products, arithmetic and copies ran while one was open for 6% -> 0% of each run, Pallas kernels for 0% -> 4%
where the time goes in v1:
time: 140 us; the launch traced here: 139 us
  blocking collectives  80.3 us (57%)
  starting transfers between devices  21.8 us (16%)
  Pallas kernels  19.5 us (14%)
  waiting for transfers between devices  12.1 us (9%)
  local copies, waits for them, and re-layouts  4.54 us (3%)
    all_to_all x1, blocking collectives, body(): arrived = lax.all_to_all(sums, 'z', split_axis=0, concat_axis=0, tiled=True)  44.3 us
    all_gather x1, blocking collectives, body(): values = lax.all_gather(solved, 'z', tiled=True)  36.1 us
    ppermute x6, starting transfers between devices, swap(): lax.ppermute(x, ('section', 'core'), [(i, i ^ which) for i in range(4)])  16 us
    ppermute x1, waiting for transfers between devices, body(): high = lax.ppermute(rim, 'slab', [(i + 1, i) for i in range(slabs - 1)])  7.38 us
    pallas_call x1, Pallas kernels, node_sums(): pl.pallas_call(functools.partial(sums_kernel, sections_stride=sections_st...  5.19 us
    ppermute x6, waiting for transfers between devices, swap(): lax.ppermute(x, ('section', 'core'), [(i, i ^ which) for i in range(4)])  4.7 us
    ppermute x1, starting transfers between devices, body(): low = lax.ppermute(rim, 'slab', [(i, i + 1) for i in range(slabs - 1)])  3.87 us
    pallas_call x1, Pallas kernels, back(): pl.pallas_call(functools.partial(back_kernel, tiles=tiles), out_shape=jax...  3.85 us
  transfers between devices with their start and end apart: 8, of which 3 were waited for; matrix products, arithmetic and copies ran while one was open for 0% of the time, Pallas kernels for 4%

profile of v1, /device:TPU:24, one launch (start us, length us, event | category | flops | bytes accessed | tf_op | source)
XLA Modules:
  0.0 139.0 jit_solution(7241440722064487675)
XLA Ops:
  0.0 1.5 %pack.1.own = f32[16,16,128]{2,1,0:T(8,128)} custom-call(s32[16]{0:T(128)} %bitcast.7, s32[16]{0:T(128)} %slot.1, f32[8,2048]{1,0:T(8,128)} %residual.5, f32[3,2048]{1,0:T(4,128)} %tangents.1, s32[2,2048]{1,0:T(2,128)} %ends.1), custom_call_target="tpu_custom_call" | custom-call | tf_op jit(solution)/shard_map/pack/pallas_call | solution.py:61
  1.5 1.9 %collective-permute-start.2 = (f32[16,16,128]{2,1,0:T(8,128)}, f32[16,16,128]{2,1,0:T(8,128)S(1)}, u32[]{:S(2)}, u32[]{:S(2)}) collective-permute-start(f32[16,16,128]{2,1,0:T(8,128)} %pack.1.own), channel_id=1, source_target_pairs={{0,8},{8,0},{256,264},{264,256},{1,9},{9,1},{257,265},{265,257},{2... | collective-permute-start | bytes 393224 | tf_op jit(solution)/shard_map/ppermute | solution.py:312
  3.5 3.4 %collective-permute-start.3 = (f32[16,16,128]{2,1,0:T(8,128)}, f32[16,16,128]{2,1,0:T(8,128)S(1)}, u32[]{:S(2)}, u32[]{:S(2)}) collective-permute-start(f32[16,16,128]{2,1,0:T(8,128)} %pack.1.own), channel_id=1, source_target_pairs={{0,256},{8,264},{256,0},{264,8},{1,257},{9,265},{257,1},{265,9},{2... | collective-permute-start | bytes 393224 | tf_op jit(solution)/shard_map/ppermute | solution.py:312
  6.9 2.3 %collective-permute-start.4 = (f32[16,16,128]{2,1,0:T(8,128)}, f32[16,16,128]{2,1,0:T(8,128)S(1)}, u32[]{:S(2)}, u32[]{:S(2)}) collective-permute-start(f32[16,16,128]{2,1,0:T(8,128)} %pack.1.own), channel_id=1, source_target_pairs={{0,264},{8,256},{256,8},{264,0},{1,265},{9,257},{257,9},{265,1},{2... | collective-permute-start | bytes 393224 | tf_op jit(solution)/shard_map/ppermute | solution.py:312
  9.2 0.6 pad_add_fusion.where
  9.8 1.7 %collective-permute-done.3.second = f32[16,16,128]{2,1,0:T(8,128)S(1)} collective-permute-done((f32[16,16,128]{2,1,0:T(8,128)}, f32[16,16,128]{2,1,0:T(8,128)S(1)}, u32[]{:S(2)}, u32[]{:S(2)}) %collective-permute-start.3) | collective-permute-done | bytes 131104 | tf_op jit(solution)/shard_map/ppermute | solution.py:312
  11.5 3.0 %collective-permute-done.4.third = f32[16,16,128]{2,1,0:T(8,128)S(1)} collective-permute-done((f32[16,16,128]{2,1,0:T(8,128)}, f32[16,16,128]{2,1,0:T(8,128)S(1)}, u32[]{:S(2)}, u32[]{:S(2)}) %collective-permute-start.4) | collective-permute-done | bytes 131104 | tf_op jit(solution)/shard_map/ppermute | solution.py:312
  14.5 0.6 copy-done.2
  15.1 5.2 %node_sums.1 = (f32[33,32,128]{2,1,0:T(8,128)}, s32[2,69]{1,0:T(2,128)}) custom-call(s32[2]{0:T(128)} %pad_add_fusion.where, f32[16,16,128]{2,1,0:T(8,128)} %pack.1.own, f32[16,16,128]{2,1,0:T(8,128)} %copy-done, f32[16,16,128]{2,1,0:T(8,128)} %copy-done.1, f32[16,16,128]{2,1,0:T(8,128)} %copy-done.2), custom_call_target="tpu_custom_call" | custom-call | tf_op jit(solution)/shard_map/node_sums/pallas_call | solution.py:132
  20.3 1.1 slice.19
  21.4 44.3 %all_to_all.5 = f32[16,64,128]{2,1,0:T(8,128)} all-to-all(f32[16,64,128]{2,1,0:T(8,128)S(1)} %bitcast.5), channel_id=1, replica_groups=mesh['section'=2,'z'=16,'core'=2,'slab'=8] {'z'}, dimensions={0} | all-to-all | bytes 1048576 | tf_op jit(solution)/shard_map/all_to_all | solution.py:347
  65.6 2.0 %solve.1 = f32[2,32,128]{2,1,0:T(8,128)} custom-call(f32[16,2,32,128]{3,2,1,0:T(8,128)} %bitcast.6, f32[2,128,128]{2,1,0:T(8,128)} %grad.1, f32[2,128,128]{2,1,0:T(8,128)} %vec.1), custom_call_target="tpu_custom_call" | custom-call | tf_op jit(solution)/shard_map/solve/pallas_call | solution.py:163
  67.7 36.1 %all_gather.3.values = f32[32,32,128]{2,1,0:T(8,128)} all-gather(f32[2,32,128]{2,1,0:T(8,128)} %solve.1), channel_id=1, replica_groups=mesh['section'=2,'z'=16,'core'=2,'slab'=8] {'z'}, dimensions={0}, use_global_device_ids=true | all-gather | bytes 557056 | tf_op jit(solution)/shard_map/all_gather | solution.py:355
  103.7 3.8 %back.1 = f32[64,8,128]{2,1,0:T(8,128)} custom-call(s32[2,69]{1,0:T(2,128)} %get-tuple-element.11.chosen, f32[16,16,128]{2,1,0:T(8,128)} %pack.1.own, f32[16,16,128]{2,1,0:T(8,128)} %copy-done, f32[16,16,128]{2,1,0:T(8,128)} %copy-done.1, f32[16,16,128]{2,1,0:T(8,128)} %copy-done.2, f32[32,32,128]{2,1,0:T(8,128)} %all_gather.3.values), custom_call_target="tpu_custom_call" | custom-call | tf_op jit(solution)/shard_map/back/pallas_call | solution.py:207
  107.6 1.6 %fusion = (f32[16,8,128]{2,1,0:T(8,128)S(1)}, f32[16,8,128]{2,1,0:T(8,128)S(1)}, f32[16,8,128]{2,1,0:T(8,128)S(1)}, f32[16,8,128]{2,1,0:T(8,128)}) fusion(f32[64,8,128]{2,1,0:T(8,128)} %back.1), kind=kLoop, calls=%fused_computation.1 | loop fusion | bytes 524288 | tf_op jit(solution)/shard_map/slice | solution.py:357
  109.2 1.9 %collective-permute-start.5 = (f32[16,8,128]{2,1,0:T(8,128)S(1)}, f32[16,8,128]{2,1,0:T(8,128)S(1)}, u32[]{:S(2)}, u32[]{:S(2)}) collective-permute-start(f32[16,8,128]{2,1,0:T(8,128)S(1)} %get-tuple-element.15), channel_id=1, source_target_pairs={{0,8},{8,0},{256,264},{264,256},{1,9},{9,1},{257,265},{265,257},{2... | collective-permute-start | bytes 196616 | tf_op jit(solution)/shard_map/ppermute | solution.py:312
  111.1 4.5 %collective-permute-start.6 = (f32[16,8,128]{2,1,0:T(8,128)S(1)}, f32[16,8,128]{2,1,0:T(8,128)S(1)}, u32[]{:S(2)}, u32[]{:S(2)}) collective-permute-start(f32[16,8,128]{2,1,0:T(8,128)S(1)} %get-tuple-element.14), channel_id=1, source_target_pairs={{0,256},{8,264},{256,0},{264,8},{1,257},{9,265},{257,1},{265,9},{2... | collective-permute-start | bytes 196616 | tf_op jit(solution)/shard_map/ppermute | solution.py:312
  115.6 2.0 %collective-permute-start.7 = (f32[16,8,128]{2,1,0:T(8,128)S(1)}, f32[16,8,128]{2,1,0:T(8,128)S(1)}, u32[]{:S(2)}, u32[]{:S(2)}) collective-permute-start(f32[16,8,128]{2,1,0:T(8,128)S(1)} %get-tuple-element.13), channel_id=1, source_target_pairs={{0,264},{8,256},{256,8},{264,0},{1,265},{9,257},{257,9},{265,1},{2... | collective-permute-start | bytes 196616 | tf_op jit(solution)/shard_map/ppermute | solution.py:312
  117.6 2.2 %smooth_once.1 = (f32[16,8,128]{2,1,0:T(8,128)}, f32[2,8,128]{2,1,0:T(8,128)}) custom-call(s32[16]{0:T(128)} %kind.3, f32[16]{0:T(128)} %coeff.3, s32[2]{0:T(128)} %halo.1, f32[8,2048]{1,0:T(8,128)} %residual.5, f32[8,128,128]{2,1,0:T(8,128)} %inverse.3), custom_call_target="tpu_custom_call" | custom-call | tf_op jit(solution)/shard_map/smooth_once/pallas_call | solution.py:235
  119.8 3.9 %collective-permute-start = (f32[2,8,128]{2,1,0:T(8,128)}, f32[2,8,128]{2,1,0:T(8,128)S(1)}, u32[]{:S(2)}, u32[]{:S(2)}) collective-permute-start(f32[2,8,128]{2,1,0:T(8,128)} %get-tuple-element.10), channel_id=1, source_target_pairs={{0,1},{1,2},{2,3},{3,4},{4,5},{5,6},{6,7},{8,9},{9,10},{10,11},{11... | collective-permute-start | bytes 24584 | tf_op jit(solution)/shard_map/ppermute | solution.py:342
  123.7 2.0 %collective-permute-start.1 = (f32[2,8,128]{2,1,0:T(8,128)}, f32[2,8,128]{2,1,0:T(8,128)S(1)}, u32[]{:S(2)}, u32[]{:S(2)}) collective-permute-start(f32[2,8,128]{2,1,0:T(8,128)} %get-tuple-element.10), channel_id=1, source_target_pairs={{1,0},{2,1},{3,2},{4,3},{5,4},{6,5},{7,6},{9,8},{10,9},{11,10},{12... | collective-permute-start | bytes 24584 | tf_op jit(solution)/shard_map/ppermute | solution.py:343
  125.7 7.4 %collective-permute-done.1.high = f32[2,8,128]{2,1,0:T(8,128)S(1)} collective-permute-done((f32[2,8,128]{2,1,0:T(8,128)}, f32[2,8,128]{2,1,0:T(8,128)S(1)}, u32[]{:S(2)}, u32[]{:S(2)}) %collective-permute-start.1) | collective-permute-done | bytes 8224 | tf_op jit(solution)/shard_map/ppermute | solution.py:343
  133.6 3.1 %smooth_again.1.smoothed = f32[16,8,128]{2,1,0:T(8,128)} custom-call(s32[16]{0:T(128)} %kind.3, f32[16]{0:T(128)} %coeff.3, s32[8,16]{1,0:T(8,128)} %cols.1, s32[8,16]{1,0:T(8,128)} %kinds.1, f32[8,16]{1,0:T(8,128)} %coeffs.1, f32[16,8,128]{2,1,0:T(8,128)} %get-tuple-element.9.smoothed, f32[2,8,128]{2,1,0:T(8,128)} %copy-done.6, f32[2,8,128]{2,1,0:T(8,128)} %copy-done.7, ...), custom_call_target="tpu_custom_call" | custom-call | tf_op jit(solution)/shard_map/smooth_again/pallas_call | solution.py:279
  137.4 1.6 %finish.1 = f32[8,2048]{1,0:T(8,128)} custom-call(f32[16,8,128]{2,1,0:T(8,128)} %smooth_again.1.smoothed, f32[16,8,128]{2,1,0:T(8,128)} %get-tuple-element.16.own, f32[16,8,128]{2,1,0:T(8,128)} %copy-done.3, f32[16,8,128]{2,1,0:T(8,128)} %copy-done.4, f32[16,8,128]{2,1,0:T(8,128)} %copy-done.5), custom_call_target="tpu_custom_call" | custom-call | tf_op jit(solution)/shard_map/finish/pallas_call | solution.py:302
  (20 shorter events, 1.3 us)
Async XLA Ops:
  1.5 8.2 %collective-permute-start.2 = (f32[16,16,128]{2,1,0:T(8,128)}, f32[16,16,128]{2,1,0:T(8,128)S(1)}, u32[]{:S(2)}, u32[]{:S(2)}) collective-permute-start(f32[16,16,128]{2,1,0:T(8,128)} %pack.1.own), channel_id=1, source_target_pairs={{0,8},{8,0},{256,264},{264,256},{1,9},{9,1},{257,265},{265,257},{2... | collective-permute-start | bytes 393224 | tf_op jit(solution)/shard_map/ppermute | solution.py:312
  3.5 8.0 %collective-permute-start.3 = (f32[16,16,128]{2,1,0:T(8,128)}, f32[16,16,128]{2,1,0:T(8,128)S(1)}, u32[]{:S(2)}, u32[]{:S(2)}) collective-permute-start(f32[16,16,128]{2,1,0:T(8,128)} %pack.1.own), channel_id=1, source_target_pairs={{0,256},{8,264},{256,0},{264,8},{1,257},{9,265},{257,1},{265,9},{2... | collective-permute-start | bytes 393224 | tf_op jit(solution)/shard_map/ppermute | solution.py:312
  6.9 7.6 %collective-permute-start.4 = (f32[16,16,128]{2,1,0:T(8,128)}, f32[16,16,128]{2,1,0:T(8,128)S(1)}, u32[]{:S(2)}, u32[]{:S(2)}) collective-permute-start(f32[16,16,128]{2,1,0:T(8,128)} %pack.1.own), channel_id=1, source_target_pairs={{0,264},{8,256},{256,8},{264,0},{1,265},{9,257},{257,9},{265,1},{2... | collective-permute-start | bytes 393224 | tf_op jit(solution)/shard_map/ppermute | solution.py:312
  9.8 4.7 %copy-start = (f32[16,16,128]{2,1,0:T(8,128)}, f32[16,16,128]{2,1,0:T(8,128)S(1)}, u32[]{:S(2)}) copy-start(f32[16,16,128]{2,1,0:T(8,128)S(1)} %collective-permute-done.2.first) | copy-start | bytes 393220
  11.5 3.0 %copy-start.1 = (f32[16,16,128]{2,1,0:T(8,128)}, f32[16,16,128]{2,1,0:T(8,128)S(1)}, u32[]{:S(2)}) copy-start(f32[16,16,128]{2,1,0:T(8,128)S(1)} %collective-permute-done.3.second) | copy-start | bytes 393220
  14.5 0.6 copy-start.2
  109.2 27.6 %collective-permute-start.5 = (f32[16,8,128]{2,1,0:T(8,128)S(1)}, f32[16,8,128]{2,1,0:T(8,128)S(1)}, u32[]{:S(2)}, u32[]{:S(2)}) collective-permute-start(f32[16,8,128]{2,1,0:T(8,128)S(1)} %get-tuple-element.15), channel_id=1, source_target_pairs={{0,8},{8,0},{256,264},{264,256},{1,9},{9,1},{257,265},{265,257},{2... | collective-permute-start | bytes 196616 | tf_op jit(solution)/shard_map/ppermute | solution.py:312
  111.1 25.7 %collective-permute-start.6 = (f32[16,8,128]{2,1,0:T(8,128)S(1)}, f32[16,8,128]{2,1,0:T(8,128)S(1)}, u32[]{:S(2)}, u32[]{:S(2)}) collective-permute-start(f32[16,8,128]{2,1,0:T(8,128)S(1)} %get-tuple-element.14), channel_id=1, source_target_pairs={{0,256},{8,264},{256,0},{264,8},{1,257},{9,265},{257,1},{265,9},{2... | collective-permute-start | bytes 196616 | tf_op jit(solution)/shard_map/ppermute | solution.py:312
  115.6 21.2 %collective-permute-start.7 = (f32[16,8,128]{2,1,0:T(8,128)S(1)}, f32[16,8,128]{2,1,0:T(8,128)S(1)}, u32[]{:S(2)}, u32[]{:S(2)}) collective-permute-start(f32[16,8,128]{2,1,0:T(8,128)S(1)} %get-tuple-element.13), channel_id=1, source_target_pairs={{0,264},{8,256},{256,8},{264,0},{1,265},{9,257},{257,9},{265,1},{2... | collective-permute-start | bytes 196616 | tf_op jit(solution)/shard_map/ppermute | solution.py:312
  119.8 5.8 %collective-permute-start = (f32[2,8,128]{2,1,0:T(8,128)}, f32[2,8,128]{2,1,0:T(8,128)S(1)}, u32[]{:S(2)}, u32[]{:S(2)}) collective-permute-start(f32[2,8,128]{2,1,0:T(8,128)} %get-tuple-element.10), channel_id=1, source_target_pairs={{0,1},{1,2},{2,3},{3,4},{4,5},{5,6},{6,7},{8,9},{9,10},{10,11},{11... | collective-permute-start | bytes 24584 | tf_op jit(solution)/shard_map/ppermute | solution.py:342
  123.7 9.4 %collective-permute-start.1 = (f32[2,8,128]{2,1,0:T(8,128)}, f32[2,8,128]{2,1,0:T(8,128)S(1)}, u32[]{:S(2)}, u32[]{:S(2)}) collective-permute-start(f32[2,8,128]{2,1,0:T(8,128)} %get-tuple-element.10), channel_id=1, source_target_pairs={{1,0},{2,1},{3,2},{4,3},{5,4},{6,5},{7,6},{9,8},{10,9},{11,10},{12... | collective-permute-start | bytes 24584 | tf_op jit(solution)/shard_map/ppermute | solution.py:343
  125.7 7.4 %copy-start.6 = (f32[2,8,128]{2,1,0:T(8,128)}, f32[2,8,128]{2,1,0:T(8,128)S(1)}, u32[]{:S(2)}) copy-start(f32[2,8,128]{2,1,0:T(8,128)S(1)} %collective-permute-done.low) | copy-start | bytes 24580
  133.0 0.6 copy-start.7
  136.7 0.6 copy-start.3
  136.7 0.6 copy-start.4
  136.8 0.6 copy-start.5

commit v2 on v1

--- a/solution.py
+++ b/solution.py
@@ -9,6 +9,7 @@
 
 DAMPING = 0.7
 CORES = 2
+NEAR = 1
 F32 = jnp.float32
 BF16 = jnp.bfloat16
 SMEM = pltpu.SMEM
@@ -67,43 +68,39 @@
     )(owner, slot, residual, tangents, ends)
 
 
-def sums_kernel(
-    where, own, first, second, third, sums, chosen, buf, meta, sems, msems, *, sections_stride, tiles, group
-):
-    sources = (own, first, second, third)
-    copies = []
-    for q, src in enumerate(sources):
-        copies.append(
-            pltpu.make_async_copy(src.at[0, pl.ds(8, 8), :], meta.at[q], msems.at[q])
-        )
-        copies[-1].start()
-    data = []
-    for q, src in enumerate(sources):
-        data.append(pltpu.make_async_copy(src, buf.at[pl.ds(q * tiles, tiles)], sems.at[q]))
-        data[-1].start()
-    trash = sums.shape[0] - 1
+def sums_kernel(where, gathered, sums, chosen, buf, meta, sems, *, doms, stride, team, tiles, group):
+    width = buf.shape[2]
+    total = team * tiles
+    copies = [
+        pltpu.make_async_copy(gathered.at[q * tiles, pl.ds(8, 8), :], meta.at[q], sems.at[q])
+        for q in range(team)
+    ]
+    for copy in copies:
+        copy.start()
+    data = pltpu.make_async_copy(gathered, buf.at[pl.ds(0, total)], sems.at[team])
+    data.start()
     sums[...] = jnp.zeros_like(sums)
+    buf[total] = jnp.zeros(buf.shape[1:], F32)
     for copy in copies:
         copy.wait()
-    my_section, my_core = where[0], where[1]
+    mine = where[0]
 
     count = jnp.int32(0)
-    for q in range(4):
+    for q in range(team):
         for t in range(tiles):
             dst = meta[q, 5, t].astype(jnp.int32)
-            owner = dst // 2
-            mine = (owner // sections_stride == my_section) & (owner % CORES == my_core)
-            local = ((owner % sections_stride) // CORES) * 2 + dst % 2
+            owner, slot = dst // 2, dst % 2
+            section, dom = owner // doms, owner % doms
+            z, core = dom // CORES, dom % CORES
+            cls = (section * stride + z % stride) * CORES + core
             chosen[0, count + 1] = q * tiles + t
-            chosen[1, count + 1] = local
-            count = jnp.where(mine, count + 1, count)
+            chosen[1, count + 1] = (z // stride) * 2 + slot
+            count = jnp.where(cls == mine, count + 1, count)
     chosen[0, 0] = count
     for extra in range(group):
-        chosen[0, count + 1 + extra] = 0
-        chosen[1, count + 1 + extra] = trash
-    for copy in data:
-        copy.wait()
-    width = buf.shape[2]
+        chosen[0, count + 1 + extra] = total
+        chosen[1, count + 1 + extra] = 0
+    data.wait()
     nodes = lax.broadcasted_iota(jnp.int32, (width, width), 0).astype(F32)
 
     def step(i, carry):
@@ -126,27 +123,26 @@
     lax.fori_loop(0, (count + group - 1) // group, step, 0)
 
 
-def node_sums(where, payloads, places, sections_stride):
-    tiles, _, width = payloads[0].shape
+def node_sums(where, gathered, team, places, doms, stride):
+    total, _, width = gathered.shape
     group = 4
     return pl.pallas_call(
         functools.partial(
-            sums_kernel, sections_stride=sections_stride, tiles=tiles, group=group
+            sums_kernel, doms=doms, stride=stride, team=team, tiles=total // team, group=group
         ),
         out_shape=(
-            jax.ShapeDtypeStruct((places + 1, 32, width), F32),
-            jax.ShapeDtypeStruct((2, 4 * tiles + 1 + group), jnp.int32),
+            jax.ShapeDtypeStruct((places, 32, width), F32),
+            jax.ShapeDtypeStruct((2, total + 1 + group), jnp.int32),
         ),
-        in_specs=[smem_spec] + [any_spec] * 4,
+        in_specs=[smem_spec, any_spec],
         out_specs=(vmem_spec, smem_spec),
         scratch_shapes=[
-            VMEM((4 * tiles, 16, width), F32),
-            SMEM((4, 8, width), F32),
-            pltpu.SemaphoreType.DMA((4,)),
-            pltpu.SemaphoreType.DMA((4,)),
+            VMEM((total + 1, 16, width), F32),
+            SMEM((team, 8, width), F32),
+            pltpu.SemaphoreType.DMA((team + 1,)),
         ],
         name="node_sums",
-    )(where, *payloads)
+    )(where, gathered)
 
 
 def solve_kernel(arrived, grad, vec, out):
@@ -169,18 +165,11 @@
     )(arrived, grad, vec)
 
 
-def back_kernel(chosen, own, first, second, third, values, out, buf, sems, *, tiles):
-    data = []
-    for q, src in enumerate((own, first, second, third)):
-        data.append(
-            pltpu.make_async_copy(
-                src.at[:, pl.ds(8, 8), :], buf.at[pl.ds(q * tiles, tiles)], sems.at[q]
-            )
-        )
-        data[-1].start()
+def back_kernel(chosen, gathered, values, out, buf, sem):
+    data = pltpu.make_async_copy(gathered.at[:, pl.ds(8, 8), :], buf, sem)
+    data.start()
     out[...] = jnp.zeros_like(out)
-    for copy in data:
-        copy.wait()
+    data.wait()
     width = buf.shape[2]
 
     def pick(rows, index):
@@ -202,16 +191,16 @@
     lax.fori_loop(0, chosen[0, 0], step, 0)
 
 
-def back(chosen, payloads, values):
-    tiles, _, width = payloads[0].shape
-    return pl.pallas_call(
-        functools.partial(back_kernel, tiles=tiles),
-        out_shape=jax.ShapeDtypeStruct((4 * tiles, 8, width), F32),
-        in_specs=[smem_spec] + [any_spec] * 4 + [vmem_spec],
-        out_specs=vmem_spec,
-        scratch_shapes=[VMEM((4 * tiles, 8, width), F32), pltpu.SemaphoreType.DMA((4,))],
+def back(chosen, gathered, values):
+    total, _, width = gathered.shape
+    return pl.pallas_call(
+        back_kernel,
+        out_shape=jax.ShapeDtypeStruct((total, 8, width), F32),
+        in_specs=[smem_spec, any_spec, vmem_spec],
+        out_specs=vmem_spec,
+        scratch_shapes=[VMEM((total, 8, width), F32), pltpu.SemaphoreType.DMA(())],
         name="back",
-    )(chosen, *payloads, values)
+    )(chosen, gathered, values)
 
 
 def by_tile(ref, tiles, width):
@@ -289,12 +278,13 @@
     )(kind, coeff, cols, kinds, coeffs, smoothed, low, high, residual, coupling, inverse)
 
 
-def finish_kernel(smoothed, own, first, second, third, out):
+def finish_kernel(smoothed, pieces, out):
     tiles, _, width = smoothed.shape
     for t in range(tiles):
-        out[:, t * width : (t + 1) * width] = smoothed[t] + (
-            (own[t] + first[t]) + (second[t] + third[t])
-        )
+        rows = pieces[0, t]
+        for q in range(1, pieces.shape[0]):
+            rows = rows + pieces[q, t]
+        out[:, t * width : (t + 1) * width] = smoothed[t] + rows
 
 
 def finish(smoothed, pieces):
@@ -302,14 +292,13 @@
     return pl.pallas_call(
         finish_kernel,
         out_shape=jax.ShapeDtypeStruct((cases, tiles * width), F32),
-        in_specs=[vmem_spec] * 5,
+        in_specs=[vmem_spec] * 2,
         out_specs=vmem_spec,
         name="finish",
-    )(smoothed, *pieces)
-
-
-def swap(x, which):
-    return lax.ppermute(x, ("section", "core"), [(i, i ^ which) for i in range(4)])
+    )(smoothed, pieces)
+
+
+TEAM = ("section", "near", "core")
 
 
 def body(
@@ -329,39 +318,42 @@
     grad_blocks,
     vec_blocks,
 ):
-    heights = lax.axis_size("z")
+    heights, stride, team = lax.axis_size("far"), lax.axis_size("near"), lax.axis_size(TEAM)
     node_tiles = grad_blocks.shape[0]
     tiles = diag_kind.shape[0]
     width = coupling_tiles.shape[1]
-    where = jnp.stack([lax.axis_index("section"), lax.axis_index("core")]).astype(jnp.int32)
+    where = lax.axis_index(TEAM).astype(jnp.int32).reshape(1)
     own = pack(tile_owner[:, 0], node_slot, residual, tangents, edge_nodes)
-    payloads = [own] + [swap(own, which) for which in (1, 2, 3)]
+    gathered = lax.all_gather(own, TEAM, tiled=True)
 
     smoothed, rim = smooth(diag_kind, diag_coeff, halo_rows, residual, inverse_tiles)
     slabs = lax.axis_size("slab")
     low = lax.ppermute(rim, "slab", [(i, i + 1) for i in range(slabs - 1)])
     high = lax.ppermute(rim, "slab", [(i + 1, i) for i in range(slabs - 1)])
 
-    sums, chosen = node_sums(where, payloads, heights * node_tiles, heights * CORES)
-    sums = sums[: heights * node_tiles].reshape(heights, node_tiles * 32, width)
-    arrived = lax.all_to_all(sums, "z", split_axis=0, concat_axis=0, tiled=True)
+    doms = heights * stride * CORES
+    sums, chosen = node_sums(where, gathered, team, heights * node_tiles, doms, stride)
+    sums = sums.reshape(heights, node_tiles * 32, width)
+    arrived = lax.all_to_all(sums, "far", split_axis=0, concat_axis=0, tiled=True)
 
     smoothed_twice = smooth_again(
         diag_kind, diag_coeff, tile_cols, tile_kinds, tile_coeff,
         smoothed, low, high, residual, coupling_tiles, inverse_tiles,
     )
+    arrived, smoothed_twice = lax.optimization_barrier((arrived, smoothed_twice))
 
     solved = solve(arrived.reshape(heights, node_tiles, 32, width), grad_blocks, vec_blocks)
-    values = lax.all_gather(solved, "z", tiled=True)
-    corrections = back(chosen, payloads, values).reshape(4, tiles, 8, width)
-    pieces = [corrections[0]] + [swap(corrections[which], which) for which in (1, 2, 3)]
+    values = lax.all_gather(solved, "far", tiled=True)
+    corrections = back(chosen, gathered, values).reshape(team, tiles, 8, width)
+    pieces = lax.all_to_all(corrections, TEAM, split_axis=0, concat_axis=0, tiled=True)
     return finish(smoothed_twice, pieces)
 
 
 def solution(mesh):
-    names = ("section", "z", "core", "slab")
+    names = ("section", "far", "near", "core", "slab")
     sections, doms, slabs = (mesh.shape[name] for name in ("section", "dom", "slab"))
-    inner = Mesh(mesh.devices.reshape(sections, doms // CORES, CORES, slabs), names)
+    shape = (sections, doms // CORES // NEAR, NEAR, CORES, slabs)
+    inner = Mesh(mesh.devices.reshape(shape), names)
     rows, cols = P(names), P(None, names)
     placed = (
         cols, P(), P(), rows, rows, cols, cols, cols, rows, rows, rows, cols, cols, rows, rows,

time: 140 us -> 116 us (0.83)
  blocking collectives: 80.3 us -> 55 us
  waiting for transfers between devices: 12.1 us -> 17.5 us
  local copies, waits for them, and re-layouts: 4.54 us -> 1.4 us
    all_to_all x1, blocking collectives: 44.3 us -> 10.2 us  [body(): lax.all_to_all(corrections, TEAM, split_axis=0, concat_axis=0, tiled=True)]
    ppermute x6 -> x0, starting transfers between devices: 16 us -> none  [swap(): lax.ppermute(x, ('section', 'core'), [(i, i ^ which) for i in range(4)])]
    all_to_all x0 -> x1, starting transfers between devices: none -> 15.2 us  [body(): lax.all_to_all(sums, 'far', split_axis=0, concat_axis=0, tiled=True)]
    all_to_all x0 -> x1, waiting for transfers between devices: none -> 10 us  [body(): lax.all_to_all(sums, 'far', split_axis=0, concat_axis=0, tiled=True)]
    all_gather x1 -> x2, blocking collectives: 36.1 us -> 44.8 us  [the longest x1 36.1 us: body(): values = lax.all_gather(solved, 'far', tiled=True)]
    ppermute x6 -> x0, waiting for transfers between devices: 4.7 us -> none  [swap(): lax.ppermute(x, ('section', 'core'), [(i, i ^ which) for i in range(4)])]
    slice x2 -> x0, local copies, waits for them, and re-layouts: 2.67 us -> none  [the longest x1 1.59 us: body(): corrections[which]]
  transfers between devices with their start and end apart: 8 -> 3, of which waited for: 3 -> 2; matrix products, arithmetic and copies ran while one was open for 0% -> 0% of each run, Pallas kernels for 4% -> 5%
where the time goes in v2:
time: 116 us; the launch traced here: 114 us
  blocking collectives  55 us (47%)
  starting transfers between devices  21.1 us (18%)
  Pallas kernels  18.8 us (16%)
  waiting for transfers between devices  17.5 us (15%)
  local copies, waits for them, and re-layouts  1.4 us (1%)
    all_gather x1, blocking collectives, body(): values = lax.all_gather(solved, 'far', tiled=True)  36.1 us
    all_to_all x1, starting transfers between devices, body(): lax.all_to_all(sums, 'far', split_axis=0, concat_axis=0, tiled=True)  15.2 us
    all_to_all x1, blocking collectives, body(): lax.all_to_all(corrections, TEAM, split_axis=0, concat_axis=0, tiled=True)  10.2 us
    all_to_all x1, waiting for transfers between devices, body(): lax.all_to_all(sums, 'far', split_axis=0, concat_axis=0, tiled=True)  10 us
    all_gather x1, blocking collectives, body(): gathered = lax.all_gather(own, TEAM, tiled=True)  8.67 us
    ppermute x1, waiting for transfers between devices, body(): high = lax.ppermute(rim, 'slab', [(i + 1, i) for i in range(slabs - 1)])  7.43 us
    pallas_call x1, Pallas kernels, node_sums(): pl.pallas_call(functools.partial(sums_kernel, doms=doms, stride=stride, t...  4.3 us
    ppermute x1, starting transfers between devices, body(): low = lax.ppermute(rim, 'slab', [(i, i + 1) for i in range(slabs - 1)])  4 us
  transfers between devices with their start and end apart: 3, of which 2 were waited for; matrix products, arithmetic and copies ran while one was open for 0% of the time, Pallas kernels for 5%

profile of v2, /device:TPU:24, one launch (start us, length us, event | category | flops | bytes accessed | tf_op | source)
XLA Modules:
  0.0 113.8 jit_solution(16557355811317710318)
XLA Ops:
  0.0 1.6 %pack.1 = f32[16,16,128]{2,1,0:T(8,128)} custom-call(s32[16]{0:T(128)} %bitcast.8, s32[16]{0:T(128)} %slot.1, f32[8,2048]{1,0:T(8,128)} %residual.5, f32[3,2048]{1,0:T(4,128)} %tangents.1, s32[2,2048]{1,0:T(2,128)} %ends.1), custom_call_target="tpu_custom_call" | custom-call | tf_op jit(solution)/shard_map/pack/pallas_call | solution.py:62
  1.6 8.7 %all_gather.6.gathered = f32[64,16,128]{2,1,0:T(8,128)} all-gather(f32[16,16,128]{2,1,0:T(8,128)} %pack.1), channel_id=1, replica_groups=mesh['section'=2,'far'=16,'near'=1,'core'=2,'slab'=8] {'section','near',..., dimensions={0}, use_global_device_ids=true | all-gather | bytes 655360 | tf_op jit(solution)/shard_map/all_gather | solution.py:327
  10.2 4.3 %node_sums.1 = (f32[32,32,128]{2,1,0:T(8,128)}, s32[2,69]{1,0:T(2,128)}) custom-call(s32[1]{0:T(128)} %bitcast.where, f32[64,16,128]{2,1,0:T(8,128)} %all_gather.6.gathered), custom_call_target="tpu_custom_call" | custom-call | tf_op jit(solution)/shard_map/node_sums/pallas_call | solution.py:129
  14.5 15.2 %all-to-all-start = ((f32[16,64,128]{2,1,0:T(8,128)}), f32[16,64,128]{2,1,0:T(8,128)S(1)}, u32[]{:S(2)}, u32[]{:S(2)}) async-start(f32[16,64,128]{2,1,0:T(8,128)} %bitcast.7), calls=%async_computation | async-start | bytes 1048576 | tf_op jit(solution)/shard_map/all_to_all | solution.py:337
  29.7 2.2 %smooth_once.1 = (f32[16,8,128]{2,1,0:T(8,128)}, f32[2,8,128]{2,1,0:T(8,128)}) custom-call(s32[16]{0:T(128)} %kind.3, f32[16]{0:T(128)} %coeff.3, s32[2]{0:T(128)} %halo.1, f32[8,2048]{1,0:T(8,128)} %residual.5, f32[8,128,128]{2,1,0:T(8,128)} %inverse.3), custom_call_target="tpu_custom_call" | custom-call | tf_op jit(solution)/shard_map/smooth_once/pallas_call | solution.py:224
  32.0 4.0 %collective-permute-start = (f32[2,8,128]{2,1,0:T(8,128)}, f32[2,8,128]{2,1,0:T(8,128)S(1)}, u32[]{:S(2)}, u32[]{:S(2)}) collective-permute-start(f32[2,8,128]{2,1,0:T(8,128)} %get-tuple-element.13), channel_id=1, source_target_pairs={{0,1},{1,2},{2,3},{3,4},{4,5},{5,6},{6,7},{8,9},{9,10},{10,11},{11... | collective-permute-start | bytes 24584 | tf_op jit(solution)/shard_map/ppermute | solution.py:331
  36.0 1.9 %collective-permute-start.1 = (f32[2,8,128]{2,1,0:T(8,128)}, f32[2,8,128]{2,1,0:T(8,128)S(1)}, u32[]{:S(2)}, u32[]{:S(2)}) collective-permute-start(f32[2,8,128]{2,1,0:T(8,128)} %get-tuple-element.13), channel_id=1, source_target_pairs={{1,0},{2,1},{3,2},{4,3},{5,4},{6,5},{7,6},{9,8},{10,9},{11,10},{12... | collective-permute-start | bytes 24584 | tf_op jit(solution)/shard_map/ppermute | solution.py:332
  37.9 0.0 collective-permute-done.low
  37.9 0.0 copy-start.1
  37.9 7.4 %collective-permute-done.1.high = f32[2,8,128]{2,1,0:T(8,128)S(1)} collective-permute-done((f32[2,8,128]{2,1,0:T(8,128)}, f32[2,8,128]{2,1,0:T(8,128)S(1)}, u32[]{:S(2)}, u32[]{:S(2)}) %collective-permute-start.1) | collective-permute-done | bytes 8224 | tf_op jit(solution)/shard_map/ppermute | solution.py:332
  45.3 0.0 copy-start.2
  45.3 0.0 copy-done.1
  45.3 0.6 copy-done.2
  45.9 3.1 %smooth_again.1.smoothed = f32[16,8,128]{2,1,0:T(8,128)} custom-call(s32[16]{0:T(128)} %kind.3, f32[16]{0:T(128)} %coeff.3, s32[8,16]{1,0:T(8,128)} %cols.1, s32[8,16]{1,0:T(8,128)} %kinds.1, f32[8,16]{1,0:T(8,128)} %coeffs.1, f32[16,8,128]{2,1,0:T(8,128)} %get-tuple-element.12.smoothed, f32[2,8,128]{2,1,0:T(8,128)} %copy-done.1, f32[2,8,128]{2,1,0:T(8,128)} %copy-done.2, ...), custom_call_target="tpu_custom_call" | custom-call | tf_op jit(solution)/shard_map/smooth_again/pallas_call | solution.py:268
  49.0 10.0 %all-to-all-done = f32[16,64,128]{2,1,0:T(8,128)S(1)} async-done(((f32[16,64,128]{2,1,0:T(8,128)}), f32[16,64,128]{2,1,0:T(8,128)S(1)}, u32[]{:S(2)}, u32[]{:S(2)}) %all-to-all-start) | async-done | bytes 524320 | tf_op jit(solution)/shard_map/all_to_all | solution.py:337
  59.1 0.0 copy-start
  59.1 0.8 copy-done
  59.9 2.0 %solve.1 = f32[2,32,128]{2,1,0:T(8,128)} custom-call(f32[16,2,32,128]{3,2,1,0:T(8,128)} %bitcast.5, f32[2,128,128]{2,1,0:T(8,128)} %grad.1, f32[2,128,128]{2,1,0:T(8,128)} %vec.1), custom_call_target="tpu_custom_call" | custom-call | tf_op jit(solution)/shard_map/solve/pallas_call | solution.py:159
  61.9 36.1 %all_gather.7.values = f32[32,32,128]{2,1,0:T(8,128)} all-gather(f32[2,32,128]{2,1,0:T(8,128)} %solve.1), channel_id=1, replica_groups=mesh['section'=2,'far'=16,'near'=1,'core'=2,'slab'=8] {'far'}, dimensions={0}, use_global_device_ids=true | all-gather | bytes 557056 | tf_op jit(solution)/shard_map/all_gather | solution.py:346
  98.0 3.9 %back.1 = f32[64,8,128]{2,1,0:T(8,128)} custom-call(s32[2,69]{1,0:T(2,128)} %get-tuple-element.15.chosen, f32[64,16,128]{2,1,0:T(8,128)} %all_gather.6.gathered, f32[32,32,128]{2,1,0:T(8,128)} %all_gather.7.values), custom_call_target="tpu_custom_call" | custom-call | tf_op jit(solution)/shard_map/back/pallas_call | solution.py:196
  102.0 10.2 %all_to_all.10.pieces = f32[4,16,8,128]{3,2,1,0:T(8,128)} all-to-all(f32[4,16,8,128]{3,2,1,0:T(8,128)} %bitcast.6), channel_id=1, replica_groups=mesh['section'=2,'far'=16,'near'=1,'core'=2,'slab'=8] {'section','near',..., dimensions={0} | all-to-all | bytes 524288 | tf_op jit(solution)/shard_map/all_to_all | solution.py:348
  112.1 1.6 %finish.1 = f32[8,2048]{1,0:T(8,128)} custom-call(f32[16,8,128]{2,1,0:T(8,128)} %smooth_again.1.smoothed, f32[4,16,8,128]{3,2,1,0:T(8,128)} %all_to_all.10.pieces), custom_call_target="tpu_custom_call" | custom-call | tf_op jit(solution)/shard_map/finish/pallas_call | solution.py:292
Async XLA Ops:
  14.5 44.5 %all-to-all-start = ((f32[16,64,128]{2,1,0:T(8,128)}), f32[16,64,128]{2,1,0:T(8,128)S(1)}, u32[]{:S(2)}, u32[]{:S(2)}) async-start(f32[16,64,128]{2,1,0:T(8,128)} %bitcast.7), calls=%async_computation | async-start | bytes 1048576 | tf_op jit(solution)/shard_map/all_to_all | solution.py:337
  32.0 5.9 %collective-permute-start = (f32[2,8,128]{2,1,0:T(8,128)}, f32[2,8,128]{2,1,0:T(8,128)S(1)}, u32[]{:S(2)}, u32[]{:S(2)}) collective-permute-start(f32[2,8,128]{2,1,0:T(8,128)} %get-tuple-element.13), channel_id=1, source_target_pairs={{0,1},{1,2},{2,3},{3,4},{4,5},{5,6},{6,7},{8,9},{9,10},{10,11},{11... | collective-permute-start | bytes 24584 | tf_op jit(solution)/shard_map/ppermute | solution.py:331
  36.0 9.4 %collective-permute-start.1 = (f32[2,8,128]{2,1,0:T(8,128)}, f32[2,8,128]{2,1,0:T(8,128)S(1)}, u32[]{:S(2)}, u32[]{:S(2)}) collective-permute-start(f32[2,8,128]{2,1,0:T(8,128)} %get-tuple-element.13), channel_id=1, source_target_pairs={{1,0},{2,1},{3,2},{4,3},{5,4},{6,5},{7,6},{9,8},{10,9},{11,10},{12... | collective-permute-start | bytes 24584 | tf_op jit(solution)/shard_map/ppermute | solution.py:332
  37.9 7.4 %copy-start.1 = (f32[2,8,128]{2,1,0:T(8,128)}, f32[2,8,128]{2,1,0:T(8,128)S(1)}, u32[]{:S(2)}) copy-start(f32[2,8,128]{2,1,0:T(8,128)S(1)} %collective-permute-done.low) | copy-start | bytes 24580
  45.3 0.6 copy-start.2
  59.1 0.8 copy-start

commit v3 on v2

--- a/solution.py
+++ b/solution.py
@@ -9,7 +9,7 @@
 
 DAMPING = 0.7
 CORES = 2
-NEAR = 1
+NEAR = 2
 F32 = jnp.float32
 BF16 = jnp.bfloat16
 SMEM = pltpu.SMEM

time: 116 us -> 149 us (1.28)
  the two profiles are of different devices: /device:TPU:24 before, /device:TPU:4 now
where the time goes in v3:
time: 149 us; the launch traced here: 148 us
  blocking collectives  50.2 us (34%)
  waiting for transfers between devices  44.3 us (30%)
  Pallas kernels  20 us (13%)
  starting transfers between devices  18.9 us (13%)
  between operations  13.5 us (9%)
    all_gather x1, waiting for transfers between devices, body(): gathered = lax.all_gather(own, TEAM, tiled=True)  35.3 us
    all_gather x1, blocking collectives, body(): values = lax.all_gather(solved, 'far', tiled=True)  33.7 us
    all_to_all x1, blocking collectives, body(): lax.all_to_all(corrections, TEAM, split_axis=0, concat_axis=0, tiled=True)  16.5 us
    all_to_all x1, starting transfers between devices, body(): lax.all_to_all(sums, 'far', split_axis=0, concat_axis=0, tiled=True)  12.5 us
    ppermute x1, waiting for transfers between devices, body(): low = lax.ppermute(rim, 'slab', [(i, i + 1) for i in range(slabs - 1)])  7.42 us
    pallas_call x1, Pallas kernels, node_sums(): pl.pallas_call(functools.partial(sums_kernel, doms=doms, stride=stride, t...  5.95 us
    ppermute x1, starting transfers between devices, body(): high = lax.ppermute(rim, 'slab', [(i + 1, i) for i in range(slabs - 1)])  4.49 us
    pallas_call x1, Pallas kernels, back(): pl.pallas_call(back_kernel, out_shape=jax.ShapeDtypeStruct((total, 8, wid...  3.52 us
  transfers between devices with their start and end apart: 4, of which 3 were waited for; matrix products, arithmetic and copies ran while one was open for 0% of the time, Pallas kernels for 4%

profile of v3, /device:TPU:4, one launch (start us, length us, event | category | flops | bytes accessed | tf_op | source)
XLA Modules:
  0.0 148.1 jit_solution(16293142360219678392)
XLA Ops:
  6.5 0.0 all-gather.2.cloned.1.call-start
  6.5 1.5 %pack.1 = f32[16,16,128]{2,1,0:T(8,128)} custom-call(s32[16]{0:T(128)} %bitcast.8, s32[16]{0:T(128)} %slot.1, f32[8,2048]{1,0:T(8,128)} %residual.5, f32[3,2048]{1,0:T(4,128)} %tangents.1, s32[2,2048]{1,0:T(2,128)} %ends.1), custom_call_target="tpu_custom_call" | custom-call | tf_op jit(solution)/shard_map/pack/pallas_call | solution.py:62
  8.1 0.0 all-gather.2.cloned.1.call-update
  8.1 35.3 %all-gather.2.cloned.1.call-done.gathered = f32[128,16,128]{2,1,0:T(8,128)} async-done(((f32[16,16,128]{2,1,0:T(8,128)}), f32[128,16,128]{2,1,0:T(8,128)}) %all-gather.2.cloned.1.call-update) | async-done | bytes 1048592 | tf_op jit(solution)/shard_map/all_gather | solution.py:327
  43.4 6.0 %node_sums.1 = (f32[16,32,128]{2,1,0:T(8,128)}, s32[2,133]{1,0:T(2,128)}) custom-call(s32[1]{0:T(128)} %bitcast.where, f32[128,16,128]{2,1,0:T(8,128)} %all-gather.2.cloned.1.call-done.gathered), custom_call_target="tpu_custom_call" | custom-call | tf_op jit(solution)/shard_map/node_sums/pallas_call | solution.py:129
  49.4 12.5 %all-to-all-start = ((f32[8,64,128]{2,1,0:T(8,128)}), f32[8,64,128]{2,1,0:T(8,128)S(1)}, u32[]{:S(2)}, u32[]{:S(2)}) async-start(f32[8,64,128]{2,1,0:T(8,128)} %bitcast.7), calls=%async_computation | async-start | bytes 524288 | tf_op jit(solution)/shard_map/all_to_all | solution.py:337
  61.9 2.2 %smooth_once.1 = (f32[16,8,128]{2,1,0:T(8,128)}, f32[2,8,128]{2,1,0:T(8,128)}) custom-call(s32[16]{0:T(128)} %kind.3, f32[16]{0:T(128)} %coeff.3, s32[2]{0:T(128)} %halo.1, f32[8,2048]{1,0:T(8,128)} %residual.5, f32[8,128,128]{2,1,0:T(8,128)} %inverse.3), custom_call_target="tpu_custom_call" | custom-call | tf_op jit(solution)/shard_map/smooth_once/pallas_call | solution.py:224
  64.1 4.5 %collective-permute-start.1 = (f32[2,8,128]{2,1,0:T(8,128)}, f32[2,8,128]{2,1,0:T(8,128)S(1)}, u32[]{:S(2)}, u32[]{:S(2)}) collective-permute-start(f32[2,8,128]{2,1,0:T(8,128)} %get-tuple-element.13), channel_id=1, source_target_pairs={{1,0},{2,1},{3,2},{4,3},{5,4},{6,5},{7,6},{9,8},{10,9},{11,10},{12... | collective-permute-start | bytes 24584 | tf_op jit(solution)/shard_map/ppermute | solution.py:332
  68.6 1.9 %collective-permute-start = (f32[2,8,128]{2,1,0:T(8,128)}, f32[2,8,128]{2,1,0:T(8,128)S(1)}, u32[]{:S(2)}, u32[]{:S(2)}) collective-permute-start(f32[2,8,128]{2,1,0:T(8,128)} %get-tuple-element.13), channel_id=1, source_target_pairs={{0,1},{1,2},{2,3},{3,4},{4,5},{5,6},{6,7},{8,9},{9,10},{10,11},{11... | collective-permute-start | bytes 24584 | tf_op jit(solution)/shard_map/ppermute | solution.py:331
  70.5 0.0 collective-permute-done.1.high
  70.5 0.0 copy-start.1
  70.5 7.4 %collective-permute-done.low = f32[2,8,128]{2,1,0:T(8,128)S(1)} collective-permute-done((f32[2,8,128]{2,1,0:T(8,128)}, f32[2,8,128]{2,1,0:T(8,128)S(1)}, u32[]{:S(2)}, u32[]{:S(2)}) %collective-permute-start) | collective-permute-done | bytes 8224 | tf_op jit(solution)/shard_map/ppermute | solution.py:331
  78.0 0.0 copy-start.2
  78.0 0.0 copy-done.1
  78.0 0.6 copy-done.2
  78.5 3.1 %smooth_again.1.smoothed = f32[16,8,128]{2,1,0:T(8,128)} custom-call(s32[16]{0:T(128)} %kind.3, f32[16]{0:T(128)} %coeff.3, s32[8,16]{1,0:T(8,128)} %cols.1, s32[8,16]{1,0:T(8,128)} %kinds.1, f32[8,16]{1,0:T(8,128)} %coeffs.1, f32[16,8,128]{2,1,0:T(8,128)} %get-tuple-element.12.smoothed, f32[2,8,128]{2,1,0:T(8,128)} %copy-done.2, f32[2,8,128]{2,1,0:T(8,128)} %copy-done.1, ...), custom_call_target="tpu_custom_call" | custom-call | tf_op jit(solution)/shard_map/smooth_again/pallas_call | solution.py:268
  81.6 1.5 %all-to-all-done = f32[8,64,128]{2,1,0:T(8,128)S(1)} async-done(((f32[8,64,128]{2,1,0:T(8,128)}), f32[8,64,128]{2,1,0:T(8,128)S(1)}, u32[]{:S(2)}, u32[]{:S(2)}) %all-to-all-start) | async-done | bytes 262176 | tf_op jit(solution)/shard_map/all_to_all | solution.py:337
  83.2 0.0 copy-start
  83.2 0.7 copy-done
  83.9 1.9 %solve.1 = f32[2,32,128]{2,1,0:T(8,128)} custom-call(f32[8,2,32,128]{3,2,1,0:T(8,128)} %bitcast.6, f32[2,128,128]{2,1,0:T(8,128)} %grad.1, f32[2,128,128]{2,1,0:T(8,128)} %vec.1), custom_call_target="tpu_custom_call" | custom-call | tf_op jit(solution)/shard_map/solve/pallas_call | solution.py:159
  85.8 33.7 %all_gather.7.values = f32[16,32,128]{2,1,0:T(8,128)} all-gather(f32[2,32,128]{2,1,0:T(8,128)} %solve.1), channel_id=1, replica_groups=mesh['section'=2,'far'=8,'near'=2,'core'=2,'slab'=8] {'far'}, dimensions={0}, use_global_device_ids=true | all-gather | bytes 294912 | tf_op jit(solution)/shard_map/all_gather | solution.py:346
  119.5 3.5 %back.1 = f32[128,8,128]{2,1,0:T(8,128)} custom-call(s32[2,133]{1,0:T(2,128)} %get-tuple-element.15.chosen, f32[128,16,128]{2,1,0:T(8,128)} %all-gather.2.cloned.1.call-done.gathered, f32[16,32,128]{2,1,0:T(8,128)} %all_gather.7.values), custom_call_target="tpu_custom_call" | custom-call | tf_op jit(solution)/shard_map/back/pallas_call | solution.py:196
  123.0 16.5 %all_to_all.10.pieces = f32[8,16,8,128]{3,2,1,0:T(8,128)} all-to-all(f32[8,16,8,128]{3,2,1,0:T(8,128)} %bitcast.5), channel_id=1, replica_groups=mesh['section'=2,'far'=8,'near'=2,'core'=2,'slab'=8] {'section','near','..., dimensions={0} | all-to-all | bytes 1048576 | tf_op jit(solution)/shard_map/all_to_all | solution.py:348
  139.5 1.7 %finish.1 = f32[8,2048]{1,0:T(8,128)} custom-call(f32[16,8,128]{2,1,0:T(8,128)} %smooth_again.1.smoothed, f32[8,16,8,128]{3,2,1,0:T(8,128)} %all_to_all.10.pieces), custom_call_target="tpu_custom_call" | custom-call | tf_op jit(solution)/shard_map/finish/pallas_call | solution.py:292
Async XLA Ops:
  6.5 36.9 %all-gather.2.cloned.1.call-start = ((), (), s32[]{:S(2)}) async-start(), calls=%async_computation.2 | async-start | bytes 1179648 | tf_op jit(solution)/shard_map/all_gather | solution.py:327
  49.4 33.8 %all-to-all-start = ((f32[8,64,128]{2,1,0:T(8,128)}), f32[8,64,128]{2,1,0:T(8,128)S(1)}, u32[]{:S(2)}, u32[]{:S(2)}) async-start(f32[8,64,128]{2,1,0:T(8,128)} %bitcast.7), calls=%async_computation | async-start | bytes 524288 | tf_op jit(solution)/shard_map/all_to_all | solution.py:337
  64.1 6.4 %collective-permute-start.1 = (f32[2,8,128]{2,1,0:T(8,128)}, f32[2,8,128]{2,1,0:T(8,128)S(1)}, u32[]{:S(2)}, u32[]{:S(2)}) collective-permute-start(f32[2,8,128]{2,1,0:T(8,128)} %get-tuple-element.13), channel_id=1, source_target_pairs={{1,0},{2,1},{3,2},{4,3},{5,4},{6,5},{7,6},{9,8},{10,9},{11,10},{12... | collective-permute-start | bytes 24584 | tf_op jit(solution)/shard_map/ppermute | solution.py:332
  68.6 9.4 %collective-permute-start = (f32[2,8,128]{2,1,0:T(8,128)}, f32[2,8,128]{2,1,0:T(8,128)S(1)}, u32[]{:S(2)}, u32[]{:S(2)}) collective-permute-start(f32[2,8,128]{2,1,0:T(8,128)} %get-tuple-element.13), channel_id=1, source_target_pairs={{0,1},{1,2},{2,3},{3,4},{4,5},{5,6},{6,7},{8,9},{9,10},{10,11},{11... | collective-permute-start | bytes 24584 | tf_op jit(solution)/shard_map/ppermute | solution.py:331
  70.5 7.4 %copy-start.1 = (f32[2,8,128]{2,1,0:T(8,128)}, f32[2,8,128]{2,1,0:T(8,128)S(1)}, u32[]{:S(2)}) copy-start(f32[2,8,128]{2,1,0:T(8,128)S(1)} %collective-permute-done.1.high) | copy-start | bytes 24580
  78.0 0.6 copy-start.2
  83.2 0.7 copy-start
Sparse Core Ops, SparseCore 0:
  9.5 33.8 all-gather.1

commit v4 on v2

--- a/solution.py
+++ b/solution.py
@@ -20,6 +20,14 @@
 any_spec = pl.BlockSpec(memory_space=pl.ANY)
 
 
+def held(shape):
+    return pltpu.VMEM(shape, F32)
+
+
+def hold(x):
+    return pltpu.with_memory_space_constraint(x, VMEM)
+
+
 def split(x):
     high = x.astype(BF16)
     low = (x - high.astype(F32)).astype(BF16)
@@ -61,26 +69,22 @@
     width = residual.shape[1] // tiles
     return pl.pallas_call(
         pack_kernel,
-        out_shape=jax.ShapeDtypeStruct((tiles, 16, width), F32),
+        out_shape=held((tiles, 16, width)),
         in_specs=[smem_spec, smem_spec, vmem_spec, vmem_spec, vmem_spec],
         out_specs=vmem_spec,
         name="pack",
     )(owner, slot, residual, tangents, ends)
 
 
-def sums_kernel(where, gathered, sums, chosen, buf, meta, sems, *, doms, stride, team, tiles, group):
-    width = buf.shape[2]
-    total = team * tiles
+def sums_kernel(where, gathered, sums, chosen, meta, sems, *, doms, stride, team, tiles, group):
+    width = gathered.shape[2]
     copies = [
         pltpu.make_async_copy(gathered.at[q * tiles, pl.ds(8, 8), :], meta.at[q], sems.at[q])
         for q in range(team)
     ]
     for copy in copies:
         copy.start()
-    data = pltpu.make_async_copy(gathered, buf.at[pl.ds(0, total)], sems.at[team])
-    data.start()
     sums[...] = jnp.zeros_like(sums)
-    buf[total] = jnp.zeros(buf.shape[1:], F32)
     for copy in copies:
         copy.wait()
     mine = where[0]
@@ -98,19 +102,18 @@
             count = jnp.where(cls == mine, count + 1, count)
     chosen[0, 0] = count
     for extra in range(group):
-        chosen[0, count + 1 + extra] = total
+        chosen[0, count + 1 + extra] = 0
         chosen[1, count + 1 + extra] = 0
-    data.wait()
     nodes = lax.broadcasted_iota(jnp.int32, (width, width), 0).astype(F32)
 
     def step(i, carry):
         for j in range(group):
             at = i * group + j + 1
             tile, local = chosen[0, at], chosen[1, at]
-            rows = buf[tile, 0:8, :]
-            halves = 0.5 * buf[tile, 8:11, :]
-            at_a = (nodes == buf[tile, 11:12, :]).astype(F32)
-            at_b = (nodes == buf[tile, 12:13, :]).astype(F32)
+            rows = gathered[tile, 0:8, :] * jnp.where(at <= count, 1.0, 0.0)
+            halves = 0.5 * gathered[tile, 8:11, :]
+            at_a = (nodes == gathered[tile, 11:12, :]).astype(F32)
+            at_b = (nodes == gathered[tile, 12:13, :]).astype(F32)
             plus = (at_a + at_b).astype(BF16)
             minus = (at_b - at_a).astype(BF16)
             vec = jnp.concatenate([halves[c : c + 1] * rows for c in range(3)], axis=0)
@@ -131,18 +134,17 @@
             sums_kernel, doms=doms, stride=stride, team=team, tiles=total // team, group=group
         ),
         out_shape=(
-            jax.ShapeDtypeStruct((places, 32, width), F32),
+            held((places, 32, width)),
             jax.ShapeDtypeStruct((2, total + 1 + group), jnp.int32),
         ),
-        in_specs=[smem_spec, any_spec],
+        in_specs=[smem_spec, vmem_spec],
         out_specs=(vmem_spec, smem_spec),
         scratch_shapes=[
-            VMEM((total + 1, 16, width), F32),
             SMEM((team, 8, width), F32),
-            pltpu.SemaphoreType.DMA((team + 1,)),
+            pltpu.SemaphoreType.DMA((team,)),
         ],
         name="node_sums",
-    )(where, gathered)
+    )(where, hold(gathered))
 
 
 def solve_kernel(arrived, grad, vec, out):
@@ -158,32 +160,29 @@
 def solve(arrived, grad, vec):
     return pl.pallas_call(
         solve_kernel,
-        out_shape=jax.ShapeDtypeStruct(arrived.shape[1:], F32),
+        out_shape=held(arrived.shape[1:]),
         in_specs=[vmem_spec] * 3,
         out_specs=vmem_spec,
         name="solve",
-    )(arrived, grad, vec)
-
-
-def back_kernel(chosen, gathered, values, out, buf, sem):
-    data = pltpu.make_async_copy(gathered.at[:, pl.ds(8, 8), :], buf, sem)
-    data.start()
+    )(hold(arrived), hold(grad), hold(vec))
+
+
+def back_kernel(chosen, gathered, values, out):
     out[...] = jnp.zeros_like(out)
-    data.wait()
-    width = buf.shape[2]
+    width = gathered.shape[2]
 
     def pick(rows, index):
         return jnp.take_along_axis(rows, index, axis=1)
 
     def step(i, carry):
         tile, local = chosen[0, i + 1], chosen[1, i + 1]
-        index_a = jnp.broadcast_to(buf[tile, 3:4, :].astype(jnp.int32), (8, width))
-        index_b = jnp.broadcast_to(buf[tile, 4:5, :].astype(jnp.int32), (8, width))
+        index_a = jnp.broadcast_to(gathered[tile, 11:12, :].astype(jnp.int32), (8, width))
+        index_b = jnp.broadcast_to(gathered[tile, 12:13, :].astype(jnp.int32), (8, width))
         grad = values[local, 0:8, :]
         total = pick(grad, index_b) - pick(grad, index_a)
         for c in range(3):
             rows = values[local, 8 + 8 * c : 16 + 8 * c, :]
-            half = 0.5 * buf[tile, c : c + 1, :]
+            half = 0.5 * gathered[tile, 8 + c : 9 + c, :]
             total = total + half * (pick(rows, index_a) + pick(rows, index_b))
         out[tile] = total
         return carry
@@ -195,12 +194,11 @@
     total, _, width = gathered.shape
     return pl.pallas_call(
         back_kernel,
-        out_shape=jax.ShapeDtypeStruct((total, 8, width), F32),
-        in_specs=[smem_spec, any_spec, vmem_spec],
-        out_specs=vmem_spec,
-        scratch_shapes=[VMEM((total, 8, width), F32), pltpu.SemaphoreType.DMA(())],
+        out_shape=held((total, 8, width)),
+        in_specs=[smem_spec, vmem_spec, vmem_spec],
+        out_specs=vmem_spec,
         name="back",
-    )(chosen, gathered, values)
+    )(chosen, hold(gathered), hold(values))
 
 
 def by_tile(ref, tiles, width):
@@ -224,14 +222,14 @@
     return pl.pallas_call(
         smooth_kernel,
         out_shape=(
-            jax.ShapeDtypeStruct((tiles, 8, width), F32),
-            jax.ShapeDtypeStruct((halo.shape[0], 8, width), F32),
+            held((tiles, 8, width)),
+            held((halo.shape[0], 8, width)),
         ),
         in_specs=[smem_spec] * 3 + [vmem_spec] * 2,
         out_specs=(vmem_spec, vmem_spec),
         scratch_shapes=[VMEM((kinds, tiles, 8, width), F32)],
         name="smooth_once",
-    )(kind, coeff, halo, residual, inverse)
+    )(kind, coeff, halo, hold(residual), hold(inverse))
 
 
 def again_kernel(
@@ -267,7 +265,7 @@
     count = tiles + low.shape[0] + high.shape[0]
     return pl.pallas_call(
         again_kernel,
-        out_shape=jax.ShapeDtypeStruct((tiles, 8, width), F32),
+        out_shape=held((tiles, 8, width)),
         in_specs=[smem_spec] * 5 + [vmem_spec] * 6,
         out_specs=vmem_spec,
         scratch_shapes=[
@@ -275,7 +273,10 @@
             VMEM((tiles, 8, width), F32),
         ],
         name="smooth_again",
-    )(kind, coeff, cols, kinds, coeffs, smoothed, low, high, residual, coupling, inverse)
+    )(
+        kind, coeff, cols, kinds, coeffs,
+        hold(smoothed), hold(low), hold(high), hold(residual), hold(coupling), hold(inverse),
+    )
 
 
 def finish_kernel(smoothed, pieces, out):
@@ -295,7 +296,7 @@
         in_specs=[vmem_spec] * 2,
         out_specs=vmem_spec,
         name="finish",
-    )(smoothed, pieces)
+    )(hold(smoothed), hold(pieces))
 
 
 TEAM = ("section", "near", "core")

time: 116 us -> 103 us (0.89)
  Pallas kernels: 18.8 us -> 11.8 us
  blocking collectives: 55 us -> 48.4 us
  waiting for transfers between devices: 17.5 us -> 20 us
  local copies, waits for them, and re-layouts: 1.4 us -> 0.03 us
    pallas_call x5, Pallas kernels: 12.8 us -> 6.75 us  [the longest x1 2.17 us: back(): pl.pallas_call(back_kernel, out_shape=held((total, 8, width)), in_specs=[...]
    all_gather x1, blocking collectives: 36.1 us -> 32.8 us  [body(): values = lax.all_gather(solved, 'far', tiled=True)]
    all_to_all x1, waiting for transfers between devices: 10 us -> 12.7 us  [body(): lax.all_to_all(sums, 'far', split_axis=0, concat_axis=0, tiled=True)]
    all_to_all x1, blocking collectives: 10.2 us -> 8.43 us  [body(): lax.all_to_all(corrections, TEAM, split_axis=0, concat_axis=0, tiled=True)]
    all_gather x1, blocking collectives: 8.67 us -> 7.17 us  [body(): gathered = lax.all_gather(own, TEAM, tiled=True)]
    unnamed x6 -> x10, local copies, waits for them, and re-layouts: 1.4 us -> 0.03 us
  transfers between devices with their start and end apart: 3 -> 3, of which waited for: 2 -> 2; matrix products, arithmetic and copies ran while one was open for 0% -> 0% of each run, Pallas kernels for 5% -> 3%
where the time goes in v4:
time: 103 us; the launch traced here: 102 us
  blocking collectives  48.4 us (47%)
  starting transfers between devices  21.3 us (21%)
  waiting for transfers between devices  20 us (19%)
  Pallas kernels  11.8 us (11%)
    all_gather x1, blocking collectives, body(): values = lax.all_gather(solved, 'far', tiled=True)  32.8 us
    all_to_all x1, starting transfers between devices, body(): lax.all_to_all(sums, 'far', split_axis=0, concat_axis=0, tiled=True)  15.1 us
    all_to_all x1, waiting for transfers between devices, body(): lax.all_to_all(sums, 'far', split_axis=0, concat_axis=0, tiled=True)  12.7 us
    all_to_all x1, blocking collectives, body(): lax.all_to_all(corrections, TEAM, split_axis=0, concat_axis=0, tiled=True)  8.43 us
    ppermute x1, waiting for transfers between devices, body(): high = lax.ppermute(rim, 'slab', [(i + 1, i) for i in range(slabs - 1)])  7.22 us
    all_gather x1, blocking collectives, body(): gathered = lax.all_gather(own, TEAM, tiled=True)  7.17 us
    pallas_call x1, Pallas kernels, node_sums(): pl.pallas_call(functools.partial(sums_kernel, doms=doms, stride=stride, t...  4.44 us
    ppermute x1, starting transfers between devices, body(): low = lax.ppermute(rim, 'slab', [(i, i + 1) for i in range(slabs - 1)])  4.3 us
  transfers between devices with their start and end apart: 3, of which 2 were waited for; matrix products, arithmetic and copies ran while one was open for 0% of the time, Pallas kernels for 3%

profile of v4, /device:TPU:24, one launch (start us, length us, event | category | flops | bytes accessed | tf_op | source)
XLA Modules:
  0.0 101.7 jit_solution(12544510805332959729)
XLA Ops:
  0.0 0.9 pack.1
  0.9 7.2 %all_gather.6.gathered = f32[64,16,128]{2,1,0:T(8,128)S(1)} all-gather(f32[16,16,128]{2,1,0:T(8,128)S(1)} %pack.1), channel_id=1, replica_groups=mesh['section'=2,'far'=16,'near'=1,'core'=2,'slab'=8] {'section','near',..., dimensions={0}, use_global_device_ids=true | all-gather | bytes 655360 | tf_op jit(solution)/shard_map/all_gather | solution.py:328
  8.1 4.4 %node_sums.1 = (f32[32,32,128]{2,1,0:T(8,128)}, s32[2,69]{1,0:T(2,128)}) custom-call(s32[1]{0:T(128)} %bitcast.where, f32[64,16,128]{2,1,0:T(8,128)S(1)} %all_gather.6.gathered), custom_call_target="tpu_custom_call" | custom-call | tf_op jit(solution)/shard_map/node_sums/pallas_call | solution.py:132
  12.5 0.0 copy-start
  12.5 0.0 copy-start.1
  12.6 15.1 %all-to-all-start = ((f32[16,64,128]{2,1,0:T(8,128)}), f32[16,64,128]{2,1,0:T(8,128)S(1)}, u32[]{:S(2)}, u32[]{:S(2)}) async-start(f32[16,64,128]{2,1,0:T(8,128)} %bitcast.2), calls=%async_computation | async-start | bytes 1048576 | tf_op jit(solution)/shard_map/all_to_all | solution.py:338
  27.6 0.0 copy-done
  27.6 0.0 copy-done.1
  27.6 0.0 copy-start.2
  27.6 1.3 %smooth_once.1 = (f32[16,8,128]{2,1,0:T(8,128)S(1)}, f32[2,8,128]{2,1,0:T(8,128)S(1)}) custom-call(s32[16]{0:T(128)} %kind.3, f32[16]{0:T(128)} %coeff.3, s32[2]{0:T(128)} %halo.1, f32[8,2048]{1,0:T(8,128)S(1)} %copy-done.1, f32[8,128,128]{2,1,0:T(8,128)S(1)} %copy-done), custom_call_target="tpu_custom_call" | custom-call | tf_op jit(solution)/shard_map/smooth_once/pallas_call | solution.py:222
  28.9 4.3 %collective-permute-start = (f32[2,8,128]{2,1,0:T(8,128)S(1)}, f32[2,8,128]{2,1,0:T(8,128)S(1)}, u32[]{:S(2)}, u32[]{:S(2)}) collective-permute-start(f32[2,8,128]{2,1,0:T(8,128)S(1)} %get-tuple-element.13), channel_id=1, source_target_pairs={{0,1},{1,2},{2,3},{3,4},{4,5},{5,6},{6,7},{8,9},{9,10},{10,11},{11... | collective-permute-start | bytes 24584 | tf_op jit(solution)/shard_map/ppermute | solution.py:332
  33.2 1.9 %collective-permute-start.1 = (f32[2,8,128]{2,1,0:T(8,128)S(1)}, f32[2,8,128]{2,1,0:T(8,128)S(1)}, u32[]{:S(2)}, u32[]{:S(2)}) collective-permute-start(f32[2,8,128]{2,1,0:T(8,128)S(1)} %get-tuple-element.13), channel_id=1, source_target_pairs={{1,0},{2,1},{3,2},{4,3},{5,4},{6,5},{7,6},{9,8},{10,9},{11,10},{12... | collective-permute-start | bytes 24584 | tf_op jit(solution)/shard_map/ppermute | solution.py:333
  35.2 0.0 collective-permute-done.low
  35.2 7.2 %collective-permute-done.1.high = f32[2,8,128]{2,1,0:T(8,128)S(1)} collective-permute-done((f32[2,8,128]{2,1,0:T(8,128)S(1)}, f32[2,8,128]{2,1,0:T(8,128)S(1)}, u32[]{:S(2)}, u32[]{:S(2)}) %collective-permute-start.1) | collective-permute-done | bytes 8224 | tf_op jit(solution)/shard_map/ppermute | solution.py:333
  42.4 0.0 copy-done.2
  42.4 2.2 %smooth_again.1.smoothed = f32[16,8,128]{2,1,0:T(8,128)S(1)} custom-call(s32[16]{0:T(128)} %kind.3, f32[16]{0:T(128)} %coeff.3, s32[8,16]{1,0:T(8,128)} %cols.1, s32[8,16]{1,0:T(8,128)} %kinds.1, f32[8,16]{1,0:T(8,128)} %coeffs.1, f32[16,8,128]{2,1,0:T(8,128)S(1)} %get-tuple-element.12.smoothed, f32[2,8,128]{2,1,0:T(8,128)S(1)} %collective-permute-done.low, ...), custom_call_target="tpu_custom_call" | custom-call | tf_op jit(solution)/shard_map/smooth_again/pallas_call | solution.py:266
  44.6 12.7 %all-to-all-done = f32[16,64,128]{2,1,0:T(8,128)S(1)} async-done(((f32[16,64,128]{2,1,0:T(8,128)}), f32[16,64,128]{2,1,0:T(8,128)S(1)}, u32[]{:S(2)}, u32[]{:S(2)}) %all-to-all-start) | async-done | bytes 524320 | tf_op jit(solution)/shard_map/all_to_all | solution.py:338
  57.3 0.0 copy-done.3
  57.3 0.0 copy-done.4
  57.3 0.2 solve.1
  57.6 32.8 %all_gather.7.values = f32[32,32,128]{2,1,0:T(8,128)S(1)} all-gather(f32[2,32,128]{2,1,0:T(8,128)S(1)} %solve.1), channel_id=1, replica_groups=mesh['section'=2,'far'=16,'near'=1,'core'=2,'slab'=8] {'far'}, dimensions={0}, use_global_device_ids=true | all-gather | bytes 557056 | tf_op jit(solution)/shard_map/all_gather | solution.py:347
  90.4 2.2 %back.1 = f32[64,8,128]{2,1,0:T(8,128)S(1)} custom-call(s32[2,69]{1,0:T(2,128)} %get-tuple-element.15.chosen, f32[64,16,128]{2,1,0:T(8,128)S(1)} %all_gather.6.gathered, f32[32,32,128]{2,1,0:T(8,128)S(1)} %all_gather.7.values), custom_call_target="tpu_custom_call" | custom-call | tf_op jit(solution)/shard_map/back/pallas_call | solution.py:195
  92.6 8.4 %all_to_all.10.pieces = f32[4,16,8,128]{3,2,1,0:T(8,128)S(1)} all-to-all(f32[4,16,8,128]{3,2,1,0:T(8,128)S(1)} %bitcast.6), channel_id=1, replica_groups=mesh['section'=2,'far'=16,'near'=1,'core'=2,'slab'=8] {'section','near',..., dimensions={0} | all-to-all | bytes 524288 | tf_op jit(solution)/shard_map/all_to_all | solution.py:349
  101.0 0.6 finish.1
  (2 shorter events, 0.0 us)
Async XLA Ops:
  12.5 15.1 %copy-start = (f32[8,128,128]{2,1,0:T(8,128)S(1)}, f32[8,128,128]{2,1,0:T(8,128)}, u32[]{:S(2)}) copy-start(f32[8,128,128]{2,1,0:T(8,128)} %inverse.3) | copy-start | bytes 1572868
  12.5 15.1 %copy-start.1 = (f32[8,2048]{1,0:T(8,128)S(1)}, f32[8,2048]{1,0:T(8,128)}, u32[]{:S(2)}) copy-start(f32[8,2048]{1,0:T(8,128)} %residual.5) | copy-start | bytes 196612
  12.6 44.8 %all-to-all-start = ((f32[16,64,128]{2,1,0:T(8,128)}), f32[16,64,128]{2,1,0:T(8,128)S(1)}, u32[]{:S(2)}, u32[]{:S(2)}) async-start(f32[16,64,128]{2,1,0:T(8,128)} %bitcast.2), calls=%async_computation | async-start | bytes 1048576 | tf_op jit(solution)/shard_map/all_to_all | solution.py:338
  27.6 14.8 %copy-start.2 = (f32[8,128,128]{2,1,0:T(8,128)S(1)}, f32[8,128,128]{2,1,0:T(8,128)}, u32[]{:S(2)}) copy-start(f32[8,128,128]{2,1,0:T(8,128)} %coupling.1) | copy-start | bytes 1572868
  28.9 6.2 %collective-permute-start = (f32[2,8,128]{2,1,0:T(8,128)S(1)}, f32[2,8,128]{2,1,0:T(8,128)S(1)}, u32[]{:S(2)}, u32[]{:S(2)}) collective-permute-start(f32[2,8,128]{2,1,0:T(8,128)S(1)} %get-tuple-element.13), channel_id=1, source_target_pairs={{0,1},{1,2},{2,3},{3,4},{4,5},{5,6},{6,7},{8,9},{9,10},{10,11},{11... | collective-permute-start | bytes 24584 | tf_op jit(solution)/shard_map/ppermute | solution.py:332
  33.2 9.2 %collective-permute-start.1 = (f32[2,8,128]{2,1,0:T(8,128)S(1)}, f32[2,8,128]{2,1,0:T(8,128)S(1)}, u32[]{:S(2)}, u32[]{:S(2)}) collective-permute-start(f32[2,8,128]{2,1,0:T(8,128)S(1)} %get-tuple-element.13), channel_id=1, source_target_pairs={{1,0},{2,1},{3,2},{4,3},{5,4},{6,5},{7,6},{9,8},{10,9},{11,10},{12... | collective-permute-start | bytes 24584 | tf_op jit(solution)/shard_map/ppermute | solution.py:333
  42.4 14.9 %copy-start.3 = (f32[2,128,128]{2,1,0:T(8,128)S(1)}, f32[2,128,128]{2,1,0:T(8,128)}, u32[]{:S(2)}) copy-start(f32[2,128,128]{2,1,0:T(8,128)} %grad.1) | copy-start | bytes 393220
  42.4 14.9 %copy-start.4 = (f32[2,128,128]{2,1,0:T(8,128)S(1)}, f32[2,128,128]{2,1,0:T(8,128)}, u32[]{:S(2)}) copy-start(f32[2,128,128]{2,1,0:T(8,128)} %vec.1) | copy-start | bytes 393220

commit v5 on v4

--- a/solution.py
+++ b/solution.py
@@ -10,6 +10,7 @@
 DAMPING = 0.7
 CORES = 2
 NEAR = 1
+GROUP = 8
 F32 = jnp.float32
 BF16 = jnp.bfloat16
 SMEM = pltpu.SMEM
@@ -50,25 +51,37 @@
     return jnp.concatenate([high, low], axis=0)
 
 
-def pack_kernel(owner, slot, residual, tangents, ends, out):
+def parts_of(x, size):
+    if size & (size - 1) == 0:
+        return lax.shift_right_logical(x, jnp.int32(size.bit_length() - 1)), x & (size - 1)
+    return x // size, x % size
+
+
+def pack_kernel(owner, slot, residual, tangents, ends, out, *, doms, stride):
     tiles, width = out.shape[0], out.shape[2]
     lanes = lax.broadcasted_iota(jnp.int32, (1, width), 1)
-    row = jnp.zeros((1, width), jnp.int32)
-    for t in range(tiles):
-        row = jnp.where(lanes == t, owner[t] * 2 + slot[t], row)
+    owners = jnp.zeros((1, width), jnp.int32)
+    slots = jnp.zeros((1, width), jnp.int32)
+    for t in range(tiles):
+        owners = jnp.where(lanes == t, owner[t], owners)
+        slots = jnp.where(lanes == t, slot[t], slots)
+    section, dom = parts_of(owners, doms)
+    z, core = parts_of(dom, CORES)
+    far, near = parts_of(z, stride)
     for t in range(tiles):
         part = slice(t * width, (t + 1) * width)
         out[t, 0:8, :] = residual[:, part]
         out[t, 8:11, :] = tangents[:, part]
         out[t, 11:13, :] = ends[:, part].astype(F32)
-        out[t, 13:14, :] = row.astype(F32)
-
-
-def pack(owner, slot, residual, tangents, ends):
+    out[0, 13:14, :] = ((section * stride + near) * CORES + core).astype(F32)
+    out[0, 14:15, :] = (far * 2 + slots).astype(F32)
+
+
+def pack(owner, slot, residual, tangents, ends, doms, stride):
     tiles = owner.shape[0]
     width = residual.shape[1] // tiles
     return pl.pallas_call(
-        pack_kernel,
+        functools.partial(pack_kernel, doms=doms, stride=stride),
         out_shape=held((tiles, 16, width)),
         in_specs=[smem_spec, smem_spec, vmem_spec, vmem_spec, vmem_spec],
         out_specs=vmem_spec,
@@ -76,7 +89,7 @@
     )(owner, slot, residual, tangents, ends)
 
 
-def sums_kernel(where, gathered, sums, chosen, meta, sems, *, doms, stride, team, tiles, group):
+def sums_kernel(where, gathered, sums, chosen, meta, sems, *, team, tiles, group):
     width = gathered.shape[2]
     copies = [
         pltpu.make_async_copy(gathered.at[q * tiles, pl.ds(8, 8), :], meta.at[q], sems.at[q])
@@ -87,23 +100,19 @@
     sums[...] = jnp.zeros_like(sums)
     for copy in copies:
         copy.wait()
-    mine = where[0]
+    mine = where[0].astype(F32)
 
     count = jnp.int32(0)
     for q in range(team):
         for t in range(tiles):
-            dst = meta[q, 5, t].astype(jnp.int32)
-            owner, slot = dst // 2, dst % 2
-            section, dom = owner // doms, owner % doms
-            z, core = dom // CORES, dom % CORES
-            cls = (section * stride + z % stride) * CORES + core
             chosen[0, count + 1] = q * tiles + t
-            chosen[1, count + 1] = (z // stride) * 2 + slot
-            count = jnp.where(cls == mine, count + 1, count)
+            chosen[1, count + 1] = meta[q, 6, t].astype(jnp.int32)
+            count = count + (meta[q, 5, t] == mine).astype(jnp.int32)
     chosen[0, 0] = count
+    last, place = chosen[0, count], chosen[1, count]
     for extra in range(group):
-        chosen[0, count + 1 + extra] = 0
-        chosen[1, count + 1 + extra] = 0
+        chosen[0, count + 1 + extra] = last
+        chosen[1, count + 1 + extra] = place
     nodes = lax.broadcasted_iota(jnp.int32, (width, width), 0).astype(F32)
 
     def step(i, carry):
@@ -126,16 +135,13 @@
     lax.fori_loop(0, (count + group - 1) // group, step, 0)
 
 
-def node_sums(where, gathered, team, places, doms, stride):
+def node_sums(where, gathered, team, places):
     total, _, width = gathered.shape
-    group = 4
-    return pl.pallas_call(
-        functools.partial(
-            sums_kernel, doms=doms, stride=stride, team=team, tiles=total // team, group=group
-        ),
+    return pl.pallas_call(
+        functools.partial(sums_kernel, team=team, tiles=total // team, group=GROUP),
         out_shape=(
             held((places, 32, width)),
-            jax.ShapeDtypeStruct((2, total + 1 + group), jnp.int32),
+            jax.ShapeDtypeStruct((2, total + 1 + GROUP), jnp.int32),
         ),
         in_specs=[smem_spec, vmem_spec],
         out_specs=(vmem_spec, smem_spec),
@@ -175,19 +181,21 @@
         return jnp.take_along_axis(rows, index, axis=1)
 
     def step(i, carry):
-        tile, local = chosen[0, i + 1], chosen[1, i + 1]
-        index_a = jnp.broadcast_to(gathered[tile, 11:12, :].astype(jnp.int32), (8, width))
-        index_b = jnp.broadcast_to(gathered[tile, 12:13, :].astype(jnp.int32), (8, width))
-        grad = values[local, 0:8, :]
-        total = pick(grad, index_b) - pick(grad, index_a)
-        for c in range(3):
-            rows = values[local, 8 + 8 * c : 16 + 8 * c, :]
-            half = 0.5 * gathered[tile, 8 + c : 9 + c, :]
-            total = total + half * (pick(rows, index_a) + pick(rows, index_b))
-        out[tile] = total
+        for j in range(GROUP):
+            at = i * GROUP + j + 1
+            tile, local = chosen[0, at], chosen[1, at]
+            index_a = jnp.broadcast_to(gathered[tile, 11:12, :].astype(jnp.int32), (8, width))
+            index_b = jnp.broadcast_to(gathered[tile, 12:13, :].astype(jnp.int32), (8, width))
+            grad = values[local, 0:8, :]
+            total = pick(grad, index_b) - pick(grad, index_a)
+            for c in range(3):
+                rows = values[local, 8 + 8 * c : 16 + 8 * c, :]
+                half = 0.5 * gathered[tile, 8 + c : 9 + c, :]
+                total = total + half * (pick(rows, index_a) + pick(rows, index_b))
+            out[tile] = total
         return carry
 
-    lax.fori_loop(0, chosen[0, 0], step, 0)
+    lax.fori_loop(0, (chosen[0, 0] + GROUP - 1) // GROUP, step, 0)
 
 
 def back(chosen, gathered, values):
@@ -324,7 +332,8 @@
     tiles = diag_kind.shape[0]
     width = coupling_tiles.shape[1]
     where = lax.axis_index(TEAM).astype(jnp.int32).reshape(1)
-    own = pack(tile_owner[:, 0], node_slot, residual, tangents, edge_nodes)
+    doms = heights * stride * CORES
+    own = pack(tile_owner[:, 0], node_slot, residual, tangents, edge_nodes, doms, stride)
     gathered = lax.all_gather(own, TEAM, tiled=True)
 
     smoothed, rim = smooth(diag_kind, diag_coeff, halo_rows, residual, inverse_tiles)
@@ -332,8 +341,7 @@
     low = lax.ppermute(rim, "slab", [(i, i + 1) for i in range(slabs - 1)])
     high = lax.ppermute(rim, "slab", [(i + 1, i) for i in range(slabs - 1)])
 
-    doms = heights * stride * CORES
-    sums, chosen = node_sums(where, gathered, team, heights * node_tiles, doms, stride)
+    sums, chosen = node_sums(where, gathered, team, heights * node_tiles)
     sums = sums.reshape(heights, node_tiles * 32, width)
     arrived = lax.all_to_all(sums, "far", split_axis=0, concat_axis=0, tiled=True)
 

time: 103 us -> 101 us (0.981)
  Pallas kernels: 11.8 us -> 9.97 us
where the time goes in v5:
time: 101 us; the launch traced here: 100 us
  blocking collectives  49 us (49%)
  starting transfers between devices  21.6 us (21%)
  waiting for transfers between devices  19.4 us (19%)
  Pallas kernels  9.97 us (10%)
    all_gather x1, blocking collectives, body(): values = lax.all_gather(solved, 'far', tiled=True)  33.4 us
    all_to_all x1, starting transfers between devices, body(): lax.all_to_all(sums, 'far', split_axis=0, concat_axis=0, tiled=True)  15.3 us
    all_to_all x1, waiting for transfers between devices, body(): lax.all_to_all(sums, 'far', split_axis=0, concat_axis=0, tiled=True)  12.2 us
    all_to_all x1, blocking collectives, body(): lax.all_to_all(corrections, TEAM, split_axis=0, concat_axis=0, tiled=True)  8.42 us
    ppermute x1, waiting for transfers between devices, body(): high = lax.ppermute(rim, 'slab', [(i + 1, i) for i in range(slabs - 1)])  7.22 us
    all_gather x1, blocking collectives, body(): gathered = lax.all_gather(own, TEAM, tiled=True)  7.17 us
    ppermute x1, starting transfers between devices, body(): low = lax.ppermute(rim, 'slab', [(i, i + 1) for i in range(slabs - 1)])  4.3 us
    pallas_call x1, Pallas kernels, node_sums(): pl.pallas_call(functools.partial(sums_kernel, team=team, tiles=total // t...  3.41 us
  transfers between devices with their start and end apart: 3, of which 2 were waited for; matrix products, arithmetic and copies ran while one was open for 0% of the time, Pallas kernels for 3%

profile of v5, /device:TPU:24, one launch (start us, length us, event | category | flops | bytes accessed | tf_op | source)
XLA Modules:
  0.0 100.0 jit_solution(3566725733414986371)
XLA Ops:
  0.0 0.9 pack.1
  0.9 7.2 %all_gather.6.gathered = f32[64,16,128]{2,1,0:T(8,128)S(1)} all-gather(f32[16,16,128]{2,1,0:T(8,128)S(1)} %pack.1), channel_id=1, replica_groups=mesh['section'=2,'far'=16,'near'=1,'core'=2,'slab'=8] {'section','near',..., dimensions={0}, use_global_device_ids=true | all-gather | bytes 655360 | tf_op jit(solution)/shard_map/all_gather | solution.py:337
  8.1 3.4 %node_sums.1 = (f32[32,32,128]{2,1,0:T(8,128)}, s32[2,73]{1,0:T(2,128)}) custom-call(s32[1]{0:T(128)} %bitcast.where, f32[64,16,128]{2,1,0:T(8,128)S(1)} %all_gather.6.gathered), custom_call_target="tpu_custom_call" | custom-call | tf_op jit(solution)/shard_map/node_sums/pallas_call | solution.py:140
  11.5 0.0 copy-start
  11.5 0.0 copy-start.1
  11.5 15.3 %all-to-all-start = ((f32[16,64,128]{2,1,0:T(8,128)}), f32[16,64,128]{2,1,0:T(8,128)S(1)}, u32[]{:S(2)}, u32[]{:S(2)}) async-start(f32[16,64,128]{2,1,0:T(8,128)} %bitcast.2), calls=%async_computation | async-start | bytes 1048576 | tf_op jit(solution)/shard_map/all_to_all | solution.py:346
  26.9 0.0 copy-done
  26.9 0.0 copy-done.1
  26.9 0.0 copy-start.2
  26.9 1.3 %smooth_once.1 = (f32[16,8,128]{2,1,0:T(8,128)S(1)}, f32[2,8,128]{2,1,0:T(8,128)S(1)}) custom-call(s32[16]{0:T(128)} %kind.3, f32[16]{0:T(128)} %coeff.3, s32[2]{0:T(128)} %halo.1, f32[8,2048]{1,0:T(8,128)S(1)} %copy-done.1, f32[8,128,128]{2,1,0:T(8,128)S(1)} %copy-done), custom_call_target="tpu_custom_call" | custom-call | tf_op jit(solution)/shard_map/smooth_once/pallas_call | solution.py:230
  28.2 4.3 %collective-permute-start = (f32[2,8,128]{2,1,0:T(8,128)S(1)}, f32[2,8,128]{2,1,0:T(8,128)S(1)}, u32[]{:S(2)}, u32[]{:S(2)}) collective-permute-start(f32[2,8,128]{2,1,0:T(8,128)S(1)} %get-tuple-element.13), channel_id=1, source_target_pairs={{0,1},{1,2},{2,3},{3,4},{4,5},{5,6},{6,7},{8,9},{9,10},{10,11},{11... | collective-permute-start | bytes 24584 | tf_op jit(solution)/shard_map/ppermute | solution.py:341
  32.5 1.9 %collective-permute-start.1 = (f32[2,8,128]{2,1,0:T(8,128)S(1)}, f32[2,8,128]{2,1,0:T(8,128)S(1)}, u32[]{:S(2)}, u32[]{:S(2)}) collective-permute-start(f32[2,8,128]{2,1,0:T(8,128)S(1)} %get-tuple-element.13), channel_id=1, source_target_pairs={{1,0},{2,1},{3,2},{4,3},{5,4},{6,5},{7,6},{9,8},{10,9},{11,10},{12... | collective-permute-start | bytes 24584 | tf_op jit(solution)/shard_map/ppermute | solution.py:342
  34.4 0.0 collective-permute-done.low
  34.4 7.2 %collective-permute-done.1.high = f32[2,8,128]{2,1,0:T(8,128)S(1)} collective-permute-done((f32[2,8,128]{2,1,0:T(8,128)S(1)}, f32[2,8,128]{2,1,0:T(8,128)S(1)}, u32[]{:S(2)}, u32[]{:S(2)}) %collective-permute-start.1) | collective-permute-done | bytes 8224 | tf_op jit(solution)/shard_map/ppermute | solution.py:342
  41.7 0.0 copy-done.2
  41.7 2.2 %smooth_again.1.smoothed = f32[16,8,128]{2,1,0:T(8,128)S(1)} custom-call(s32[16]{0:T(128)} %kind.3, f32[16]{0:T(128)} %coeff.3, s32[8,16]{1,0:T(8,128)} %cols.1, s32[8,16]{1,0:T(8,128)} %kinds.1, f32[8,16]{1,0:T(8,128)} %coeffs.1, f32[16,8,128]{2,1,0:T(8,128)S(1)} %get-tuple-element.12.smoothed, f32[2,8,128]{2,1,0:T(8,128)S(1)} %collective-permute-done.low, ...), custom_call_target="tpu_custom_call" | custom-call | tf_op jit(solution)/shard_map/smooth_again/pallas_call | solution.py:274
  43.8 12.2 %all-to-all-done = f32[16,64,128]{2,1,0:T(8,128)S(1)} async-done(((f32[16,64,128]{2,1,0:T(8,128)}), f32[16,64,128]{2,1,0:T(8,128)S(1)}, u32[]{:S(2)}, u32[]{:S(2)}) %all-to-all-start) | async-done | bytes 524320 | tf_op jit(solution)/shard_map/all_to_all | solution.py:346
  56.0 0.0 copy-done.3
  56.0 0.0 copy-done.4
  56.0 0.2 solve.1
  56.3 33.4 %all_gather.7.values = f32[32,32,128]{2,1,0:T(8,128)S(1)} all-gather(f32[2,32,128]{2,1,0:T(8,128)S(1)} %solve.1), channel_id=1, replica_groups=mesh['section'=2,'far'=16,'near'=1,'core'=2,'slab'=8] {'far'}, dimensions={0}, use_global_device_ids=true | all-gather | bytes 557056 | tf_op jit(solution)/shard_map/all_gather | solution.py:355
  89.6 1.3 %back.1 = f32[64,8,128]{2,1,0:T(8,128)S(1)} custom-call(s32[2,73]{1,0:T(2,128)} %get-tuple-element.15.chosen, f32[64,16,128]{2,1,0:T(8,128)S(1)} %all_gather.6.gathered, f32[32,32,128]{2,1,0:T(8,128)S(1)} %all_gather.7.values), custom_call_target="tpu_custom_call" | custom-call | tf_op jit(solution)/shard_map/back/pallas_call | solution.py:203
  91.0 8.4 %all_to_all.10.pieces = f32[4,16,8,128]{3,2,1,0:T(8,128)S(1)} all-to-all(f32[4,16,8,128]{3,2,1,0:T(8,128)S(1)} %bitcast.6), channel_id=1, replica_groups=mesh['section'=2,'far'=16,'near'=1,'core'=2,'slab'=8] {'section','near',..., dimensions={0} | all-to-all | bytes 524288 | tf_op jit(solution)/shard_map/all_to_all | solution.py:357
  99.4 0.6 finish.1
  (2 shorter events, 0.0 us)
Async XLA Ops:
  11.5 15.4 %copy-start = (f32[8,128,128]{2,1,0:T(8,128)S(1)}, f32[8,128,128]{2,1,0:T(8,128)}, u32[]{:S(2)}) copy-start(f32[8,128,128]{2,1,0:T(8,128)} %inverse.3) | copy-start | bytes 1572868
  11.5 15.4 %copy-start.1 = (f32[8,2048]{1,0:T(8,128)S(1)}, f32[8,2048]{1,0:T(8,128)}, u32[]{:S(2)}) copy-start(f32[8,2048]{1,0:T(8,128)} %residual.5) | copy-start | bytes 196612
  11.5 44.5 %all-to-all-start = ((f32[16,64,128]{2,1,0:T(8,128)}), f32[16,64,128]{2,1,0:T(8,128)S(1)}, u32[]{:S(2)}, u32[]{:S(2)}) async-start(f32[16,64,128]{2,1,0:T(8,128)} %bitcast.2), calls=%async_computation | async-start | bytes 1048576 | tf_op jit(solution)/shard_map/all_to_all | solution.py:346
  26.9 14.8 %copy-start.2 = (f32[8,128,128]{2,1,0:T(8,128)S(1)}, f32[8,128,128]{2,1,0:T(8,128)}, u32[]{:S(2)}) copy-start(f32[8,128,128]{2,1,0:T(8,128)} %coupling.1) | copy-start | bytes 1572868
  28.2 6.2 %collective-permute-start = (f32[2,8,128]{2,1,0:T(8,128)S(1)}, f32[2,8,128]{2,1,0:T(8,128)S(1)}, u32[]{:S(2)}, u32[]{:S(2)}) collective-permute-start(f32[2,8,128]{2,1,0:T(8,128)S(1)} %get-tuple-element.13), channel_id=1, source_target_pairs={{0,1},{1,2},{2,3},{3,4},{4,5},{5,6},{6,7},{8,9},{9,10},{10,11},{11... | collective-permute-start | bytes 24584 | tf_op jit(solution)/shard_map/ppermute | solution.py:341
  32.5 9.2 %collective-permute-start.1 = (f32[2,8,128]{2,1,0:T(8,128)S(1)}, f32[2,8,128]{2,1,0:T(8,128)S(1)}, u32[]{:S(2)}, u32[]{:S(2)}) collective-permute-start(f32[2,8,128]{2,1,0:T(8,128)S(1)} %get-tuple-element.13), channel_id=1, source_target_pairs={{1,0},{2,1},{3,2},{4,3},{5,4},{6,5},{7,6},{9,8},{10,9},{11,10},{12... | collective-permute-start | bytes 24584 | tf_op jit(solution)/shard_map/ppermute | solution.py:342
  41.7 14.3 %copy-start.3 = (f32[2,128,128]{2,1,0:T(8,128)S(1)}, f32[2,128,128]{2,1,0:T(8,128)}, u32[]{:S(2)}) copy-start(f32[2,128,128]{2,1,0:T(8,128)} %grad.1) | copy-start | bytes 393220
  41.7 14.3 %copy-start.4 = (f32[2,128,128]{2,1,0:T(8,128)S(1)}, f32[2,128,128]{2,1,0:T(8,128)}, u32[]{:S(2)}) copy-start(f32[2,128,128]{2,1,0:T(8,128)} %vec.1) | copy-start | bytes 393220

commit v6 on v5

--- a/solution.py
+++ b/solution.py
@@ -57,8 +57,12 @@
     return x // size, x % size
 
 
+FIELDS = 5
+
+
 def pack_kernel(owner, slot, residual, tangents, ends, out, *, doms, stride):
-    tiles, width = out.shape[0], out.shape[2]
+    tiles = owner.shape[0]
+    width = residual.shape[1] // tiles
     lanes = lax.broadcasted_iota(jnp.int32, (1, width), 1)
     owners = jnp.zeros((1, width), jnp.int32)
     slots = jnp.zeros((1, width), jnp.int32)
@@ -68,13 +72,17 @@
     section, dom = parts_of(owners, doms)
     z, core = parts_of(dom, CORES)
     far, near = parts_of(z, stride)
+    out[:, 0 : tiles * width] = residual[...]
     for t in range(tiles):
         part = slice(t * width, (t + 1) * width)
-        out[t, 0:8, :] = residual[:, part]
-        out[t, 8:11, :] = tangents[:, part]
-        out[t, 11:13, :] = ends[:, part].astype(F32)
-    out[0, 13:14, :] = ((section * stride + near) * CORES + core).astype(F32)
-    out[0, 14:15, :] = (far * 2 + slots).astype(F32)
+        for f in range(FIELDS):
+            row = tangents[f : f + 1, part] if f < 3 else ends[f - 3 : f - 2, part].astype(F32)
+            at = (tiles + (t // 8) * FIELDS + f) * width
+            out[t % 8 : t % 8 + 1, at : at + width] = row
+    at = (tiles + tiles // 8 * FIELDS) * width
+    out[:, at : at + width] = jnp.zeros((8, width), F32)
+    out[0:1, at : at + width] = ((section * stride + near) * CORES + core).astype(F32)
+    out[1:2, at : at + width] = (far * 2 + slots).astype(F32)
 
 
 def pack(owner, slot, residual, tangents, ends, doms, stride):
@@ -82,32 +90,39 @@
     width = residual.shape[1] // tiles
     return pl.pallas_call(
         functools.partial(pack_kernel, doms=doms, stride=stride),
-        out_shape=held((tiles, 16, width)),
+        out_shape=held((8, (tiles + tiles // 8 * FIELDS + 1) * width)),
         in_specs=[smem_spec, smem_spec, vmem_spec, vmem_spec, vmem_spec],
         out_specs=vmem_spec,
         name="pack",
     )(owner, slot, residual, tangents, ends)
 
 
-def sums_kernel(where, gathered, sums, chosen, meta, sems, *, team, tiles, group):
-    width = gathered.shape[2]
-    copies = [
-        pltpu.make_async_copy(gathered.at[q * tiles, pl.ds(8, 8), :], meta.at[q], sems.at[q])
-        for q in range(team)
-    ]
-    for copy in copies:
-        copy.start()
+def tile_reader(gathered, tile, tiles, width):
+    device, t = parts_of(tile, tiles)
+    block, row = parts_of(t, 8)
+    base = tiles + block * FIELDS
+
+    def lanes(at):
+        return pl.ds(pl.multiple_of(at * width, width), width)
+
+    return (
+        lambda: gathered[device, :, lanes(t)],
+        lambda f: pltpu.roll(gathered[device, :, lanes(base + f)], 8 - row, 0)[0:1],
+    )
+
+
+def sums_kernel(where, gathered, sums, chosen, *, tiles, width, group):
     sums[...] = jnp.zeros_like(sums)
-    for copy in copies:
-        copy.wait()
     mine = where[0].astype(F32)
-
     count = jnp.int32(0)
-    for q in range(team):
+    for q in range(gathered.shape[0]):
+        last_block = gathered[q, :, gathered.shape[2] - width :]
+        codes = jnp.where(last_block[0:1] == mine, last_block[1:2], -1.0).astype(jnp.int32)
         for t in range(tiles):
+            code = codes[0, t]
             chosen[0, count + 1] = q * tiles + t
-            chosen[1, count + 1] = meta[q, 6, t].astype(jnp.int32)
-            count = count + (meta[q, 5, t] == mine).astype(jnp.int32)
+            chosen[1, count + 1] = code
+            count = count + (code >= 0).astype(jnp.int32)
     chosen[0, 0] = count
     last, place = chosen[0, count], chosen[1, count]
     for extra in range(group):
@@ -119,13 +134,13 @@
         for j in range(group):
             at = i * group + j + 1
             tile, local = chosen[0, at], chosen[1, at]
-            rows = gathered[tile, 0:8, :] * jnp.where(at <= count, 1.0, 0.0)
-            halves = 0.5 * gathered[tile, 8:11, :]
-            at_a = (nodes == gathered[tile, 11:12, :]).astype(F32)
-            at_b = (nodes == gathered[tile, 12:13, :]).astype(F32)
+            residual, field = tile_reader(gathered, tile, tiles, width)
+            rows = residual() * jnp.where(at <= count, 1.0, 0.0)
+            at_a = (nodes == field(3)).astype(F32)
+            at_b = (nodes == field(4)).astype(F32)
             plus = (at_a + at_b).astype(BF16)
             minus = (at_b - at_a).astype(BF16)
-            vec = jnp.concatenate([halves[c : c + 1] * rows for c in range(3)], axis=0)
+            vec = jnp.concatenate([(0.5 * field(c)) * rows for c in range(3)], axis=0)
             total_vec = dot_nt(stacked(vec), plus)
             total_grad = dot_nt(stacked(rows), minus)
             sums[local, 0:8, :] += total_grad[:8] + total_grad[8:]
@@ -135,20 +150,16 @@
     lax.fori_loop(0, (count + group - 1) // group, step, 0)
 
 
-def node_sums(where, gathered, team, places):
-    total, _, width = gathered.shape
-    return pl.pallas_call(
-        functools.partial(sums_kernel, team=team, tiles=total // team, group=GROUP),
+def node_sums(where, gathered, tiles, width, places):
+    total = gathered.shape[0] * tiles
+    return pl.pallas_call(
+        functools.partial(sums_kernel, tiles=tiles, width=width, group=GROUP),
         out_shape=(
             held((places, 32, width)),
             jax.ShapeDtypeStruct((2, total + 1 + GROUP), jnp.int32),
         ),
         in_specs=[smem_spec, vmem_spec],
         out_specs=(vmem_spec, smem_spec),
-        scratch_shapes=[
-            SMEM((team, 8, width), F32),
-            pltpu.SemaphoreType.DMA((team,)),
-        ],
         name="node_sums",
     )(where, hold(gathered))
 
@@ -175,7 +186,7 @@
 
 def back_kernel(chosen, gathered, values, out):
     out[...] = jnp.zeros_like(out)
-    width = gathered.shape[2]
+    total, _, width = out.shape
 
     def pick(rows, index):
         return jnp.take_along_axis(rows, index, axis=1)
@@ -184,25 +195,26 @@
         for j in range(GROUP):
             at = i * GROUP + j + 1
             tile, local = chosen[0, at], chosen[1, at]
-            index_a = jnp.broadcast_to(gathered[tile, 11:12, :].astype(jnp.int32), (8, width))
-            index_b = jnp.broadcast_to(gathered[tile, 12:13, :].astype(jnp.int32), (8, width))
+            _, field = tile_reader(gathered, tile, total // gathered.shape[0], width)
+            index_a = jnp.broadcast_to(field(3).astype(jnp.int32), (8, width))
+            index_b = jnp.broadcast_to(field(4).astype(jnp.int32), (8, width))
             grad = values[local, 0:8, :]
-            total = pick(grad, index_b) - pick(grad, index_a)
+            found = pick(grad, index_b) - pick(grad, index_a)
             for c in range(3):
                 rows = values[local, 8 + 8 * c : 16 + 8 * c, :]
-                half = 0.5 * gathered[tile, 8 + c : 9 + c, :]
-                total = total + half * (pick(rows, index_a) + pick(rows, index_b))
-            out[tile] = total
+                half = 0.5 * field(c)
+                found = found + half * (pick(rows, index_a) + pick(rows, index_b))
+            out[tile] = found
         return carry
 
     lax.fori_loop(0, (chosen[0, 0] + GROUP - 1) // GROUP, step, 0)
 
 
-def back(chosen, gathered, values):
-    total, _, width = gathered.shape
+def back(chosen, gathered, values, tiles):
+    width = values.shape[2]
     return pl.pallas_call(
         back_kernel,
-        out_shape=held((total, 8, width)),
+        out_shape=held((gathered.shape[0] * tiles, 8, width)),
         in_specs=[smem_spec, vmem_spec, vmem_spec],
         out_specs=vmem_spec,
         name="back",
@@ -334,14 +346,14 @@
     where = lax.axis_index(TEAM).astype(jnp.int32).reshape(1)
     doms = heights * stride * CORES
     own = pack(tile_owner[:, 0], node_slot, residual, tangents, edge_nodes, doms, stride)
-    gathered = lax.all_gather(own, TEAM, tiled=True)
+    gathered = lax.all_gather(own, TEAM)
 
     smoothed, rim = smooth(diag_kind, diag_coeff, halo_rows, residual, inverse_tiles)
     slabs = lax.axis_size("slab")
     low = lax.ppermute(rim, "slab", [(i, i + 1) for i in range(slabs - 1)])
     high = lax.ppermute(rim, "slab", [(i + 1, i) for i in range(slabs - 1)])
 
-    sums, chosen = node_sums(where, gathered, team, heights * node_tiles)
+    sums, chosen = node_sums(where, gathered, tiles, width, heights * node_tiles)
     sums = sums.reshape(heights, node_tiles * 32, width)
     arrived = lax.all_to_all(sums, "far", split_axis=0, concat_axis=0, tiled=True)
 
@@ -353,7 +365,7 @@
 
     solved = solve(arrived.reshape(heights, node_tiles, 32, width), grad_blocks, vec_blocks)
     values = lax.all_gather(solved, "far", tiled=True)
-    corrections = back(chosen, gathered, values).reshape(team, tiles, 8, width)
+    corrections = back(chosen, gathered, values, tiles).reshape(team, tiles, 8, width)
     pieces = lax.all_to_all(corrections, TEAM, split_axis=0, concat_axis=0, tiled=True)
     return finish(smoothed_twice, pieces)
 

time: 101 us -> 99.6 us (0.986)
  no operation moved by 1% of the time
where the time goes in v6:
time: 99.6 us; the launch traced here: 99 us
  blocking collectives  48.5 us (49%)
  starting transfers between devices  21.1 us (21%)
  waiting for transfers between devices  19.4 us (19%)
  Pallas kernels  9.89 us (10%)
    all_gather x1, blocking collectives, body(): values = lax.all_gather(solved, 'far', tiled=True)  33.4 us
    all_to_all x1, starting transfers between devices, body(): lax.all_to_all(sums, 'far', split_axis=0, concat_axis=0, tiled=True)  14.9 us
    all_to_all x1, waiting for transfers between devices, body(): lax.all_to_all(sums, 'far', split_axis=0, concat_axis=0, tiled=True)  12.2 us
    all_to_all x1, blocking collectives, body(): lax.all_to_all(corrections, TEAM, split_axis=0, concat_axis=0, tiled=True)  8.42 us
    ppermute x1, waiting for transfers between devices, body(): high = lax.ppermute(rim, 'slab', [(i + 1, i) for i in range(slabs - 1)])  7.22 us
    all_gather x1, blocking collectives, body(): gathered = lax.all_gather(own, TEAM)  6.73 us
    ppermute x1, starting transfers between devices, body(): low = lax.ppermute(rim, 'slab', [(i, i + 1) for i in range(slabs - 1)])  4.3 us
    pallas_call x1, Pallas kernels, node_sums(): pl.pallas_call(functools.partial(sums_kernel, tiles=tiles, width=width, g...  3.08 us
  transfers between devices with their start and end apart: 3, of which 2 were waited for; matrix products, arithmetic and copies ran while one was open for 0% of the time, Pallas kernels for 3%

profile of v6, /device:TPU:24, one launch (start us, length us, event | category | flops | bytes accessed | tf_op | source)
XLA Modules:
  0.0 99.0 jit_solution(9931076510318103918)
XLA Ops:
  0.0 0.9 pack.1
  0.9 6.7 %all-gather = f32[32,3456]{1,0:T(8,128)S(1)} all-gather(f32[8,3456]{1,0:T(8,128)S(1)} %pack.1), channel_id=2, replica_groups=mesh['section'=2,'far'=16,'near'=1,'core'=2,'slab'=8] {'section','near',..., dimensions={0}, use_global_device_ids=true | all-gather | bytes 552960 | tf_op jit(solution)/shard_map/all_gather | solution.py:349
  7.7 3.1 %node_sums.1 = (f32[32,32,128]{2,1,0:T(8,128)}, s32[2,73]{1,0:T(2,128)}) custom-call(s32[1]{0:T(128)} %bitcast.where, f32[4,8,3456]{2,1,0:T(8,128)S(1)} %bitcast.6), custom_call_target="tpu_custom_call" | custom-call | tf_op jit(solution)/shard_map/node_sums/pallas_call | solution.py:155
  10.7 0.0 copy-start
  10.8 0.0 copy-start.1
  10.8 14.9 %all-to-all-start = ((f32[16,64,128]{2,1,0:T(8,128)}), f32[16,64,128]{2,1,0:T(8,128)S(1)}, u32[]{:S(2)}, u32[]{:S(2)}) async-start(f32[16,64,128]{2,1,0:T(8,128)} %bitcast.3), calls=%async_computation | async-start | bytes 1048576 | tf_op jit(solution)/shard_map/all_to_all | solution.py:358
  25.7 0.0 copy-done
  25.7 0.0 copy-done.1
  25.7 0.0 copy-start.2
  25.7 1.3 %smooth_once.1 = (f32[16,8,128]{2,1,0:T(8,128)S(1)}, f32[2,8,128]{2,1,0:T(8,128)S(1)}) custom-call(s32[16]{0:T(128)} %kind.3, f32[16]{0:T(128)} %coeff.3, s32[2]{0:T(128)} %halo.1, f32[8,2048]{1,0:T(8,128)S(1)} %copy-done.1, f32[8,128,128]{2,1,0:T(8,128)S(1)} %copy-done), custom_call_target="tpu_custom_call" | custom-call | tf_op jit(solution)/shard_map/smooth_once/pallas_call | solution.py:242
  27.0 4.3 %collective-permute-start = (f32[2,8,128]{2,1,0:T(8,128)S(1)}, f32[2,8,128]{2,1,0:T(8,128)S(1)}, u32[]{:S(2)}, u32[]{:S(2)}) collective-permute-start(f32[2,8,128]{2,1,0:T(8,128)S(1)} %get-tuple-element.13), channel_id=1, source_target_pairs={{0,1},{1,2},{2,3},{3,4},{4,5},{5,6},{6,7},{8,9},{9,10},{10,11},{11... | collective-permute-start | bytes 24584 | tf_op jit(solution)/shard_map/ppermute | solution.py:353
  31.3 1.9 %collective-permute-start.1 = (f32[2,8,128]{2,1,0:T(8,128)S(1)}, f32[2,8,128]{2,1,0:T(8,128)S(1)}, u32[]{:S(2)}, u32[]{:S(2)}) collective-permute-start(f32[2,8,128]{2,1,0:T(8,128)S(1)} %get-tuple-element.13), channel_id=1, source_target_pairs={{1,0},{2,1},{3,2},{4,3},{5,4},{6,5},{7,6},{9,8},{10,9},{11,10},{12... | collective-permute-start | bytes 24584 | tf_op jit(solution)/shard_map/ppermute | solution.py:354
  33.2 0.0 collective-permute-done.low
  33.2 7.2 %collective-permute-done.1.high = f32[2,8,128]{2,1,0:T(8,128)S(1)} collective-permute-done((f32[2,8,128]{2,1,0:T(8,128)S(1)}, f32[2,8,128]{2,1,0:T(8,128)S(1)}, u32[]{:S(2)}, u32[]{:S(2)}) %collective-permute-start.1) | collective-permute-done | bytes 8224 | tf_op jit(solution)/shard_map/ppermute | solution.py:354
  40.4 0.0 copy-done.2
  40.5 2.2 %smooth_again.1.smoothed = f32[16,8,128]{2,1,0:T(8,128)S(1)} custom-call(s32[16]{0:T(128)} %kind.3, f32[16]{0:T(128)} %coeff.3, s32[8,16]{1,0:T(8,128)} %cols.1, s32[8,16]{1,0:T(8,128)} %kinds.1, f32[8,16]{1,0:T(8,128)} %coeffs.1, f32[16,8,128]{2,1,0:T(8,128)S(1)} %get-tuple-element.12.smoothed, f32[2,8,128]{2,1,0:T(8,128)S(1)} %collective-permute-done.low, ...), custom_call_target="tpu_custom_call" | custom-call | tf_op jit(solution)/shard_map/smooth_again/pallas_call | solution.py:286
  42.6 12.2 %all-to-all-done = f32[16,64,128]{2,1,0:T(8,128)S(1)} async-done(((f32[16,64,128]{2,1,0:T(8,128)}), f32[16,64,128]{2,1,0:T(8,128)S(1)}, u32[]{:S(2)}, u32[]{:S(2)}) %all-to-all-start) | async-done | bytes 524320 | tf_op jit(solution)/shard_map/all_to_all | solution.py:358
  54.8 0.0 copy-done.3
  54.8 0.0 copy-done.4
  54.8 0.2 solve.1
  55.0 33.4 %all_gather.11.values = f32[32,32,128]{2,1,0:T(8,128)S(1)} all-gather(f32[2,32,128]{2,1,0:T(8,128)S(1)} %solve.1), channel_id=1, replica_groups=mesh['section'=2,'far'=16,'near'=1,'core'=2,'slab'=8] {'far'}, dimensions={0}, use_global_device_ids=true | all-gather | bytes 557056 | tf_op jit(solution)/shard_map/all_gather | solution.py:367
  88.4 1.5 %back.1 = f32[64,8,128]{2,1,0:T(8,128)S(1)} custom-call(s32[2,73]{1,0:T(2,128)} %get-tuple-element.15.chosen, f32[4,8,3456]{2,1,0:T(8,128)S(1)} %bitcast.7, f32[32,32,128]{2,1,0:T(8,128)S(1)} %all_gather.11.values), custom_call_target="tpu_custom_call" | custom-call | tf_op jit(solution)/shard_map/back/pallas_call | solution.py:215
  90.0 8.4 %all_to_all.10.pieces = f32[4,16,8,128]{3,2,1,0:T(8,128)S(1)} all-to-all(f32[4,16,8,128]{3,2,1,0:T(8,128)S(1)} %bitcast.9), channel_id=1, replica_groups=mesh['section'=2,'far'=16,'near'=1,'core'=2,'slab'=8] {'section','near',..., dimensions={0} | all-to-all | bytes 524288 | tf_op jit(solution)/shard_map/all_to_all | solution.py:369
  98.4 0.6 finish.1
  (2 shorter events, 0.0 us)
Async XLA Ops:
  10.7 14.9 %copy-start = (f32[8,128,128]{2,1,0:T(8,128)S(1)}, f32[8,128,128]{2,1,0:T(8,128)}, u32[]{:S(2)}) copy-start(f32[8,128,128]{2,1,0:T(8,128)} %inverse.3) | copy-start | bytes 1572868
  10.8 14.9 %copy-start.1 = (f32[8,2048]{1,0:T(8,128)S(1)}, f32[8,2048]{1,0:T(8,128)}, u32[]{:S(2)}) copy-start(f32[8,2048]{1,0:T(8,128)} %residual.5) | copy-start | bytes 196612
  10.8 44.0 %all-to-all-start = ((f32[16,64,128]{2,1,0:T(8,128)}), f32[16,64,128]{2,1,0:T(8,128)S(1)}, u32[]{:S(2)}, u32[]{:S(2)}) async-start(f32[16,64,128]{2,1,0:T(8,128)} %bitcast.3), calls=%async_computation | async-start | bytes 1048576 | tf_op jit(solution)/shard_map/all_to_all | solution.py:358
  25.7 14.8 %copy-start.2 = (f32[8,128,128]{2,1,0:T(8,128)S(1)}, f32[8,128,128]{2,1,0:T(8,128)}, u32[]{:S(2)}) copy-start(f32[8,128,128]{2,1,0:T(8,128)} %coupling.1) | copy-start | bytes 1572868
  27.0 6.2 %collective-permute-start = (f32[2,8,128]{2,1,0:T(8,128)S(1)}, f32[2,8,128]{2,1,0:T(8,128)S(1)}, u32[]{:S(2)}, u32[]{:S(2)}) collective-permute-start(f32[2,8,128]{2,1,0:T(8,128)S(1)} %get-tuple-element.13), channel_id=1, source_target_pairs={{0,1},{1,2},{2,3},{3,4},{4,5},{5,6},{6,7},{8,9},{9,10},{10,11},{11... | collective-permute-start | bytes 24584 | tf_op jit(solution)/shard_map/ppermute | solution.py:353
  31.3 9.2 %collective-permute-start.1 = (f32[2,8,128]{2,1,0:T(8,128)S(1)}, f32[2,8,128]{2,1,0:T(8,128)S(1)}, u32[]{:S(2)}, u32[]{:S(2)}) collective-permute-start(f32[2,8,128]{2,1,0:T(8,128)S(1)} %get-tuple-element.13), channel_id=1, source_target_pairs={{1,0},{2,1},{3,2},{4,3},{5,4},{6,5},{7,6},{9,8},{10,9},{11,10},{12... | collective-permute-start | bytes 24584 | tf_op jit(solution)/shard_map/ppermute | solution.py:354
  40.4 14.3 %copy-start.3 = (f32[2,128,128]{2,1,0:T(8,128)S(1)}, f32[2,128,128]{2,1,0:T(8,128)}, u32[]{:S(2)}) copy-start(f32[2,128,128]{2,1,0:T(8,128)} %grad.1) | copy-start | bytes 393220
  40.5 14.3 %copy-start.4 = (f32[2,128,128]{2,1,0:T(8,128)S(1)}, f32[2,128,128]{2,1,0:T(8,128)}, u32[]{:S(2)}) copy-start(f32[2,128,128]{2,1,0:T(8,128)} %vec.1) | copy-start | bytes 393220

commit v7 on v6

--- a/solution.py
+++ b/solution.py
@@ -9,7 +9,7 @@
 
 DAMPING = 0.7
 CORES = 2
-NEAR = 1
+NEAR = 2
 GROUP = 8
 F32 = jnp.float32
 BF16 = jnp.bfloat16
@@ -60,7 +60,7 @@
 FIELDS = 5
 
 
-def pack_kernel(owner, slot, residual, tangents, ends, out, *, doms, stride):
+def pack_kernel(owner, slot, residual, tangents, ends, out, *, doms):
     tiles = owner.shape[0]
     width = residual.shape[1] // tiles
     lanes = lax.broadcasted_iota(jnp.int32, (1, width), 1)
@@ -71,7 +71,6 @@
         slots = jnp.where(lanes == t, slot[t], slots)
     section, dom = parts_of(owners, doms)
     z, core = parts_of(dom, CORES)
-    far, near = parts_of(z, stride)
     out[:, 0 : tiles * width] = residual[...]
     for t in range(tiles):
         part = slice(t * width, (t + 1) * width)
@@ -81,15 +80,15 @@
             out[t % 8 : t % 8 + 1, at : at + width] = row
     at = (tiles + tiles // 8 * FIELDS) * width
     out[:, at : at + width] = jnp.zeros((8, width), F32)
-    out[0:1, at : at + width] = ((section * stride + near) * CORES + core).astype(F32)
-    out[1:2, at : at + width] = (far * 2 + slots).astype(F32)
-
-
-def pack(owner, slot, residual, tangents, ends, doms, stride):
+    out[0:1, at : at + width] = (section * CORES + core).astype(F32)
+    out[1:2, at : at + width] = (z * 2 + slots).astype(F32)
+
+
+def pack(owner, slot, residual, tangents, ends, doms):
     tiles = owner.shape[0]
     width = residual.shape[1] // tiles
     return pl.pallas_call(
-        functools.partial(pack_kernel, doms=doms, stride=stride),
+        functools.partial(pack_kernel, doms=doms),
         out_shape=held((8, (tiles + tiles // 8 * FIELDS + 1) * width)),
         in_specs=[smem_spec, smem_spec, vmem_spec, vmem_spec, vmem_spec],
         out_specs=vmem_spec,
@@ -111,13 +110,11 @@
     )
 
 
-def sums_kernel(where, gathered, sums, chosen, *, tiles, width, group):
-    sums[...] = jnp.zeros_like(sums)
-    mine = where[0].astype(F32)
+def choose(chosen, gathered, tiles, width, rule):
     count = jnp.int32(0)
     for q in range(gathered.shape[0]):
-        last_block = gathered[q, :, gathered.shape[2] - width :]
-        codes = jnp.where(last_block[0:1] == mine, last_block[1:2], -1.0).astype(jnp.int32)
+        block = gathered[q, :, gathered.shape[2] - width :]
+        codes = rule(block[0:1], block[1:2].astype(jnp.int32))
         for t in range(tiles):
             code = codes[0, t]
             chosen[0, count + 1] = q * tiles + t
@@ -125,42 +122,76 @@
             count = count + (code >= 0).astype(jnp.int32)
     chosen[0, 0] = count
     last, place = chosen[0, count], chosen[1, count]
-    for extra in range(group):
+    for extra in range(GROUP):
         chosen[0, count + 1 + extra] = last
         chosen[1, count + 1 + extra] = place
+    return count
+
+
+def sums_kernel(where, own, other, sums, chosen_own, chosen_other, *, tiles, width):
+    sums[...] = jnp.zeros_like(sums)
+    mine, near = where[0].astype(F32), where[1]
+
+    def rule(classes, places):
+        fits = (classes == mine) & (((places >> 1) & (NEAR - 1)) == near)
+        return jnp.where(fits, (places >> NEAR) * 2 + (places & 1), -1)
+
     nodes = lax.broadcasted_iota(jnp.int32, (width, width), 0).astype(F32)
-
-    def step(i, carry):
-        for j in range(group):
-            at = i * group + j + 1
-            tile, local = chosen[0, at], chosen[1, at]
-            residual, field = tile_reader(gathered, tile, tiles, width)
-            rows = residual() * jnp.where(at <= count, 1.0, 0.0)
-            at_a = (nodes == field(3)).astype(F32)
-            at_b = (nodes == field(4)).astype(F32)
-            plus = (at_a + at_b).astype(BF16)
-            minus = (at_b - at_a).astype(BF16)
-            vec = jnp.concatenate([(0.5 * field(c)) * rows for c in range(3)], axis=0)
-            total_vec = dot_nt(stacked(vec), plus)
-            total_grad = dot_nt(stacked(rows), minus)
-            sums[local, 0:8, :] += total_grad[:8] + total_grad[8:]
-            sums[local, 8:32, :] += total_vec[:24] + total_vec[24:]
-        return carry
-
-    lax.fori_loop(0, (count + group - 1) // group, step, 0)
-
-
-def node_sums(where, gathered, tiles, width, places):
-    total = gathered.shape[0] * tiles
-    return pl.pallas_call(
-        functools.partial(sums_kernel, tiles=tiles, width=width, group=GROUP),
-        out_shape=(
-            held((places, 32, width)),
-            jax.ShapeDtypeStruct((2, total + 1 + GROUP), jnp.int32),
-        ),
+    counts = [
+        choose(chosen, gathered, tiles, width, rule)
+        for chosen, gathered in ((chosen_own, own), (chosen_other, other))
+    ]
+    for count, chosen, gathered in zip(counts, (chosen_own, chosen_other), (own, other)):
+
+        def step(i, carry, count=count, chosen=chosen, gathered=gathered):
+            for j in range(GROUP):
+                at = i * GROUP + j + 1
+                tile, local = chosen[0, at], chosen[1, at]
+                residual, field = tile_reader(gathered, tile, tiles, width)
+                rows = residual() * jnp.where(at <= count, 1.0, 0.0)
+                at_a = (nodes == field(3)).astype(F32)
+                at_b = (nodes == field(4)).astype(F32)
+                plus = (at_a + at_b).astype(BF16)
+                minus = (at_b - at_a).astype(BF16)
+                vec = jnp.concatenate([(0.5 * field(c)) * rows for c in range(3)], axis=0)
+                total_vec = dot_nt(stacked(vec), plus)
+                total_grad = dot_nt(stacked(rows), minus)
+                sums[local, 0:8, :] += total_grad[:8] + total_grad[8:]
+                sums[local, 8:32, :] += total_vec[:24] + total_vec[24:]
+            return carry
+
+        lax.fori_loop(0, (count + GROUP - 1) // GROUP, step, 0)
+
+
+def list_shape(gathered, tiles):
+    return (2, gathered.shape[0] * tiles + 1 + GROUP)
+
+
+def node_sums(where, own, other, tiles, width, places):
+    return pl.pallas_call(
+        functools.partial(sums_kernel, tiles=tiles, width=width),
+        out_shape=held((places, 32, width)),
+        in_specs=[smem_spec, vmem_spec, vmem_spec],
+        out_specs=vmem_spec,
+        scratch_shapes=[SMEM(list_shape(own, tiles), jnp.int32) for _ in range(2)],
+        name="node_sums",
+    )(where, hold(own), hold(other))
+
+
+def list_kernel(where, gathered, chosen, *, tiles, width):
+    mine = where[0].astype(F32)
+    choose(
+        chosen, gathered, tiles, width, lambda classes, places: jnp.where(classes == mine, places, -1)
+    )
+
+
+def class_list(where, gathered, tiles, width):
+    return pl.pallas_call(
+        functools.partial(list_kernel, tiles=tiles, width=width),
+        out_shape=jax.ShapeDtypeStruct(list_shape(gathered, tiles), jnp.int32),
         in_specs=[smem_spec, vmem_spec],
-        out_specs=(vmem_spec, smem_spec),
-        name="node_sums",
+        out_specs=smem_spec,
+        name="class_list",
     )(where, hold(gathered))
 
 
@@ -319,7 +350,8 @@
     )(hold(smoothed), hold(pieces))
 
 
-TEAM = ("section", "near", "core")
+TEAM = ("section", "core")
+HEIGHT = ("far", "near")
 
 
 def body(
@@ -339,32 +371,34 @@
     grad_blocks,
     vec_blocks,
 ):
-    heights, stride, team = lax.axis_size("far"), lax.axis_size("near"), lax.axis_size(TEAM)
+    far, team = lax.axis_size("far"), lax.axis_size(TEAM)
     node_tiles = grad_blocks.shape[0]
     tiles = diag_kind.shape[0]
     width = coupling_tiles.shape[1]
-    where = lax.axis_index(TEAM).astype(jnp.int32).reshape(1)
-    doms = heights * stride * CORES
-    own = pack(tile_owner[:, 0], node_slot, residual, tangents, edge_nodes, doms, stride)
+    where = jnp.stack([lax.axis_index(TEAM), lax.axis_index("near")]).astype(jnp.int32)
+    own = pack(tile_owner[:, 0], node_slot, residual, tangents, edge_nodes, far * NEAR * CORES)
+    other = lax.ppermute(own, "near", [(0, 1), (1, 0)])
     gathered = lax.all_gather(own, TEAM)
+    gathered_other = lax.all_gather(other, TEAM)
 
     smoothed, rim = smooth(diag_kind, diag_coeff, halo_rows, residual, inverse_tiles)
     slabs = lax.axis_size("slab")
     low = lax.ppermute(rim, "slab", [(i, i + 1) for i in range(slabs - 1)])
     high = lax.ppermute(rim, "slab", [(i + 1, i) for i in range(slabs - 1)])
 
-    sums, chosen = node_sums(where, gathered, tiles, width, heights * node_tiles)
-    sums = sums.reshape(heights, node_tiles * 32, width)
+    sums = node_sums(where, gathered, gathered_other, tiles, width, far * node_tiles)
+    sums = sums.reshape(far, node_tiles * 32, width)
     arrived = lax.all_to_all(sums, "far", split_axis=0, concat_axis=0, tiled=True)
 
+    chosen = class_list(where, gathered, tiles, width)
     smoothed_twice = smooth_again(
         diag_kind, diag_coeff, tile_cols, tile_kinds, tile_coeff,
         smoothed, low, high, residual, coupling_tiles, inverse_tiles,
     )
-    arrived, smoothed_twice = lax.optimization_barrier((arrived, smoothed_twice))
-
-    solved = solve(arrived.reshape(heights, node_tiles, 32, width), grad_blocks, vec_blocks)
-    values = lax.all_gather(solved, "far", tiled=True)
+    arrived, smoothed_twice, chosen = lax.optimization_barrier((arrived, smoothed_twice, chosen))
+
+    solved = solve(arrived.reshape(far, node_tiles, 32, width), grad_blocks, vec_blocks)
+    values = lax.all_gather(solved, HEIGHT, tiled=True)
     corrections = back(chosen, gathered, values, tiles).reshape(team, tiles, 8, width)
     pieces = lax.all_to_all(corrections, TEAM, split_axis=0, concat_axis=0, tiled=True)
     return finish(smoothed_twice, pieces)

time: 99.6 us -> 99.3 us (level)
  waiting for transfers between devices: 19.4 us -> 4.78 us
  starting transfers between devices: 21.1 us -> 27.1 us
  blocking collectives: 48.5 us -> 53.1 us
  Pallas kernels: 9.89 us -> 12.3 us
    all_to_all x1, waiting for transfers between devices: 12.2 us -> 4.77 us  [body(): lax.all_to_all(sums, 'far', split_axis=0, concat_axis=0, tiled=True)]
    ppermute x1, waiting for transfers between devices: 7.22 us -> 0.01 us  [body(): high = lax.ppermute(rim, 'slab', [(i + 1, i) for i in range(slabs - 1)])]
    all_gather x1 -> x2, blocking collectives: 33.4 us -> 37.9 us  [the longest x1 31.1 us: body(): values = lax.all_gather(solved, HEIGHT, tiled=True)]
    ppermute x0 -> x1, starting transfers between devices: none -> 3.83 us  [body(): other = lax.ppermute(own, 'near', [(0, 1), (1, 0)])]
    pallas_call x2 -> x3, Pallas kernels: 4 us -> 6.63 us  [the longest x1 4.07 us: node_sums(): pl.pallas_call(functools.partial(sums_kernel, tiles=tiles, width=width),...]
    ppermute x1, starting transfers between devices: 4.3 us -> 6.35 us  [body(): low = lax.ppermute(rim, 'slab', [(i, i + 1) for i in range(slabs - 1)])]
    ppermute x1, starting transfers between devices: 1.92 us -> 3.11 us  [body(): high = lax.ppermute(rim, 'slab', [(i + 1, i) for i in range(slabs - 1)])]
    all_to_all x1, starting transfers between devices: 14.9 us -> 13.9 us  [body(): lax.all_to_all(sums, 'far', split_axis=0, concat_axis=0, tiled=True)]
  transfers between devices with their start and end apart: 3 -> 4, of which waited for: 2 -> 1; matrix products, arithmetic and copies ran while one was open for 0% -> 1% of each run, Pallas kernels for 3% -> 5%
where the time goes in v7:
time: 99.3 us; the launch traced here: 98.1 us
  blocking collectives  53.1 us (53%)
  starting transfers between devices  27.1 us (27%)
  Pallas kernels  12.3 us (12%)
  waiting for transfers between devices  4.78 us (5%)
    all_gather x1, blocking collectives, body(): values = lax.all_gather(solved, HEIGHT, tiled=True)  31.1 us
    all_to_all x1, starting transfers between devices, body(): lax.all_to_all(sums, 'far', split_axis=0, concat_axis=0, tiled=True)  13.9 us
    all_to_all x1, blocking collectives, body(): lax.all_to_all(corrections, TEAM, split_axis=0, concat_axis=0, tiled=True)  8.42 us
    all_gather x1, blocking collectives, body(): gathered_other = lax.all_gather(other, TEAM)  6.83 us
    all_gather x1, blocking collectives, body(): gathered = lax.all_gather(own, TEAM)  6.73 us
    ppermute x1, starting transfers between devices, body(): low = lax.ppermute(rim, 'slab', [(i, i + 1) for i in range(slabs - 1)])  6.35 us
    all_to_all x1, waiting for transfers between devices, body(): lax.all_to_all(sums, 'far', split_axis=0, concat_axis=0, tiled=True)  4.77 us
    pallas_call x1, Pallas kernels, node_sums(): pl.pallas_call(functools.partial(sums_kernel, tiles=tiles, width=width),...  4.07 us
  transfers between devices with their start and end apart: 4, of which 1 were waited for; matrix products, arithmetic and copies ran while one was open for 1% of the time, Pallas kernels for 5%

profile of v7, /device:TPU:24, one launch (start us, length us, event | category | flops | bytes accessed | tf_op | source)
XLA Modules:
  0.0 98.1 jit_solution(15663762554325336788)
XLA Ops:
  0.0 0.9 pack.1
  0.9 3.8 %collective-permute-start = (f32[8,3456]{1,0:T(8,128)S(1)}, f32[8,3456]{1,0:T(8,128)S(1)}, u32[]{:S(2)}, u32[]{:S(2)}) collective-permute-start(f32[8,3456]{1,0:T(8,128)S(1)} %pack.1), channel_id=1, source_target_pairs={{0,16},{16,0},{1,17},{17,1},{2,18},{18,2},{3,19},{19,3},{4,20},{20... | collective-permute-start | bytes 331784 | tf_op jit(solution)/shard_map/ppermute | solution.py:380
  4.8 6.7 %all-gather = f32[32,3456]{1,0:T(8,128)S(1)} all-gather(f32[8,3456]{1,0:T(8,128)S(1)} %pack.1), channel_id=2, replica_groups=mesh['section'=2,'far'=8,'near'=2,'core'=2,'slab'=8] {'section','core'}, dimensions={0}, use_global_device_ids=true | all-gather | bytes 552960 | tf_op jit(solution)/shard_map/all_gather | solution.py:381
  11.5 0.6 pad_add_fusion.where
  12.1 0.0 collective-permute-done
  12.1 6.8 %all-gather.1 = f32[32,3456]{1,0:T(8,128)S(1)} all-gather(f32[8,3456]{1,0:T(8,128)S(1)} %collective-permute-done), channel_id=3, replica_groups=mesh['section'=2,'far'=8,'near'=2,'core'=2,'slab'=8] {'section','core'}, dimensions={0}, use_global_device_ids=true | all-gather | bytes 552960 | tf_op jit(solution)/shard_map/all_gather | solution.py:382
  18.9 4.1 %node_sums.1 = f32[16,32,128]{2,1,0:T(8,128)} custom-call(s32[2]{0:T(128)} %pad_add_fusion.where, f32[4,8,3456]{2,1,0:T(8,128)S(1)} %bitcast.8, f32[4,8,3456]{2,1,0:T(8,128)S(1)} %bitcast.11), custom_call_target="tpu_custom_call" | custom-call | tf_op jit(solution)/shard_map/node_sums/pallas_call | solution.py:171
  23.0 13.9 %all-to-all-start = ((f32[8,64,128]{2,1,0:T(8,128)}), f32[8,64,128]{2,1,0:T(8,128)S(1)}, u32[]{:S(2)}, u32[]{:S(2)}) async-start(f32[8,64,128]{2,1,0:T(8,128)} %bitcast.5), calls=%async_computation | async-start | bytes 524288 | tf_op jit(solution)/shard_map/all_to_all | solution.py:391
  36.9 0.0 copy-start.2
  36.9 1.3 %smooth_once.1 = (f32[16,8,128]{2,1,0:T(8,128)S(1)}, f32[2,8,128]{2,1,0:T(8,128)S(1)}) custom-call(s32[16]{0:T(128)} %kind.3, f32[16]{0:T(128)} %coeff.3, s32[2]{0:T(128)} %halo.1, f32[8,2048]{1,0:T(8,128)S(1)} %copy-done.1, f32[8,128,128]{2,1,0:T(8,128)S(1)} %copy-done), custom_call_target="tpu_custom_call" | custom-call | tf_op jit(solution)/shard_map/smooth_once/pallas_call | solution.py:273
  38.2 3.1 %collective-permute-start.2 = (f32[2,8,128]{2,1,0:T(8,128)S(1)}, f32[2,8,128]{2,1,0:T(8,128)S(1)}, u32[]{:S(2)}, u32[]{:S(2)}) collective-permute-start(f32[2,8,128]{2,1,0:T(8,128)S(1)} %get-tuple-element.11), channel_id=1, source_target_pairs={{1,0},{2,1},{3,2},{4,3},{5,4},{6,5},{7,6},{9,8},{10,9},{11,10},{12... | collective-permute-start | bytes 24584 | tf_op jit(solution)/shard_map/ppermute | solution.py:387
  41.3 6.3 %collective-permute-start.1 = (f32[2,8,128]{2,1,0:T(8,128)S(1)}, f32[2,8,128]{2,1,0:T(8,128)S(1)}, u32[]{:S(2)}, u32[]{:S(2)}) collective-permute-start(f32[2,8,128]{2,1,0:T(8,128)S(1)} %get-tuple-element.11), channel_id=1, source_target_pairs={{0,1},{1,2},{2,3},{3,4},{4,5},{5,6},{6,7},{8,9},{9,10},{10,11},{11... | collective-permute-start | bytes 24584 | tf_op jit(solution)/shard_map/ppermute | solution.py:386
  47.7 1.6 %class_list.1.chosen = s32[2,73]{1,0:T(2,128)} custom-call(s32[2]{0:T(128)} %pad_add_fusion.where, f32[4,8,3456]{2,1,0:T(8,128)S(1)} %bitcast.9), custom_call_target="tpu_custom_call" | custom-call | tf_op jit(solution)/shard_map/class_list/pallas_call | solution.py:189
  49.3 0.0 collective-permute-done.2.high
  49.3 0.0 collective-permute-done.1.low
  49.3 0.0 copy-start.3
  49.3 0.0 copy-start.4
  49.4 2.2 %smooth_again.1.smoothed = f32[16,8,128]{2,1,0:T(8,128)S(1)} custom-call(s32[16]{0:T(128)} %kind.3, f32[16]{0:T(128)} %coeff.3, s32[8,16]{1,0:T(8,128)} %cols.1, s32[8,16]{1,0:T(8,128)} %kinds.1, f32[8,16]{1,0:T(8,128)} %coeffs.1, f32[16,8,128]{2,1,0:T(8,128)S(1)} %get-tuple-element.10.smoothed, f32[2,8,128]{2,1,0:T(8,128)S(1)} %collective-permute-done.1.low, ...), custom_call_target="tpu_custom_call" | custom-call | tf_op jit(solution)/shard_map/smooth_again/pallas_call | solution.py:317
  51.5 4.8 %all-to-all-done = f32[8,64,128]{2,1,0:T(8,128)S(1)} async-done(((f32[8,64,128]{2,1,0:T(8,128)}), f32[8,64,128]{2,1,0:T(8,128)S(1)}, u32[]{:S(2)}, u32[]{:S(2)}) %all-to-all-start) | async-done | bytes 262176 | tf_op jit(solution)/shard_map/all_to_all | solution.py:391
  56.3 0.2 solve.1
  56.6 31.1 %all_gather.19.values = f32[32,32,128]{2,1,0:T(8,128)S(1)} all-gather(f32[2,32,128]{2,1,0:T(8,128)S(1)} %solve.1), channel_id=1, replica_groups=mesh['section'=2,'far'=8,'near'=2,'core'=2,'slab'=8] {'far','near'}, dimensions={0}, use_global_device_ids=true | all-gather | bytes 557056 | tf_op jit(solution)/shard_map/all_gather | solution.py:401
  87.6 1.3 %back.1 = f32[64,8,128]{2,1,0:T(8,128)S(1)} custom-call(s32[2,73]{1,0:T(2,128)} %class_list.1.chosen, f32[4,8,3456]{2,1,0:T(8,128)S(1)} %bitcast.10, f32[32,32,128]{2,1,0:T(8,128)S(1)} %all_gather.19.values), custom_call_target="tpu_custom_call" | custom-call | tf_op jit(solution)/shard_map/back/pallas_call | solution.py:246
  89.0 8.4 %all_to_all.10.pieces = f32[4,16,8,128]{3,2,1,0:T(8,128)S(1)} all-to-all(f32[4,16,8,128]{3,2,1,0:T(8,128)S(1)} %bitcast.13), channel_id=1, replica_groups=mesh['section'=2,'far'=8,'near'=2,'core'=2,'slab'=8] {'section','core'}, dimensions={0} | all-to-all | bytes 524288 | tf_op jit(solution)/shard_map/all_to_all | solution.py:403
  97.4 0.6 finish.1
  (7 shorter events, 0.0 us)
Async XLA Ops:
  0.9 11.2 %collective-permute-start = (f32[8,3456]{1,0:T(8,128)S(1)}, f32[8,3456]{1,0:T(8,128)S(1)}, u32[]{:S(2)}, u32[]{:S(2)}) collective-permute-start(f32[8,3456]{1,0:T(8,128)S(1)} %pack.1), channel_id=1, source_target_pairs={{0,16},{16,0},{1,17},{17,1},{2,18},{18,2},{3,19},{19,3},{4,20},{20... | collective-permute-start | bytes 331784 | tf_op jit(solution)/shard_map/ppermute | solution.py:380
  18.9 17.9 %copy-start.1 = (f32[8,2048]{1,0:T(8,128)S(1)}, f32[8,2048]{1,0:T(8,128)}, u32[]{:S(2)}) copy-start(f32[8,2048]{1,0:T(8,128)} %residual.5) | copy-start | bytes 196612
  23.0 13.9 %copy-start = (f32[8,128,128]{2,1,0:T(8,128)S(1)}, f32[8,128,128]{2,1,0:T(8,128)}, u32[]{:S(2)}) copy-start(f32[8,128,128]{2,1,0:T(8,128)} %inverse.3) | copy-start | bytes 1572868
  23.0 33.3 %all-to-all-start = ((f32[8,64,128]{2,1,0:T(8,128)}), f32[8,64,128]{2,1,0:T(8,128)S(1)}, u32[]{:S(2)}, u32[]{:S(2)}) async-start(f32[8,64,128]{2,1,0:T(8,128)} %bitcast.5), calls=%async_computation | async-start | bytes 524288 | tf_op jit(solution)/shard_map/all_to_all | solution.py:391
  36.9 12.5 %copy-start.2 = (f32[8,128,128]{2,1,0:T(8,128)S(1)}, f32[8,128,128]{2,1,0:T(8,128)}, u32[]{:S(2)}) copy-start(f32[8,128,128]{2,1,0:T(8,128)} %coupling.1) | copy-start | bytes 1572868
  38.2 11.1 %collective-permute-start.2 = (f32[2,8,128]{2,1,0:T(8,128)S(1)}, f32[2,8,128]{2,1,0:T(8,128)S(1)}, u32[]{:S(2)}, u32[]{:S(2)}) collective-permute-start(f32[2,8,128]{2,1,0:T(8,128)S(1)} %get-tuple-element.11), channel_id=1, source_target_pairs={{1,0},{2,1},{3,2},{4,3},{5,4},{6,5},{7,6},{9,8},{10,9},{11,10},{12... | collective-permute-start | bytes 24584 | tf_op jit(solution)/shard_map/ppermute | solution.py:387
  41.3 8.0 %collective-permute-start.1 = (f32[2,8,128]{2,1,0:T(8,128)S(1)}, f32[2,8,128]{2,1,0:T(8,128)S(1)}, u32[]{:S(2)}, u32[]{:S(2)}) collective-permute-start(f32[2,8,128]{2,1,0:T(8,128)S(1)} %get-tuple-element.11), channel_id=1, source_target_pairs={{0,1},{1,2},{2,3},{3,4},{4,5},{5,6},{6,7},{8,9},{9,10},{10,11},{11... | collective-permute-start | bytes 24584 | tf_op jit(solution)/shard_map/ppermute | solution.py:386
  49.3 7.0 %copy-start.3 = (f32[2,128,128]{2,1,0:T(8,128)S(1)}, f32[2,128,128]{2,1,0:T(8,128)}, u32[]{:S(2)}) copy-start(f32[2,128,128]{2,1,0:T(8,128)} %grad.1) | copy-start | bytes 393220
  49.3 7.0 %copy-start.4 = (f32[2,128,128]{2,1,0:T(8,128)S(1)}, f32[2,128,128]{2,1,0:T(8,128)}, u32[]{:S(2)}) copy-start(f32[2,128,128]{2,1,0:T(8,128)} %vec.1) | copy-start | bytes 393220

commit v8 on v7

--- a/solution.py
+++ b/solution.py
@@ -128,9 +128,9 @@
     return count
 
 
-def sums_kernel(where, own, other, sums, chosen_own, chosen_other, *, tiles, width):
+def sums_kernel(cls, parity, own, other, sums, chosen_own, chosen_other, *, tiles, width):
     sums[...] = jnp.zeros_like(sums)
-    mine, near = where[0].astype(F32), where[1]
+    mine, near = cls[0].astype(F32), parity[0]
 
     def rule(classes, places):
         fits = (classes == mine) & (((places >> 1) & (NEAR - 1)) == near)
@@ -167,32 +167,15 @@
     return (2, gathered.shape[0] * tiles + 1 + GROUP)
 
 
-def node_sums(where, own, other, tiles, width, places):
+def node_sums(cls, parity, own, other, tiles, width, places):
     return pl.pallas_call(
         functools.partial(sums_kernel, tiles=tiles, width=width),
         out_shape=held((places, 32, width)),
-        in_specs=[smem_spec, vmem_spec, vmem_spec],
+        in_specs=[smem_spec, smem_spec, vmem_spec, vmem_spec],
         out_specs=vmem_spec,
         scratch_shapes=[SMEM(list_shape(own, tiles), jnp.int32) for _ in range(2)],
         name="node_sums",
-    )(where, hold(own), hold(other))
-
-
-def list_kernel(where, gathered, chosen, *, tiles, width):
-    mine = where[0].astype(F32)
-    choose(
-        chosen, gathered, tiles, width, lambda classes, places: jnp.where(classes == mine, places, -1)
-    )
-
-
-def class_list(where, gathered, tiles, width):
-    return pl.pallas_call(
-        functools.partial(list_kernel, tiles=tiles, width=width),
-        out_shape=jax.ShapeDtypeStruct(list_shape(gathered, tiles), jnp.int32),
-        in_specs=[smem_spec, vmem_spec],
-        out_specs=smem_spec,
-        name="class_list",
-    )(where, hold(gathered))
+    )(cls, parity, hold(own), hold(other))
 
 
 def solve_kernel(arrived, grad, vec, out):
@@ -284,9 +267,14 @@
 
 
 def again_kernel(
-    kind, coeff, cols, kinds, coeffs, smoothed, low, high, residual, coupling, inverse, out, work, rest
+    kind, coeff, cols, kinds, coeffs, cls, smoothed, low, high, residual, coupling, inverse, gathered,
+    out, chosen, work, rest,
 ):
     tiles, _, width = smoothed.shape
+    mine = cls[0].astype(F32)
+    choose(
+        chosen, gathered, tiles, width, lambda classes, places: jnp.where(classes == mine, places, -1)
+    )
     sources = jnp.concatenate(
         [
             smoothed[...].reshape(tiles * 8, width),
@@ -311,22 +299,28 @@
         out[t] = smoothed[t] + DAMPING * (work[kind[t], t] / coeff[t])
 
 
-def smooth_again(kind, coeff, cols, kinds, coeffs, smoothed, low, high, residual, coupling, inverse):
+def smooth_again(
+    kind, coeff, cols, kinds, coeffs, smoothed, low, high, residual, coupling, inverse, cls, gathered
+):
     tiles, _, width = smoothed.shape
     count = tiles + low.shape[0] + high.shape[0]
     return pl.pallas_call(
         again_kernel,
-        out_shape=held((tiles, 8, width)),
-        in_specs=[smem_spec] * 5 + [vmem_spec] * 6,
-        out_specs=vmem_spec,
+        out_shape=(
+            held((tiles, 8, width)),
+            jax.ShapeDtypeStruct(list_shape(gathered, tiles), jnp.int32),
+        ),
+        in_specs=[smem_spec] * 6 + [vmem_spec] * 7,
+        out_specs=(vmem_spec, smem_spec),
         scratch_shapes=[
             VMEM((coupling.shape[0], count, 8, width), F32),
             VMEM((tiles, 8, width), F32),
         ],
         name="smooth_again",
     )(
-        kind, coeff, cols, kinds, coeffs,
+        kind, coeff, cols, kinds, coeffs, cls,
         hold(smoothed), hold(low), hold(high), hold(residual), hold(coupling), hold(inverse),
+        hold(gathered),
     )
 
 
@@ -375,7 +369,8 @@
     node_tiles = grad_blocks.shape[0]
     tiles = diag_kind.shape[0]
     width = coupling_tiles.shape[1]
-    where = jnp.stack([lax.axis_index(TEAM), lax.axis_index("near")]).astype(jnp.int32)
+    cls = lax.axis_index(TEAM).astype(jnp.int32).reshape(1)
+    parity = lax.axis_index("near").astype(jnp.int32).reshape(1)
     own = pack(tile_owner[:, 0], node_slot, residual, tangents, edge_nodes, far * NEAR * CORES)
     other = lax.ppermute(own, "near", [(0, 1), (1, 0)])
     gathered = lax.all_gather(own, TEAM)
@@ -386,14 +381,13 @@
     low = lax.ppermute(rim, "slab", [(i, i + 1) for i in range(slabs - 1)])
     high = lax.ppermute(rim, "slab", [(i + 1, i) for i in range(slabs - 1)])
 
-    sums = node_sums(where, gathered, gathered_other, tiles, width, far * node_tiles)
+    sums = node_sums(cls, parity, gathered, gathered_other, tiles, width, far * node_tiles)
     sums = sums.reshape(far, node_tiles * 32, width)
     arrived = lax.all_to_all(sums, "far", split_axis=0, concat_axis=0, tiled=True)
 
-    chosen = class_list(where, gathered, tiles, width)
-    smoothed_twice = smooth_again(
+    smoothed_twice, chosen = smooth_again(
         diag_kind, diag_coeff, tile_cols, tile_kinds, tile_coeff,
-        smoothed, low, high, residual, coupling_tiles, inverse_tiles,
+        smoothed, low, high, residual, coupling_tiles, inverse_tiles, cls, gathered,
     )
     arrived, smoothed_twice, chosen = lax.optimization_barrier((arrived, smoothed_twice, chosen))
 

time: 99.3 us -> 97.7 us (0.984)
  waiting for transfers between devices: 4.78 us -> 7.87 us
  Pallas kernels: 12.3 us -> 10.2 us
  blocking collectives: 53.1 us -> 51.1 us
    all_gather x1, blocking collectives: 31.1 us -> 29.1 us  [body(): values = lax.all_gather(solved, HEIGHT, tiled=True)]
    all_to_all x1, waiting for transfers between devices: 4.77 us -> 6.53 us  [body(): lax.all_to_all(sums, 'far', split_axis=0, concat_axis=0, tiled=True)]
    ppermute x1, waiting for transfers between devices: 0.01 us -> 1.33 us  [body(): low = lax.ppermute(rim, 'slab', [(i, i + 1) for i in range(slabs - 1)])]
    pallas_call x2 -> x1, Pallas kernels: 3.8 us -> 2.84 us  [smooth_again(): pl.pallas_call(again_kernel, out_shape=(held((tiles, 8, width)), jax.Shap...]
  transfers between devices with their start and end apart: 4 -> 4, of which waited for: 1 -> 2; matrix products, arithmetic and copies ran while one was open for 1% -> 0% of each run, Pallas kernels for 5% -> 4%
where the time goes in v8:
time: 97.7 us; the launch traced here: 96.5 us
  blocking collectives  51.1 us (52%)
  starting transfers between devices  27.1 us (28%)
  Pallas kernels  10.2 us (10%)
  waiting for transfers between devices  7.87 us (8%)
    all_gather x1, blocking collectives, body(): values = lax.all_gather(solved, HEIGHT, tiled=True)  29.1 us
    all_to_all x1, starting transfers between devices, body(): lax.all_to_all(sums, 'far', split_axis=0, concat_axis=0, tiled=True)  13.9 us
    all_to_all x1, blocking collectives, body(): lax.all_to_all(corrections, TEAM, split_axis=0, concat_axis=0, tiled=True)  8.42 us
    all_gather x1, blocking collectives, body(): gathered_other = lax.all_gather(other, TEAM)  6.83 us
    all_gather x1, blocking collectives, body(): gathered = lax.all_gather(own, TEAM)  6.73 us
    all_to_all x1, waiting for transfers between devices, body(): lax.all_to_all(sums, 'far', split_axis=0, concat_axis=0, tiled=True)  6.53 us
    ppermute x1, starting transfers between devices, body(): low = lax.ppermute(rim, 'slab', [(i, i + 1) for i in range(slabs - 1)])  6.35 us
    ppermute x1, starting transfers between devices, body(): other = lax.ppermute(own, 'near', [(0, 1), (1, 0)])  3.83 us
  transfers between devices with their start and end apart: 4, of which 2 were waited for; matrix products, arithmetic and copies ran while one was open for 0% of the time, Pallas kernels for 4%

profile of v8, /device:TPU:24, one launch (start us, length us, event | category | flops | bytes accessed | tf_op | source)
XLA Modules:
  0.0 96.5 jit_solution(11862649640523081267)
XLA Ops:
  0.0 0.9 pack.1
  0.9 3.8 %collective-permute-start = (f32[8,3456]{1,0:T(8,128)S(1)}, f32[8,3456]{1,0:T(8,128)S(1)}, u32[]{:S(2)}, u32[]{:S(2)}) collective-permute-start(f32[8,3456]{1,0:T(8,128)S(1)} %pack.1), channel_id=1, source_target_pairs={{0,16},{16,0},{1,17},{17,1},{2,18},{18,2},{3,19},{19,3},{4,20},{20... | collective-permute-start | bytes 331784 | tf_op jit(solution)/shard_map/ppermute | solution.py:375
  4.8 6.7 %all-gather = f32[32,3456]{1,0:T(8,128)S(1)} all-gather(f32[8,3456]{1,0:T(8,128)S(1)} %pack.1), channel_id=2, replica_groups=mesh['section'=2,'far'=8,'near'=2,'core'=2,'slab'=8] {'section','core'}, dimensions={0}, use_global_device_ids=true | all-gather | bytes 552960 | tf_op jit(solution)/shard_map/all_gather | solution.py:376
  11.5 0.0 collective-permute-done
  11.5 6.8 %all-gather.1 = f32[32,3456]{1,0:T(8,128)S(1)} all-gather(f32[8,3456]{1,0:T(8,128)S(1)} %collective-permute-done), channel_id=3, replica_groups=mesh['section'=2,'far'=8,'near'=2,'core'=2,'slab'=8] {'section','core'}, dimensions={0}, use_global_device_ids=true | all-gather | bytes 552960 | tf_op jit(solution)/shard_map/all_gather | solution.py:377
  18.3 3.3 %node_sums.1 = f32[16,32,128]{2,1,0:T(8,128)} custom-call(s32[1]{0:T(128)} %bitcast.cls, s32[1]{0:T(128)} %bitcast.1.parity, f32[4,8,3456]{2,1,0:T(8,128)S(1)} %bitcast.8, f32[4,8,3456]{2,1,0:T(8,128)S(1)} %bitcast.11), custom_call_target="tpu_custom_call" | custom-call | tf_op jit(solution)/shard_map/node_sums/pallas_call | solution.py:171
  21.6 13.9 %all-to-all-start = ((f32[8,64,128]{2,1,0:T(8,128)}), f32[8,64,128]{2,1,0:T(8,128)S(1)}, u32[]{:S(2)}, u32[]{:S(2)}) async-start(f32[8,64,128]{2,1,0:T(8,128)} %bitcast.5), calls=%async_computation | async-start | bytes 524288 | tf_op jit(solution)/shard_map/all_to_all | solution.py:386
  35.5 0.0 copy-done.1
  35.5 0.0 copy-done
  35.5 1.2 %smooth_once.1 = (f32[16,8,128]{2,1,0:T(8,128)S(1)}, f32[2,8,128]{2,1,0:T(8,128)S(1)}) custom-call(s32[16]{0:T(128)} %kind.3, f32[16]{0:T(128)} %coeff.3, s32[2]{0:T(128)} %halo.1, f32[8,2048]{1,0:T(8,128)S(1)} %copy-done.1, f32[8,128,128]{2,1,0:T(8,128)S(1)} %copy-done), custom_call_target="tpu_custom_call" | custom-call | tf_op jit(solution)/shard_map/smooth_once/pallas_call | solution.py:256
  36.7 3.1 %collective-permute-start.2 = (f32[2,8,128]{2,1,0:T(8,128)S(1)}, f32[2,8,128]{2,1,0:T(8,128)S(1)}, u32[]{:S(2)}, u32[]{:S(2)}) collective-permute-start(f32[2,8,128]{2,1,0:T(8,128)S(1)} %get-tuple-element.13), channel_id=1, source_target_pairs={{1,0},{2,1},{3,2},{4,3},{5,4},{6,5},{7,6},{9,8},{10,9},{11,10},{12... | collective-permute-start | bytes 24584 | tf_op jit(solution)/shard_map/ppermute | solution.py:382
  39.8 6.3 %collective-permute-start.1 = (f32[2,8,128]{2,1,0:T(8,128)S(1)}, f32[2,8,128]{2,1,0:T(8,128)S(1)}, u32[]{:S(2)}, u32[]{:S(2)}) collective-permute-start(f32[2,8,128]{2,1,0:T(8,128)S(1)} %get-tuple-element.13), channel_id=1, source_target_pairs={{0,1},{1,2},{2,3},{3,4},{4,5},{5,6},{6,7},{8,9},{9,10},{10,11},{11... | collective-permute-start | bytes 24584 | tf_op jit(solution)/shard_map/ppermute | solution.py:381
  46.1 0.0 collective-permute-done.2.high
  46.1 1.3 %collective-permute-done.1.low = f32[2,8,128]{2,1,0:T(8,128)S(1)} collective-permute-done((f32[2,8,128]{2,1,0:T(8,128)S(1)}, f32[2,8,128]{2,1,0:T(8,128)S(1)}, u32[]{:S(2)}, u32[]{:S(2)}) %collective-permute-start.1) | collective-permute-done | bytes 8224 | tf_op jit(solution)/shard_map/ppermute | solution.py:381
  47.5 0.0 copy-done.2
  47.5 2.8 %smooth_again.1 = (f32[16,8,128]{2,1,0:T(8,128)S(1)}, s32[2,73]{1,0:T(2,128)}) custom-call(s32[16]{0:T(128)} %kind.3, f32[16]{0:T(128)} %coeff.3, s32[8,16]{1,0:T(8,128)} %cols.1, s32[8,16]{1,0:T(8,128)} %kinds.1, f32[8,16]{1,0:T(8,128)} %coeffs.1, s32[1]{0:T(128)} %bitcast.cls, f32[16,8,128]{2,1,0:T(8,128)S(1)} %get-tuple-element.12.smoothed, ...), custom_call_target="tpu_custom_call" | custom-call | tf_op jit(solution)/shard_map/smooth_again/pallas_call | solution.py:307
  50.3 6.5 %all-to-all-done = f32[8,64,128]{2,1,0:T(8,128)S(1)} async-done(((f32[8,64,128]{2,1,0:T(8,128)}), f32[8,64,128]{2,1,0:T(8,128)S(1)}, u32[]{:S(2)}, u32[]{:S(2)}) %all-to-all-start) | async-done | bytes 262176 | tf_op jit(solution)/shard_map/all_to_all | solution.py:386
  56.9 0.0 copy-done.3
  56.9 0.0 copy-done.4
  56.9 0.2 solve.1
  57.1 29.1 %all_gather.19.values = f32[32,32,128]{2,1,0:T(8,128)S(1)} all-gather(f32[2,32,128]{2,1,0:T(8,128)S(1)} %solve.1), channel_id=1, replica_groups=mesh['section'=2,'far'=8,'near'=2,'core'=2,'slab'=8] {'far','near'}, dimensions={0}, use_global_device_ids=true | all-gather | bytes 557056 | tf_op jit(solution)/shard_map/all_gather | solution.py:395
  86.3 1.1 %back.1 = f32[64,8,128]{2,1,0:T(8,128)S(1)} custom-call(s32[2,73]{1,0:T(2,128)} %get-tuple-element.17.chosen, f32[4,8,3456]{2,1,0:T(8,128)S(1)} %bitcast.10, f32[32,32,128]{2,1,0:T(8,128)S(1)} %all_gather.19.values), custom_call_target="tpu_custom_call" | custom-call | tf_op jit(solution)/shard_map/back/pallas_call | solution.py:229
  87.4 8.4 %all_to_all.10.pieces = f32[4,16,8,128]{3,2,1,0:T(8,128)S(1)} all-to-all(f32[4,16,8,128]{3,2,1,0:T(8,128)S(1)} %bitcast.13), channel_id=1, replica_groups=mesh['section'=2,'far'=8,'near'=2,'core'=2,'slab'=8] {'section','core'}, dimensions={0} | all-to-all | bytes 524288 | tf_op jit(solution)/shard_map/all_to_all | solution.py:397
  95.8 0.6 finish.1
  (5 shorter events, 0.0 us)
Async XLA Ops:
  0.9 10.6 %collective-permute-start = (f32[8,3456]{1,0:T(8,128)S(1)}, f32[8,3456]{1,0:T(8,128)S(1)}, u32[]{:S(2)}, u32[]{:S(2)}) collective-permute-start(f32[8,3456]{1,0:T(8,128)S(1)} %pack.1), channel_id=1, source_target_pairs={{0,16},{16,0},{1,17},{17,1},{2,18},{18,2},{3,19},{19,3},{4,20},{20... | collective-permute-start | bytes 331784 | tf_op jit(solution)/shard_map/ppermute | solution.py:375
  18.3 17.1 %copy-start.1 = (f32[8,2048]{1,0:T(8,128)S(1)}, f32[8,2048]{1,0:T(8,128)}, u32[]{:S(2)}) copy-start(f32[8,2048]{1,0:T(8,128)} %residual.5) | copy-start | bytes 196612
  21.6 13.9 %copy-start = (f32[8,128,128]{2,1,0:T(8,128)S(1)}, f32[8,128,128]{2,1,0:T(8,128)}, u32[]{:S(2)}) copy-start(f32[8,128,128]{2,1,0:T(8,128)} %inverse.3) | copy-start | bytes 1572868
  21.6 25.9 %copy-start.2 = (f32[8,128,128]{2,1,0:T(8,128)S(1)}, f32[8,128,128]{2,1,0:T(8,128)}, u32[]{:S(2)}) copy-start(f32[8,128,128]{2,1,0:T(8,128)} %coupling.1) | copy-start | bytes 1572868
  21.6 35.3 %all-to-all-start = ((f32[8,64,128]{2,1,0:T(8,128)}), f32[8,64,128]{2,1,0:T(8,128)S(1)}, u32[]{:S(2)}, u32[]{:S(2)}) async-start(f32[8,64,128]{2,1,0:T(8,128)} %bitcast.5), calls=%async_computation | async-start | bytes 524288 | tf_op jit(solution)/shard_map/all_to_all | solution.py:386
  36.7 9.5 %collective-permute-start.2 = (f32[2,8,128]{2,1,0:T(8,128)S(1)}, f32[2,8,128]{2,1,0:T(8,128)S(1)}, u32[]{:S(2)}, u32[]{:S(2)}) collective-permute-start(f32[2,8,128]{2,1,0:T(8,128)S(1)} %get-tuple-element.13), channel_id=1, source_target_pairs={{1,0},{2,1},{3,2},{4,3},{5,4},{6,5},{7,6},{9,8},{10,9},{11,10},{12... | collective-permute-start | bytes 24584 | tf_op jit(solution)/shard_map/ppermute | solution.py:382
  39.8 7.7 %collective-permute-start.1 = (f32[2,8,128]{2,1,0:T(8,128)S(1)}, f32[2,8,128]{2,1,0:T(8,128)S(1)}, u32[]{:S(2)}, u32[]{:S(2)}) collective-permute-start(f32[2,8,128]{2,1,0:T(8,128)S(1)} %get-tuple-element.13), channel_id=1, source_target_pairs={{0,1},{1,2},{2,3},{3,4},{4,5},{5,6},{6,7},{8,9},{9,10},{10,11},{11... | collective-permute-start | bytes 24584 | tf_op jit(solution)/shard_map/ppermute | solution.py:381
  47.5 9.4 %copy-start.3 = (f32[2,128,128]{2,1,0:T(8,128)S(1)}, f32[2,128,128]{2,1,0:T(8,128)}, u32[]{:S(2)}) copy-start(f32[2,128,128]{2,1,0:T(8,128)} %grad.1) | copy-start | bytes 393220
  47.5 9.4 %copy-start.4 = (f32[2,128,128]{2,1,0:T(8,128)S(1)}, f32[2,128,128]{2,1,0:T(8,128)}, u32[]{:S(2)}) copy-start(f32[2,128,128]{2,1,0:T(8,128)} %vec.1) | copy-start | bytes 393220

commit v9 on v7

--- a/solution.py
+++ b/solution.py
@@ -128,9 +128,9 @@
     return count
 
 
-def sums_kernel(where, own, other, sums, chosen_own, chosen_other, *, tiles, width):
+def sums_kernel(cls, parity, own, other, sums, chosen_own, chosen_other, *, tiles, width):
     sums[...] = jnp.zeros_like(sums)
-    mine, near = where[0].astype(F32), where[1]
+    mine, near = cls[0].astype(F32), parity[0]
 
     def rule(classes, places):
         fits = (classes == mine) & (((places >> 1) & (NEAR - 1)) == near)
@@ -167,32 +167,32 @@
     return (2, gathered.shape[0] * tiles + 1 + GROUP)
 
 
-def node_sums(where, own, other, tiles, width, places):
+def node_sums(cls, parity, own, other, tiles, width, places):
     return pl.pallas_call(
         functools.partial(sums_kernel, tiles=tiles, width=width),
         out_shape=held((places, 32, width)),
-        in_specs=[smem_spec, vmem_spec, vmem_spec],
+        in_specs=[smem_spec, smem_spec, vmem_spec, vmem_spec],
         out_specs=vmem_spec,
         scratch_shapes=[SMEM(list_shape(own, tiles), jnp.int32) for _ in range(2)],
         name="node_sums",
-    )(where, hold(own), hold(other))
-
-
-def list_kernel(where, gathered, chosen, *, tiles, width):
-    mine = where[0].astype(F32)
+    )(cls, parity, hold(own), hold(other))
+
+
+def list_kernel(cls, gathered, chosen, *, tiles, width):
+    mine = cls[0].astype(F32)
     choose(
         chosen, gathered, tiles, width, lambda classes, places: jnp.where(classes == mine, places, -1)
     )
 
 
-def class_list(where, gathered, tiles, width):
+def class_list(cls, gathered, tiles, width):
     return pl.pallas_call(
         functools.partial(list_kernel, tiles=tiles, width=width),
         out_shape=jax.ShapeDtypeStruct(list_shape(gathered, tiles), jnp.int32),
         in_specs=[smem_spec, vmem_spec],
         out_specs=smem_spec,
         name="class_list",
-    )(where, hold(gathered))
+    )(cls, hold(gathered))
 
 
 def solve_kernel(arrived, grad, vec, out):
@@ -375,7 +375,8 @@
     node_tiles = grad_blocks.shape[0]
     tiles = diag_kind.shape[0]
     width = coupling_tiles.shape[1]
-    where = jnp.stack([lax.axis_index(TEAM), lax.axis_index("near")]).astype(jnp.int32)
+    cls = lax.axis_index(TEAM).astype(jnp.int32).reshape(1)
+    parity = lax.axis_index("near").astype(jnp.int32).reshape(1)
     own = pack(tile_owner[:, 0], node_slot, residual, tangents, edge_nodes, far * NEAR * CORES)
     other = lax.ppermute(own, "near", [(0, 1), (1, 0)])
     gathered = lax.all_gather(own, TEAM)
@@ -386,11 +387,11 @@
     low = lax.ppermute(rim, "slab", [(i, i + 1) for i in range(slabs - 1)])
     high = lax.ppermute(rim, "slab", [(i + 1, i) for i in range(slabs - 1)])
 
-    sums = node_sums(where, gathered, gathered_other, tiles, width, far * node_tiles)
+    sums = node_sums(cls, parity, gathered, gathered_other, tiles, width, far * node_tiles)
     sums = sums.reshape(far, node_tiles * 32, width)
     arrived = lax.all_to_all(sums, "far", split_axis=0, concat_axis=0, tiled=True)
 
-    chosen = class_list(where, gathered, tiles, width)
+    chosen = class_list(cls, gathered, tiles, width)
     smoothed_twice = smooth_again(
         diag_kind, diag_coeff, tile_cols, tile_kinds, tile_coeff,
         smoothed, low, high, residual, coupling_tiles, inverse_tiles,

time: 99.3 us -> 98 us (0.987)
  waiting for transfers between devices: 4.78 us -> 6.96 us
  Pallas kernels: 12.3 us -> 10.2 us
  blocking collectives: 53.1 us -> 51.5 us
  starting transfers between devices: 27.1 us -> 28.1 us
    all_to_all x1, waiting for transfers between devices: 4.77 us -> 6.61 us  [body(): lax.all_to_all(sums, 'far', split_axis=0, concat_axis=0, tiled=True)]
    all_gather x1, blocking collectives: 31.1 us -> 29.5 us  [body(): values = lax.all_gather(solved, HEIGHT, tiled=True)]
    pallas_call x1, Pallas kernels: 4.07 us -> 2.82 us  [node_sums(): pl.pallas_call(functools.partial(sums_kernel, tiles=tiles, width=width),...]
  transfers between devices with their start and end apart: 4 -> 4, of which waited for: 1 -> 2; matrix products, arithmetic and copies ran while one was open for 1% -> 0% of each run, Pallas kernels for 5% -> 5%
where the time goes in v9:
time: 98 us; the launch traced here: 96.9 us
  blocking collectives  51.5 us (53%)
  starting transfers between devices  28.1 us (29%)
  Pallas kernels  10.2 us (10%)
  waiting for transfers between devices  6.96 us (7%)
    all_gather x1, blocking collectives, body(): values = lax.all_gather(solved, HEIGHT, tiled=True)  29.5 us
    all_to_all x1, starting transfers between devices, body(): lax.all_to_all(sums, 'far', split_axis=0, concat_axis=0, tiled=True)  14.8 us
    all_to_all x1, blocking collectives, body(): lax.all_to_all(corrections, TEAM, split_axis=0, concat_axis=0, tiled=True)  8.42 us
    ppermute x1, starting transfers between devices, body(): low = lax.ppermute(rim, 'slab', [(i, i + 1) for i in range(slabs - 1)])  7.27 us
    all_gather x1, blocking collectives, body(): gathered_other = lax.all_gather(other, TEAM)  6.83 us
    all_gather x1, blocking collectives, body(): gathered = lax.all_gather(own, TEAM)  6.73 us
    all_to_all x1, waiting for transfers between devices, body(): lax.all_to_all(sums, 'far', split_axis=0, concat_axis=0, tiled=True)  6.61 us
    ppermute x1, starting transfers between devices, body(): other = lax.ppermute(own, 'near', [(0, 1), (1, 0)])  3.83 us
  transfers between devices with their start and end apart: 4, of which 2 were waited for; matrix products, arithmetic and copies ran while one was open for 0% of the time, Pallas kernels for 5%

profile of v9, /device:TPU:24, one launch (start us, length us, event | category | flops | bytes accessed | tf_op | source)
XLA Modules:
  0.0 96.9 jit_solution(7846912736168474370)
XLA Ops:
  0.0 0.9 pack.1
  0.9 3.8 %collective-permute-start = (f32[8,3456]{1,0:T(8,128)S(1)}, f32[8,3456]{1,0:T(8,128)S(1)}, u32[]{:S(2)}, u32[]{:S(2)}) collective-permute-start(f32[8,3456]{1,0:T(8,128)S(1)} %pack.1), channel_id=1, source_target_pairs={{0,16},{16,0},{1,17},{17,1},{2,18},{18,2},{3,19},{19,3},{4,20},{20... | collective-permute-start | bytes 331784 | tf_op jit(solution)/shard_map/ppermute | solution.py:381
  4.8 6.7 %all-gather = f32[32,3456]{1,0:T(8,128)S(1)} all-gather(f32[8,3456]{1,0:T(8,128)S(1)} %pack.1), channel_id=2, replica_groups=mesh['section'=2,'far'=8,'near'=2,'core'=2,'slab'=8] {'section','core'}, dimensions={0}, use_global_device_ids=true | all-gather | bytes 552960 | tf_op jit(solution)/shard_map/all_gather | solution.py:382
  11.5 0.0 collective-permute-done
  11.5 6.8 %all-gather.1 = f32[32,3456]{1,0:T(8,128)S(1)} all-gather(f32[8,3456]{1,0:T(8,128)S(1)} %collective-permute-done), channel_id=3, replica_groups=mesh['section'=2,'far'=8,'near'=2,'core'=2,'slab'=8] {'section','core'}, dimensions={0}, use_global_device_ids=true | all-gather | bytes 552960 | tf_op jit(solution)/shard_map/all_gather | solution.py:383
  18.3 2.8 %node_sums.1 = f32[16,32,128]{2,1,0:T(8,128)} custom-call(s32[1]{0:T(128)} %bitcast.cls, s32[1]{0:T(128)} %bitcast.1.parity, f32[4,8,3456]{2,1,0:T(8,128)S(1)} %bitcast.8, f32[4,8,3456]{2,1,0:T(8,128)S(1)} %bitcast.11), custom_call_target="tpu_custom_call" | custom-call | tf_op jit(solution)/shard_map/node_sums/pallas_call | solution.py:171
  21.2 14.8 %all-to-all-start = ((f32[8,64,128]{2,1,0:T(8,128)}), f32[8,64,128]{2,1,0:T(8,128)S(1)}, u32[]{:S(2)}, u32[]{:S(2)}) async-start(f32[8,64,128]{2,1,0:T(8,128)} %bitcast.5), calls=%async_computation | async-start | bytes 524288 | tf_op jit(solution)/shard_map/all_to_all | solution.py:392
  35.9 0.0 copy-done.1
  35.9 0.0 copy-start.2
  36.0 1.3 %smooth_once.1 = (f32[16,8,128]{2,1,0:T(8,128)S(1)}, f32[2,8,128]{2,1,0:T(8,128)S(1)}) custom-call(s32[16]{0:T(128)} %kind.3, f32[16]{0:T(128)} %coeff.3, s32[2]{0:T(128)} %halo.1, f32[8,2048]{1,0:T(8,128)S(1)} %copy-done.1, f32[8,128,128]{2,1,0:T(8,128)S(1)} %copy-done), custom_call_target="tpu_custom_call" | custom-call | tf_op jit(solution)/shard_map/smooth_once/pallas_call | solution.py:273
  37.3 2.2 %collective-permute-start.2 = (f32[2,8,128]{2,1,0:T(8,128)S(1)}, f32[2,8,128]{2,1,0:T(8,128)S(1)}, u32[]{:S(2)}, u32[]{:S(2)}) collective-permute-start(f32[2,8,128]{2,1,0:T(8,128)S(1)} %get-tuple-element.11), channel_id=1, source_target_pairs={{1,0},{2,1},{3,2},{4,3},{5,4},{6,5},{7,6},{9,8},{10,9},{11,10},{12... | collective-permute-start | bytes 24584 | tf_op jit(solution)/shard_map/ppermute | solution.py:388
  39.5 7.3 %collective-permute-start.1 = (f32[2,8,128]{2,1,0:T(8,128)S(1)}, f32[2,8,128]{2,1,0:T(8,128)S(1)}, u32[]{:S(2)}, u32[]{:S(2)}) collective-permute-start(f32[2,8,128]{2,1,0:T(8,128)S(1)} %get-tuple-element.11), channel_id=1, source_target_pairs={{0,1},{1,2},{2,3},{3,4},{4,5},{5,6},{6,7},{8,9},{9,10},{10,11},{11... | collective-permute-start | bytes 24584 | tf_op jit(solution)/shard_map/ppermute | solution.py:387
  46.7 1.0 %class_list.1.chosen = s32[2,73]{1,0:T(2,128)} custom-call(s32[1]{0:T(128)} %bitcast.cls, f32[4,8,3456]{2,1,0:T(8,128)S(1)} %bitcast.9), custom_call_target="tpu_custom_call" | custom-call | tf_op jit(solution)/shard_map/class_list/pallas_call | solution.py:189
  47.7 0.0 collective-permute-done.2.high
  47.7 0.3 collective-permute-done.1.low
  48.1 0.0 copy-done.2
  48.1 2.2 %smooth_again.1.smoothed = f32[16,8,128]{2,1,0:T(8,128)S(1)} custom-call(s32[16]{0:T(128)} %kind.3, f32[16]{0:T(128)} %coeff.3, s32[8,16]{1,0:T(8,128)} %cols.1, s32[8,16]{1,0:T(8,128)} %kinds.1, f32[8,16]{1,0:T(8,128)} %coeffs.1, f32[16,8,128]{2,1,0:T(8,128)S(1)} %get-tuple-element.10.smoothed, f32[2,8,128]{2,1,0:T(8,128)S(1)} %collective-permute-done.1.low, ...), custom_call_target="tpu_custom_call" | custom-call | tf_op jit(solution)/shard_map/smooth_again/pallas_call | solution.py:317
  50.2 6.6 %all-to-all-done = f32[8,64,128]{2,1,0:T(8,128)S(1)} async-done(((f32[8,64,128]{2,1,0:T(8,128)}), f32[8,64,128]{2,1,0:T(8,128)S(1)}, u32[]{:S(2)}, u32[]{:S(2)}) %all-to-all-start) | async-done | bytes 262176 | tf_op jit(solution)/shard_map/all_to_all | solution.py:392
  56.9 0.0 copy-done.4
  56.9 0.2 solve.1
  57.1 29.5 %all_gather.19.values = f32[32,32,128]{2,1,0:T(8,128)S(1)} all-gather(f32[2,32,128]{2,1,0:T(8,128)S(1)} %solve.1), channel_id=1, replica_groups=mesh['section'=2,'far'=8,'near'=2,'core'=2,'slab'=8] {'far','near'}, dimensions={0}, use_global_device_ids=true | all-gather | bytes 557056 | tf_op jit(solution)/shard_map/all_gather | solution.py:402
  86.7 1.1 %back.1 = f32[64,8,128]{2,1,0:T(8,128)S(1)} custom-call(s32[2,73]{1,0:T(2,128)} %class_list.1.chosen, f32[4,8,3456]{2,1,0:T(8,128)S(1)} %bitcast.10, f32[32,32,128]{2,1,0:T(8,128)S(1)} %all_gather.19.values), custom_call_target="tpu_custom_call" | custom-call | tf_op jit(solution)/shard_map/back/pallas_call | solution.py:246
  87.8 8.4 %all_to_all.10.pieces = f32[4,16,8,128]{3,2,1,0:T(8,128)S(1)} all-to-all(f32[4,16,8,128]{3,2,1,0:T(8,128)S(1)} %bitcast.13), channel_id=1, replica_groups=mesh['section'=2,'far'=8,'near'=2,'core'=2,'slab'=8] {'section','core'}, dimensions={0} | all-to-all | bytes 524288 | tf_op jit(solution)/shard_map/all_to_all | solution.py:404
  96.2 0.6 finish.1
  (6 shorter events, 0.0 us)
Async XLA Ops:
  0.9 10.6 %collective-permute-start = (f32[8,3456]{1,0:T(8,128)S(1)}, f32[8,3456]{1,0:T(8,128)S(1)}, u32[]{:S(2)}, u32[]{:S(2)}) collective-permute-start(f32[8,3456]{1,0:T(8,128)S(1)} %pack.1), channel_id=1, source_target_pairs={{0,16},{16,0},{1,17},{17,1},{2,18},{18,2},{3,19},{19,3},{4,20},{20... | collective-permute-start | bytes 331784 | tf_op jit(solution)/shard_map/ppermute | solution.py:381
  18.3 17.6 %copy-start.1 = (f32[8,2048]{1,0:T(8,128)S(1)}, f32[8,2048]{1,0:T(8,128)}, u32[]{:S(2)}) copy-start(f32[8,2048]{1,0:T(8,128)} %residual.5) | copy-start | bytes 196612
  21.2 14.8 %copy-start = (f32[8,128,128]{2,1,0:T(8,128)S(1)}, f32[8,128,128]{2,1,0:T(8,128)}, u32[]{:S(2)}) copy-start(f32[8,128,128]{2,1,0:T(8,128)} %inverse.3) | copy-start | bytes 1572868
  21.2 35.7 %all-to-all-start = ((f32[8,64,128]{2,1,0:T(8,128)}), f32[8,64,128]{2,1,0:T(8,128)S(1)}, u32[]{:S(2)}, u32[]{:S(2)}) async-start(f32[8,64,128]{2,1,0:T(8,128)} %bitcast.5), calls=%async_computation | async-start | bytes 524288 | tf_op jit(solution)/shard_map/all_to_all | solution.py:392
  35.9 12.1 %copy-start.2 = (f32[8,128,128]{2,1,0:T(8,128)S(1)}, f32[8,128,128]{2,1,0:T(8,128)}, u32[]{:S(2)}) copy-start(f32[8,128,128]{2,1,0:T(8,128)} %coupling.1) | copy-start | bytes 1572868
  37.3 10.5 %collective-permute-start.2 = (f32[2,8,128]{2,1,0:T(8,128)S(1)}, f32[2,8,128]{2,1,0:T(8,128)S(1)}, u32[]{:S(2)}, u32[]{:S(2)}) collective-permute-start(f32[2,8,128]{2,1,0:T(8,128)S(1)} %get-tuple-element.11), channel_id=1, source_target_pairs={{1,0},{2,1},{3,2},{4,3},{5,4},{6,5},{7,6},{9,8},{10,9},{11,10},{12... | collective-permute-start | bytes 24584 | tf_op jit(solution)/shard_map/ppermute | solution.py:388
  39.5 8.6 %collective-permute-start.1 = (f32[2,8,128]{2,1,0:T(8,128)S(1)}, f32[2,8,128]{2,1,0:T(8,128)S(1)}, u32[]{:S(2)}, u32[]{:S(2)}) collective-permute-start(f32[2,8,128]{2,1,0:T(8,128)S(1)} %get-tuple-element.11), channel_id=1, source_target_pairs={{0,1},{1,2},{2,3},{3,4},{4,5},{5,6},{6,7},{8,9},{9,10},{10,11},{11... | collective-permute-start | bytes 24584 | tf_op jit(solution)/shard_map/ppermute | solution.py:387
  48.1 8.8 %copy-start.3 = (f32[2,128,128]{2,1,0:T(8,128)S(1)}, f32[2,128,128]{2,1,0:T(8,128)}, u32[]{:S(2)}) copy-start(f32[2,128,128]{2,1,0:T(8,128)} %grad.1) | copy-start | bytes 393220
  48.1 8.8 %copy-start.4 = (f32[2,128,128]{2,1,0:T(8,128)S(1)}, f32[2,128,128]{2,1,0:T(8,128)}, u32[]{:S(2)}) copy-start(f32[2,128,128]{2,1,0:T(8,128)} %vec.1) | copy-start | bytes 393220

commit v10 on v9

--- a/solution.py
+++ b/solution.py
@@ -392,16 +392,20 @@
     arrived = lax.all_to_all(sums, "far", split_axis=0, concat_axis=0, tiled=True)
 
     chosen = class_list(cls, gathered, tiles, width)
-    smoothed_twice = smooth_again(
-        diag_kind, diag_coeff, tile_cols, tile_kinds, tile_coeff,
-        smoothed, low, high, residual, coupling_tiles, inverse_tiles,
-    )
-    arrived, smoothed_twice, chosen = lax.optimization_barrier((arrived, smoothed_twice, chosen))
+    arrived, chosen, smoothed, low, high = lax.optimization_barrier(
+        (arrived, chosen, smoothed, low, high)
+    )
 
     solved = solve(arrived.reshape(far, node_tiles, 32, width), grad_blocks, vec_blocks)
     values = lax.all_gather(solved, HEIGHT, tiled=True)
     corrections = back(chosen, gathered, values, tiles).reshape(team, tiles, 8, width)
     pieces = lax.all_to_all(corrections, TEAM, split_axis=0, concat_axis=0, tiled=True)
+
+    low, high, values = lax.optimization_barrier((low, high, values))
+    smoothed_twice = smooth_again(
+        diag_kind, diag_coeff, tile_cols, tile_kinds, tile_coeff,
+        smoothed, low, high, residual, coupling_tiles, inverse_tiles,
+    )
     return finish(smoothed_twice, pieces)
 
 

time: 98 us -> 99.4 us (1.014)
  waiting for transfers between devices: 6.96 us -> 17.3 us
  blocking collectives: 51.5 us -> 42.6 us
    all_to_all x1 -> x0, blocking collectives: 8.42 us -> none  [body(): lax.all_to_all(corrections, TEAM, split_axis=0, concat_axis=0, tiled=True)]
    ppermute x1, waiting for transfers between devices: 0.01 us -> 6.23 us  [body(): high = lax.ppermute(rim, 'slab', [(i + 1, i) for i in range(slabs - 1)])]
    all_to_all x0 -> x1, waiting for transfers between devices: none -> 3.95 us  [body(): lax.all_to_all(corrections, TEAM, split_axis=0, concat_axis=0, tiled=True)]
    all_to_all x0 -> x1, starting transfers between devices: none -> 3.54 us  [body(): lax.all_to_all(corrections, TEAM, split_axis=0, concat_axis=0, tiled=True)]
    ppermute x1, starting transfers between devices: 7.27 us -> 4.43 us  [body(): low = lax.ppermute(rim, 'slab', [(i, i + 1) for i in range(slabs - 1)])]
  transfers between devices with their start and end apart: 4 -> 5, of which waited for: 2 -> 3; matrix products, arithmetic and copies ran while one was open for 0% -> 0% of each run, Pallas kernels for 5% -> 4%
where the time goes in v10:
time: 99.4 us; the launch traced here: 98.3 us
  blocking collectives  42.6 us (43%)
  starting transfers between devices  28 us (28%)
  waiting for transfers between devices  17.3 us (17%)
  Pallas kernels  10.2 us (10%)
    all_gather x1, blocking collectives, body(): values = lax.all_gather(solved, HEIGHT, tiled=True)  29.1 us
    all_to_all x1, starting transfers between devices, body(): lax.all_to_all(sums, 'far', split_axis=0, concat_axis=0, tiled=True)  14.3 us
    all_to_all x1, waiting for transfers between devices, body(): lax.all_to_all(sums, 'far', split_axis=0, concat_axis=0, tiled=True)  7.06 us
    all_gather x1, blocking collectives, body(): gathered_other = lax.all_gather(other, TEAM)  6.83 us
    all_gather x1, blocking collectives, body(): gathered = lax.all_gather(own, TEAM)  6.73 us
    ppermute x1, waiting for transfers between devices, body(): high = lax.ppermute(rim, 'slab', [(i + 1, i) for i in range(slabs - 1)])  6.23 us
    ppermute x1, starting transfers between devices, body(): low = lax.ppermute(rim, 'slab', [(i, i + 1) for i in range(slabs - 1)])  4.43 us
    all_to_all x1, waiting for transfers between devices, body(): lax.all_to_all(corrections, TEAM, split_axis=0, concat_axis=0, tiled=True)  3.95 us
  transfers between devices with their start and end apart: 5, of which 3 were waited for; matrix products, arithmetic and copies ran while one was open for 0% of the time, Pallas kernels for 4%

profile of v10, /device:TPU:24, one launch (start us, length us, event | category | flops | bytes accessed | tf_op | source)
XLA Modules:
  0.0 98.3 jit_solution(10998064701063664906)
XLA Ops:
  0.0 0.9 pack.1
  0.9 3.8 %collective-permute-start = (f32[8,3456]{1,0:T(8,128)S(1)}, f32[8,3456]{1,0:T(8,128)S(1)}, u32[]{:S(2)}, u32[]{:S(2)}) collective-permute-start(f32[8,3456]{1,0:T(8,128)S(1)} %pack.1), channel_id=1, source_target_pairs={{0,16},{16,0},{1,17},{17,1},{2,18},{18,2},{3,19},{19,3},{4,20},{20... | collective-permute-start | bytes 331784 | tf_op jit(solution)/shard_map/ppermute | solution.py:381
  4.8 6.7 %all-gather = f32[32,3456]{1,0:T(8,128)S(1)} all-gather(f32[8,3456]{1,0:T(8,128)S(1)} %pack.1), channel_id=2, replica_groups=mesh['section'=2,'far'=8,'near'=2,'core'=2,'slab'=8] {'section','core'}, dimensions={0}, use_global_device_ids=true | all-gather | bytes 552960 | tf_op jit(solution)/shard_map/all_gather | solution.py:382
  11.5 0.0 collective-permute-done
  11.5 6.8 %all-gather.1 = f32[32,3456]{1,0:T(8,128)S(1)} all-gather(f32[8,3456]{1,0:T(8,128)S(1)} %collective-permute-done), channel_id=3, replica_groups=mesh['section'=2,'far'=8,'near'=2,'core'=2,'slab'=8] {'section','core'}, dimensions={0}, use_global_device_ids=true | all-gather | bytes 552960 | tf_op jit(solution)/shard_map/all_gather | solution.py:383
  18.3 2.4 %node_sums.1 = f32[16,32,128]{2,1,0:T(8,128)} custom-call(s32[1]{0:T(128)} %bitcast.cls, s32[1]{0:T(128)} %bitcast.1.parity, f32[4,8,3456]{2,1,0:T(8,128)S(1)} %bitcast.8, f32[4,8,3456]{2,1,0:T(8,128)S(1)} %bitcast.11), custom_call_target="tpu_custom_call" | custom-call | tf_op jit(solution)/shard_map/node_sums/pallas_call | solution.py:171
  20.7 14.3 %all-to-all-start = ((f32[8,64,128]{2,1,0:T(8,128)}), f32[8,64,128]{2,1,0:T(8,128)S(1)}, u32[]{:S(2)}, u32[]{:S(2)}) async-start(f32[8,64,128]{2,1,0:T(8,128)} %bitcast.5), calls=%async_computation | async-start | bytes 524288 | tf_op jit(solution)/shard_map/all_to_all | solution.py:392
  35.0 0.0 copy-done.1
  35.0 1.2 %smooth_once.1 = (f32[16,8,128]{2,1,0:T(8,128)S(1)}, f32[2,8,128]{2,1,0:T(8,128)S(1)}) custom-call(s32[16]{0:T(128)} %kind.3, f32[16]{0:T(128)} %coeff.3, s32[2]{0:T(128)} %halo.1, f32[8,2048]{1,0:T(8,128)S(1)} %copy-done.1, f32[8,128,128]{2,1,0:T(8,128)S(1)} %copy-done), custom_call_target="tpu_custom_call" | custom-call | tf_op jit(solution)/shard_map/smooth_once/pallas_call | solution.py:273
  36.2 0.0 copy-start.3
  36.2 0.0 copy-start.4
  36.2 4.4 %collective-permute-start.1 = (f32[2,8,128]{2,1,0:T(8,128)S(1)}, f32[2,8,128]{2,1,0:T(8,128)S(1)}, u32[]{:S(2)}, u32[]{:S(2)}) collective-permute-start(f32[2,8,128]{2,1,0:T(8,128)S(1)} %get-tuple-element.15), channel_id=1, source_target_pairs={{0,1},{1,2},{2,3},{3,4},{4,5},{5,6},{6,7},{8,9},{9,10},{10,11},{11... | collective-permute-start | bytes 24584 | tf_op jit(solution)/shard_map/ppermute | solution.py:387
  40.7 1.9 %collective-permute-start.2 = (f32[2,8,128]{2,1,0:T(8,128)S(1)}, f32[2,8,128]{2,1,0:T(8,128)S(1)}, u32[]{:S(2)}, u32[]{:S(2)}) collective-permute-start(f32[2,8,128]{2,1,0:T(8,128)S(1)} %get-tuple-element.15), channel_id=1, source_target_pairs={{1,0},{2,1},{3,2},{4,3},{5,4},{6,5},{7,6},{9,8},{10,9},{11,10},{12... | collective-permute-start | bytes 24584 | tf_op jit(solution)/shard_map/ppermute | solution.py:388
  42.6 1.0 class_list.1.chosen
  43.6 0.0 collective-permute-done.1.low
  43.6 6.2 %collective-permute-done.2.high = f32[2,8,128]{2,1,0:T(8,128)S(1)} collective-permute-done((f32[2,8,128]{2,1,0:T(8,128)S(1)}, f32[2,8,128]{2,1,0:T(8,128)S(1)}, u32[]{:S(2)}, u32[]{:S(2)}) %collective-permute-start.2) | collective-permute-done | bytes 8224 | tf_op jit(solution)/shard_map/ppermute | solution.py:388
  49.8 7.1 %all-to-all-done = f32[8,64,128]{2,1,0:T(8,128)S(1)} async-done(((f32[8,64,128]{2,1,0:T(8,128)}), f32[8,64,128]{2,1,0:T(8,128)S(1)}, u32[]{:S(2)}, u32[]{:S(2)}) %all-to-all-start) | async-done | bytes 262176 | tf_op jit(solution)/shard_map/all_to_all | solution.py:392
  56.9 0.2 solve.1
  57.1 29.1 %all_gather.19.values = f32[32,32,128]{2,1,0:T(8,128)S(1)} all-gather(f32[2,32,128]{2,1,0:T(8,128)S(1)} %solve.1), channel_id=1, replica_groups=mesh['section'=2,'far'=8,'near'=2,'core'=2,'slab'=8] {'far','near'}, dimensions={0}, use_global_device_ids=true | all-gather | bytes 557056 | tf_op jit(solution)/shard_map/all_gather | solution.py:400
  86.2 1.8 %back.1 = f32[64,8,128]{2,1,0:T(8,128)} custom-call(s32[2,73]{1,0:T(2,128)} %class_list.1.chosen, f32[4,8,3456]{2,1,0:T(8,128)S(1)} %bitcast.10, f32[32,32,128]{2,1,0:T(8,128)S(1)} %all_gather.19.values), custom_call_target="tpu_custom_call" | custom-call | tf_op jit(solution)/shard_map/back/pallas_call | solution.py:246
  88.1 3.5 %all-to-all-start.1 = ((f32[4,16,8,128]{3,2,1,0:T(8,128)}), f32[4,16,8,128]{3,2,1,0:T(8,128)S(1)}, u32[]{:S(2)}, u32[]{:S(2)}) async-start(f32[4,16,8,128]{3,2,1,0:T(8,128)} %bitcast.7), calls=%async_computation.1 | async-start | bytes 524288 | tf_op jit(solution)/shard_map/all_to_all | solution.py:402
  91.6 2.0 %smooth_again.1.smoothed = f32[16,8,128]{2,1,0:T(8,128)S(1)} custom-call(s32[16]{0:T(128)} %kind.3, f32[16]{0:T(128)} %coeff.3, s32[8,16]{1,0:T(8,128)} %cols.1, s32[8,16]{1,0:T(8,128)} %kinds.1, f32[8,16]{1,0:T(8,128)} %coeffs.1, f32[16,8,128]{2,1,0:T(8,128)S(1)} %get-tuple-element.16.smoothed, f32[2,8,128]{2,1,0:T(8,128)S(1)} %collective-permute-done.1.low, ...), custom_call_target="tpu_custom_call" | custom-call | tf_op jit(solution)/shard_map/smooth_again/pallas_call | solution.py:317
  93.7 4.0 %all-to-all-done.1.pieces = f32[4,16,8,128]{3,2,1,0:T(8,128)S(1)} async-done(((f32[4,16,8,128]{3,2,1,0:T(8,128)}), f32[4,16,8,128]{3,2,1,0:T(8,128)S(1)}, u32[]{:S(2)}, u32[]{:S(2)}) %all-to-all-start.1) | async-done | bytes 262176 | tf_op jit(solution)/shard_map/all_to_all | solution.py:402
  97.6 0.6 finish.1
  (7 shorter events, 0.0 us)
Async XLA Ops:
  0.9 10.6 %collective-permute-start = (f32[8,3456]{1,0:T(8,128)S(1)}, f32[8,3456]{1,0:T(8,128)S(1)}, u32[]{:S(2)}, u32[]{:S(2)}) collective-permute-start(f32[8,3456]{1,0:T(8,128)S(1)} %pack.1), channel_id=1, source_target_pairs={{0,16},{16,0},{1,17},{17,1},{2,18},{18,2},{3,19},{19,3},{4,20},{20... | collective-permute-start | bytes 331784 | tf_op jit(solution)/shard_map/ppermute | solution.py:381
  18.3 16.7 %copy-start.1 = (f32[8,2048]{1,0:T(8,128)S(1)}, f32[8,2048]{1,0:T(8,128)}, u32[]{:S(2)}) copy-start(f32[8,2048]{1,0:T(8,128)} %residual.5) | copy-start | bytes 196612
  20.7 14.3 %copy-start = (f32[8,128,128]{2,1,0:T(8,128)S(1)}, f32[8,128,128]{2,1,0:T(8,128)}, u32[]{:S(2)}) copy-start(f32[8,128,128]{2,1,0:T(8,128)} %inverse.3) | copy-start | bytes 1572868
  20.7 36.2 %all-to-all-start = ((f32[8,64,128]{2,1,0:T(8,128)}), f32[8,64,128]{2,1,0:T(8,128)S(1)}, u32[]{:S(2)}, u32[]{:S(2)}) async-start(f32[8,64,128]{2,1,0:T(8,128)} %bitcast.5), calls=%async_computation | async-start | bytes 524288 | tf_op jit(solution)/shard_map/all_to_all | solution.py:392
  36.2 20.7 %copy-start.3 = (f32[2,128,128]{2,1,0:T(8,128)S(1)}, f32[2,128,128]{2,1,0:T(8,128)}, u32[]{:S(2)}) copy-start(f32[2,128,128]{2,1,0:T(8,128)} %grad.1) | copy-start | bytes 393220
  36.2 20.7 %copy-start.4 = (f32[2,128,128]{2,1,0:T(8,128)S(1)}, f32[2,128,128]{2,1,0:T(8,128)}, u32[]{:S(2)}) copy-start(f32[2,128,128]{2,1,0:T(8,128)} %vec.1) | copy-start | bytes 393220
  36.2 7.4 %collective-permute-start.1 = (f32[2,8,128]{2,1,0:T(8,128)S(1)}, f32[2,8,128]{2,1,0:T(8,128)S(1)}, u32[]{:S(2)}, u32[]{:S(2)}) collective-permute-start(f32[2,8,128]{2,1,0:T(8,128)S(1)} %get-tuple-element.15), channel_id=1, source_target_pairs={{0,1},{1,2},{2,3},{3,4},{4,5},{5,6},{6,7},{8,9},{9,10},{10,11},{11... | collective-permute-start | bytes 24584 | tf_op jit(solution)/shard_map/ppermute | solution.py:387
  40.7 9.2 %collective-permute-start.2 = (f32[2,8,128]{2,1,0:T(8,128)S(1)}, f32[2,8,128]{2,1,0:T(8,128)S(1)}, u32[]{:S(2)}, u32[]{:S(2)}) collective-permute-start(f32[2,8,128]{2,1,0:T(8,128)S(1)} %get-tuple-element.15), channel_id=1, source_target_pairs={{1,0},{2,1},{3,2},{4,3},{5,4},{6,5},{7,6},{9,8},{10,9},{11,10},{12... | collective-permute-start | bytes 24584 | tf_op jit(solution)/shard_map/ppermute | solution.py:388
  88.1 3.5 %copy-start.2 = (f32[8,128,128]{2,1,0:T(8,128)S(1)}, f32[8,128,128]{2,1,0:T(8,128)}, u32[]{:S(2)}) copy-start(f32[8,128,128]{2,1,0:T(8,128)} %coupling.1) | copy-start | bytes 1572868
  88.1 9.5 %all-to-all-start.1 = ((f32[4,16,8,128]{3,2,1,0:T(8,128)}), f32[4,16,8,128]{3,2,1,0:T(8,128)S(1)}, u32[]{:S(2)}, u32[]{:S(2)}) async-start(f32[4,16,8,128]{3,2,1,0:T(8,128)} %bitcast.7), calls=%async_computation.1 | async-start | bytes 524288 | tf_op jit(solution)/shard_map/all_to_all | solution.py:402

commit v11 on v9

--- a/solution.py
+++ b/solution.py
@@ -114,7 +114,7 @@
     count = jnp.int32(0)
     for q in range(gathered.shape[0]):
         block = gathered[q, :, gathered.shape[2] - width :]
-        codes = rule(block[0:1], block[1:2].astype(jnp.int32))
+        codes = rule(q, block[0:1], block[1:2].astype(jnp.int32))
         for t in range(tiles):
             code = codes[0, t]
             chosen[0, count + 1] = q * tiles + t
@@ -128,71 +128,70 @@
     return count
 
 
-def sums_kernel(cls, parity, own, other, sums, chosen_own, chosen_other, *, tiles, width):
+def sums_kernel(cls, parity, gathered, sums, chosen, *, tiles, width):
     sums[...] = jnp.zeros_like(sums)
     mine, near = cls[0].astype(F32), parity[0]
 
-    def rule(classes, places):
+    def rule(q, classes, places):
         fits = (classes == mine) & (((places >> 1) & (NEAR - 1)) == near)
         return jnp.where(fits, (places >> NEAR) * 2 + (places & 1), -1)
 
     nodes = lax.broadcasted_iota(jnp.int32, (width, width), 0).astype(F32)
-    counts = [
-        choose(chosen, gathered, tiles, width, rule)
-        for chosen, gathered in ((chosen_own, own), (chosen_other, other))
-    ]
-    for count, chosen, gathered in zip(counts, (chosen_own, chosen_other), (own, other)):
-
-        def step(i, carry, count=count, chosen=chosen, gathered=gathered):
-            for j in range(GROUP):
-                at = i * GROUP + j + 1
-                tile, local = chosen[0, at], chosen[1, at]
-                residual, field = tile_reader(gathered, tile, tiles, width)
-                rows = residual() * jnp.where(at <= count, 1.0, 0.0)
-                at_a = (nodes == field(3)).astype(F32)
-                at_b = (nodes == field(4)).astype(F32)
-                plus = (at_a + at_b).astype(BF16)
-                minus = (at_b - at_a).astype(BF16)
-                vec = jnp.concatenate([(0.5 * field(c)) * rows for c in range(3)], axis=0)
-                total_vec = dot_nt(stacked(vec), plus)
-                total_grad = dot_nt(stacked(rows), minus)
-                sums[local, 0:8, :] += total_grad[:8] + total_grad[8:]
-                sums[local, 8:32, :] += total_vec[:24] + total_vec[24:]
-            return carry
-
-        lax.fori_loop(0, (count + GROUP - 1) // GROUP, step, 0)
+    count = choose(chosen, gathered, tiles, width, rule)
+
+    def step(i, carry):
+        for j in range(GROUP):
+            at = i * GROUP + j + 1
+            tile, local = chosen[0, at], chosen[1, at]
+            residual, field = tile_reader(gathered, tile, tiles, width)
+            rows = residual() * jnp.where(at <= count, 1.0, 0.0)
+            at_a = (nodes == field(3)).astype(F32)
+            at_b = (nodes == field(4)).astype(F32)
+            plus = (at_a + at_b).astype(BF16)
+            minus = (at_b - at_a).astype(BF16)
+            vec = jnp.concatenate([(0.5 * field(c)) * rows for c in range(3)], axis=0)
+            total_vec = dot_nt(stacked(vec), plus)
+            total_grad = dot_nt(stacked(rows), minus)
+            sums[local, 0:8, :] += total_grad[:8] + total_grad[8:]
+            sums[local, 8:32, :] += total_vec[:24] + total_vec[24:]
+        return carry
+
+    lax.fori_loop(0, (count + GROUP - 1) // GROUP, step, 0)
 
 
 def list_shape(gathered, tiles):
     return (2, gathered.shape[0] * tiles + 1 + GROUP)
 
 
-def node_sums(cls, parity, own, other, tiles, width, places):
+def node_sums(cls, parity, gathered, tiles, width, places):
     return pl.pallas_call(
         functools.partial(sums_kernel, tiles=tiles, width=width),
         out_shape=held((places, 32, width)),
-        in_specs=[smem_spec, smem_spec, vmem_spec, vmem_spec],
-        out_specs=vmem_spec,
-        scratch_shapes=[SMEM(list_shape(own, tiles), jnp.int32) for _ in range(2)],
+        in_specs=[smem_spec, smem_spec, vmem_spec],
+        out_specs=vmem_spec,
+        scratch_shapes=[SMEM(list_shape(gathered, tiles), jnp.int32)],
         name="node_sums",
-    )(cls, parity, hold(own), hold(other))
-
-
-def list_kernel(cls, gathered, chosen, *, tiles, width):
+    )(cls, parity, hold(gathered))
+
+
+def list_kernel(cls, parity, gathered, chosen, *, tiles, width):
     mine = cls[0].astype(F32)
-    choose(
-        chosen, gathered, tiles, width, lambda classes, places: jnp.where(classes == mine, places, -1)
-    )
-
-
-def class_list(cls, gathered, tiles, width):
+
+    def rule(q, classes, places):
+        beside = jnp.where(parity[0] == (q // CORES) % NEAR, mine, -1.0)
+        return jnp.where(classes == beside, places, -1)
+
+    choose(chosen, gathered, tiles, width, rule)
+
+
+def class_list(cls, parity, gathered, tiles, width):
     return pl.pallas_call(
         functools.partial(list_kernel, tiles=tiles, width=width),
         out_shape=jax.ShapeDtypeStruct(list_shape(gathered, tiles), jnp.int32),
-        in_specs=[smem_spec, vmem_spec],
+        in_specs=[smem_spec, smem_spec, vmem_spec],
         out_specs=smem_spec,
         name="class_list",
-    )(cls, hold(gathered))
+    )(cls, parity, hold(gathered))
 
 
 def solve_kernel(arrived, grad, vec, out):
@@ -215,9 +214,9 @@
     )(hold(arrived), hold(grad), hold(vec))
 
 
-def back_kernel(chosen, gathered, values, out):
+def back_kernel(chosen, gathered, values, out, *, tiles):
     out[...] = jnp.zeros_like(out)
-    total, _, width = out.shape
+    width = out.shape[2]
 
     def pick(rows, index):
         return jnp.take_along_axis(rows, index, axis=1)
@@ -226,7 +225,7 @@
         for j in range(GROUP):
             at = i * GROUP + j + 1
             tile, local = chosen[0, at], chosen[1, at]
-            _, field = tile_reader(gathered, tile, total // gathered.shape[0], width)
+            _, field = tile_reader(gathered, tile, tiles, width)
             index_a = jnp.broadcast_to(field(3).astype(jnp.int32), (8, width))
             index_b = jnp.broadcast_to(field(4).astype(jnp.int32), (8, width))
             grad = values[local, 0:8, :]
@@ -235,7 +234,9 @@
                 rows = values[local, 8 + 8 * c : 16 + 8 * c, :]
                 half = 0.5 * field(c)
                 found = found + half * (pick(rows, index_a) + pick(rows, index_b))
-            out[tile] = found
+            device, t = parts_of(tile, tiles)
+            pair, core = parts_of(device, CORES)
+            out[(pair // NEAR * CORES + core) * tiles + t] = found
         return carry
 
     lax.fori_loop(0, (chosen[0, 0] + GROUP - 1) // GROUP, step, 0)
@@ -244,8 +245,8 @@
 def back(chosen, gathered, values, tiles):
     width = values.shape[2]
     return pl.pallas_call(
-        back_kernel,
-        out_shape=held((gathered.shape[0] * tiles, 8, width)),
+        functools.partial(back_kernel, tiles=tiles),
+        out_shape=held((gathered.shape[0] // NEAR * tiles, 8, width)),
         in_specs=[smem_spec, vmem_spec, vmem_spec],
         out_specs=vmem_spec,
         name="back",
@@ -352,6 +353,7 @@
 
 TEAM = ("section", "core")
 HEIGHT = ("far", "near")
+TEAMS = ("section", "near", "core")
 
 
 def body(
@@ -378,20 +380,18 @@
     cls = lax.axis_index(TEAM).astype(jnp.int32).reshape(1)
     parity = lax.axis_index("near").astype(jnp.int32).reshape(1)
     own = pack(tile_owner[:, 0], node_slot, residual, tangents, edge_nodes, far * NEAR * CORES)
-    other = lax.ppermute(own, "near", [(0, 1), (1, 0)])
-    gathered = lax.all_gather(own, TEAM)
-    gathered_other = lax.all_gather(other, TEAM)
+    gathered = lax.all_gather(own, TEAMS)
 
     smoothed, rim = smooth(diag_kind, diag_coeff, halo_rows, residual, inverse_tiles)
     slabs = lax.axis_size("slab")
     low = lax.ppermute(rim, "slab", [(i, i + 1) for i in range(slabs - 1)])
     high = lax.ppermute(rim, "slab", [(i + 1, i) for i in range(slabs - 1)])
 
-    sums = node_sums(cls, parity, gathered, gathered_other, tiles, width, far * node_tiles)
+    sums = node_sums(cls, parity, gathered, tiles, width, far * node_tiles)
     sums = sums.reshape(far, node_tiles * 32, width)
     arrived = lax.all_to_all(sums, "far", split_axis=0, concat_axis=0, tiled=True)
 
-    chosen = class_list(cls, gathered, tiles, width)
+    chosen = class_list(cls, parity, gathered, tiles, width)
     smoothed_twice = smooth_again(
         diag_kind, diag_coeff, tile_cols, tile_kinds, tile_coeff,
         smoothed, low, high, residual, coupling_tiles, inverse_tiles,

time: 98 us -> 96.6 us (0.986)
  blocking collectives: 51.5 us -> 54.7 us
  starting transfers between devices: 28.1 us -> 25 us
  waiting for transfers between devices: 6.96 us -> 5.31 us
    ppermute x1 -> x0, starting transfers between devices: 3.83 us -> none  [body(): other = lax.ppermute(own, 'near', [(0, 1), (1, 0)])]
    all_gather x1, blocking collectives: 29.5 us -> 31.1 us  [body(): values = lax.all_gather(solved, HEIGHT, tiled=True)]
    all_to_all x1, waiting for transfers between devices: 6.61 us -> 5.2 us  [body(): lax.all_to_all(sums, 'far', split_axis=0, concat_axis=0, tiled=True)]
    all_gather x2 -> x1, blocking collectives: 13.6 us -> 14.7 us  [body(): gathered = lax.all_gather(own, TEAMS)]
  transfers between devices with their start and end apart: 4 -> 3, of which waited for: 2 -> 2; matrix products, arithmetic and copies ran while one was open for 0% -> 0% of each run, Pallas kernels for 5% -> 5%
where the time goes in v11:
time: 96.6 us; the launch traced here: 94.9 us
  blocking collectives  54.7 us (57%)
  starting transfers between devices  25 us (26%)
  Pallas kernels  9.73 us (10%)
  waiting for transfers between devices  5.31 us (5%)
    all_gather x1, blocking collectives, body(): values = lax.all_gather(solved, HEIGHT, tiled=True)  31.1 us
    all_to_all x1, starting transfers between devices, body(): lax.all_to_all(sums, 'far', split_axis=0, concat_axis=0, tiled=True)  15.4 us
    all_gather x1, blocking collectives, body(): gathered = lax.all_gather(own, TEAMS)  14.7 us
    all_to_all x1, blocking collectives, body(): lax.all_to_all(corrections, TEAM, split_axis=0, concat_axis=0, tiled=True)  8.98 us
    ppermute x1, starting transfers between devices, body(): low = lax.ppermute(rim, 'slab', [(i, i + 1) for i in range(slabs - 1)])  7.27 us
    all_to_all x1, waiting for transfers between devices, body(): lax.all_to_all(sums, 'far', split_axis=0, concat_axis=0, tiled=True)  5.2 us
    ppermute x1, starting transfers between devices, body(): high = lax.ppermute(rim, 'slab', [(i + 1, i) for i in range(slabs - 1)])  2.32 us
    pallas_call x1, Pallas kernels, node_sums(): pl.pallas_call(functools.partial(sums_kernel, tiles=tiles, width=width),...  2.26 us
  transfers between devices with their start and end apart: 3, of which 2 were waited for; matrix products, arithmetic and copies ran while one was open for 0% of the time, Pallas kernels for 5%

profile of v11, /device:TPU:24, one launch (start us, length us, event | category | flops | bytes accessed | tf_op | source)
XLA Modules:
  0.0 94.9 jit_solution(12076649225665278195)
XLA Ops:
  0.0 0.9 pack.1
  0.9 14.7 %all-gather = f32[64,3456]{1,0:T(8,128)S(1)} all-gather(f32[8,3456]{1,0:T(8,128)S(1)} %pack.1), channel_id=2, replica_groups=mesh['section'=2,'far'=8,'near'=2,'core'=2,'slab'=8] {'section','near','..., dimensions={0}, use_global_device_ids=true | all-gather | bytes 995328 | tf_op jit(solution)/shard_map/all_gather | solution.py:383
  15.6 0.0 copy-start.1
  15.6 2.3 %node_sums.1 = f32[16,32,128]{2,1,0:T(8,128)} custom-call(s32[1]{0:T(128)} %bitcast.cls, s32[1]{0:T(128)} %bitcast.1.parity, f32[8,8,3456]{2,1,0:T(8,128)S(1)} %bitcast.7), custom_call_target="tpu_custom_call" | custom-call | tf_op jit(solution)/shard_map/node_sums/pallas_call | solution.py:167
  17.9 15.4 %all-to-all-start = ((f32[8,64,128]{2,1,0:T(8,128)}), f32[8,64,128]{2,1,0:T(8,128)S(1)}, u32[]{:S(2)}, u32[]{:S(2)}) async-start(f32[8,64,128]{2,1,0:T(8,128)} %bitcast.4), calls=%async_computation | async-start | bytes 524288 | tf_op jit(solution)/shard_map/all_to_all | solution.py:392
  33.3 0.0 copy-done.1
  33.3 0.0 copy-done
  33.3 1.2 %smooth_once.1 = (f32[16,8,128]{2,1,0:T(8,128)S(1)}, f32[2,8,128]{2,1,0:T(8,128)S(1)}) custom-call(s32[16]{0:T(128)} %kind.3, f32[16]{0:T(128)} %coeff.3, s32[2]{0:T(128)} %halo.1, f32[8,2048]{1,0:T(8,128)S(1)} %copy-done.1, f32[8,128,128]{2,1,0:T(8,128)S(1)} %copy-done), custom_call_target="tpu_custom_call" | custom-call | tf_op jit(solution)/shard_map/smooth_once/pallas_call | solution.py:274
  34.4 0.0 copy-start.2
  34.5 2.3 %collective-permute-start.1 = (f32[2,8,128]{2,1,0:T(8,128)S(1)}, f32[2,8,128]{2,1,0:T(8,128)S(1)}, u32[]{:S(2)}, u32[]{:S(2)}) collective-permute-start(f32[2,8,128]{2,1,0:T(8,128)S(1)} %get-tuple-element.11), channel_id=1, source_target_pairs={{1,0},{2,1},{3,2},{4,3},{5,4},{6,5},{7,6},{9,8},{10,9},{11,10},{12... | collective-permute-start | bytes 24584 | tf_op jit(solution)/shard_map/ppermute | solution.py:388
  36.8 7.3 %collective-permute-start = (f32[2,8,128]{2,1,0:T(8,128)S(1)}, f32[2,8,128]{2,1,0:T(8,128)S(1)}, u32[]{:S(2)}, u32[]{:S(2)}) collective-permute-start(f32[2,8,128]{2,1,0:T(8,128)S(1)} %get-tuple-element.11), channel_id=1, source_target_pairs={{0,1},{1,2},{2,3},{3,4},{4,5},{5,6},{6,7},{8,9},{9,10},{10,11},{11... | collective-permute-start | bytes 24584 | tf_op jit(solution)/shard_map/ppermute | solution.py:387
  44.1 1.2 %class_list.1.chosen = s32[2,137]{1,0:T(2,128)} custom-call(s32[1]{0:T(128)} %bitcast.cls, s32[1]{0:T(128)} %bitcast.1.parity, f32[8,8,3456]{2,1,0:T(8,128)S(1)} %bitcast.8), custom_call_target="tpu_custom_call" | custom-call | tf_op jit(solution)/shard_map/class_list/pallas_call | solution.py:188
  45.3 0.0 collective-permute-done.1.high
  45.3 0.1 collective-permute-done.low
  45.4 0.0 copy-done.2
  45.4 2.2 %smooth_again.1.smoothed = f32[16,8,128]{2,1,0:T(8,128)S(1)} custom-call(s32[16]{0:T(128)} %kind.3, f32[16]{0:T(128)} %coeff.3, s32[8,16]{1,0:T(8,128)} %cols.1, s32[8,16]{1,0:T(8,128)} %kinds.1, f32[8,16]{1,0:T(8,128)} %coeffs.1, f32[16,8,128]{2,1,0:T(8,128)S(1)} %get-tuple-element.10.smoothed, f32[2,8,128]{2,1,0:T(8,128)S(1)} %collective-permute-done.low, ...), custom_call_target="tpu_custom_call" | custom-call | tf_op jit(solution)/shard_map/smooth_again/pallas_call | solution.py:318
  47.6 5.2 %all-to-all-done = f32[8,64,128]{2,1,0:T(8,128)S(1)} async-done(((f32[8,64,128]{2,1,0:T(8,128)}), f32[8,64,128]{2,1,0:T(8,128)S(1)}, u32[]{:S(2)}, u32[]{:S(2)}) %all-to-all-start) | async-done | bytes 262176 | tf_op jit(solution)/shard_map/all_to_all | solution.py:392
  52.8 0.0 copy-done.3
  52.8 0.0 copy-done.4
  52.8 0.2 solve.1
  53.0 31.1 %all_gather.11.values = f32[32,32,128]{2,1,0:T(8,128)S(1)} all-gather(f32[2,32,128]{2,1,0:T(8,128)S(1)} %solve.1), channel_id=1, replica_groups=mesh['section'=2,'far'=8,'near'=2,'core'=2,'slab'=8] {'far','near'}, dimensions={0}, use_global_device_ids=true | all-gather | bytes 557056 | tf_op jit(solution)/shard_map/all_gather | solution.py:402
  84.1 1.1 %back.1 = f32[64,8,128]{2,1,0:T(8,128)S(1)} custom-call(s32[2,137]{1,0:T(2,128)} %class_list.1.chosen, f32[8,8,3456]{2,1,0:T(8,128)S(1)} %bitcast.9, f32[32,32,128]{2,1,0:T(8,128)S(1)} %all_gather.11.values), custom_call_target="tpu_custom_call" | custom-call | tf_op jit(solution)/shard_map/back/pallas_call | solution.py:247
  85.2 9.0 %all_to_all.10.pieces = f32[4,16,8,128]{3,2,1,0:T(8,128)S(1)} all-to-all(f32[4,16,8,128]{3,2,1,0:T(8,128)S(1)} %bitcast.10), channel_id=1, replica_groups=mesh['section'=2,'far'=8,'near'=2,'core'=2,'slab'=8] {'section','core'}, dimensions={0} | all-to-all | bytes 524288 | tf_op jit(solution)/shard_map/all_to_all | solution.py:404
  94.2 0.6 finish.1
  (3 shorter events, 0.0 us)
Async XLA Ops:
  15.6 17.7 %copy-start.1 = (f32[8,2048]{1,0:T(8,128)S(1)}, f32[8,2048]{1,0:T(8,128)}, u32[]{:S(2)}) copy-start(f32[8,2048]{1,0:T(8,128)} %residual.5) | copy-start | bytes 196612
  17.9 15.4 %copy-start = (f32[8,128,128]{2,1,0:T(8,128)S(1)}, f32[8,128,128]{2,1,0:T(8,128)}, u32[]{:S(2)}) copy-start(f32[8,128,128]{2,1,0:T(8,128)} %inverse.3) | copy-start | bytes 1572868
  17.9 34.9 %all-to-all-start = ((f32[8,64,128]{2,1,0:T(8,128)}), f32[8,64,128]{2,1,0:T(8,128)S(1)}, u32[]{:S(2)}, u32[]{:S(2)}) async-start(f32[8,64,128]{2,1,0:T(8,128)} %bitcast.4), calls=%async_computation | async-start | bytes 524288 | tf_op jit(solution)/shard_map/all_to_all | solution.py:392
  34.4 11.0 %copy-start.2 = (f32[8,128,128]{2,1,0:T(8,128)S(1)}, f32[8,128,128]{2,1,0:T(8,128)}, u32[]{:S(2)}) copy-start(f32[8,128,128]{2,1,0:T(8,128)} %coupling.1) | copy-start | bytes 1572868
  34.5 10.8 %collective-permute-start.1 = (f32[2,8,128]{2,1,0:T(8,128)S(1)}, f32[2,8,128]{2,1,0:T(8,128)S(1)}, u32[]{:S(2)}, u32[]{:S(2)}) collective-permute-start(f32[2,8,128]{2,1,0:T(8,128)S(1)} %get-tuple-element.11), channel_id=1, source_target_pairs={{1,0},{2,1},{3,2},{4,3},{5,4},{6,5},{7,6},{9,8},{10,9},{11,10},{12... | collective-permute-start | bytes 24584 | tf_op jit(solution)/shard_map/ppermute | solution.py:388
  36.8 8.6 %collective-permute-start = (f32[2,8,128]{2,1,0:T(8,128)S(1)}, f32[2,8,128]{2,1,0:T(8,128)S(1)}, u32[]{:S(2)}, u32[]{:S(2)}) collective-permute-start(f32[2,8,128]{2,1,0:T(8,128)S(1)} %get-tuple-element.11), channel_id=1, source_target_pairs={{0,1},{1,2},{2,3},{3,4},{4,5},{5,6},{6,7},{8,9},{9,10},{10,11},{11... | collective-permute-start | bytes 24584 | tf_op jit(solution)/shard_map/ppermute | solution.py:387
  45.4 7.4 %copy-start.3 = (f32[2,128,128]{2,1,0:T(8,128)S(1)}, f32[2,128,128]{2,1,0:T(8,128)}, u32[]{:S(2)}) copy-start(f32[2,128,128]{2,1,0:T(8,128)} %grad.1) | copy-start | bytes 393220
  45.4 7.4 %copy-start.4 = (f32[2,128,128]{2,1,0:T(8,128)S(1)}, f32[2,128,128]{2,1,0:T(8,128)}, u32[]{:S(2)}) copy-start(f32[2,128,128]{2,1,0:T(8,128)} %vec.1) | copy-start | bytes 393220

commit v12 on v11

--- a/solution.py
+++ b/solution.py
@@ -178,7 +178,7 @@
     mine = cls[0].astype(F32)
 
     def rule(q, classes, places):
-        beside = jnp.where(parity[0] == (q // CORES) % NEAR, mine, -1.0)
+        beside = jnp.where(parity[0] == q // (gathered.shape[0] // NEAR), mine, -1.0)
         return jnp.where(classes == beside, places, -1)
 
     choose(chosen, gathered, tiles, width, rule)
@@ -234,9 +234,8 @@
                 rows = values[local, 8 + 8 * c : 16 + 8 * c, :]
                 half = 0.5 * field(c)
                 found = found + half * (pick(rows, index_a) + pick(rows, index_b))
-            device, t = parts_of(tile, tiles)
-            pair, core = parts_of(device, CORES)
-            out[(pair // NEAR * CORES + core) * tiles + t] = found
+            _, place = parts_of(tile, out.shape[0])
+            out[place] = found
         return carry
 
     lax.fori_loop(0, (chosen[0, 0] + GROUP - 1) // GROUP, step, 0)
@@ -353,7 +352,7 @@
 
 TEAM = ("section", "core")
 HEIGHT = ("far", "near")
-TEAMS = ("section", "near", "core")
+TEAMS = ("near", "section", "core")
 
 
 def body(

time: 96.6 us -> 95.1 us (0.984)
  waiting for transfers between devices: 5.31 us -> 7.64 us
  blocking collectives: 54.7 us -> 52.4 us
    all_to_all x1, waiting for transfers between devices: 5.2 us -> 7.53 us  [body(): lax.all_to_all(sums, 'far', split_axis=0, concat_axis=0, tiled=True)]
    all_gather x1, blocking collectives: 31.1 us -> 29.5 us  [body(): values = lax.all_gather(solved, HEIGHT, tiled=True)]
where the time goes in v12:
time: 95.1 us; the launch traced here: 94.2 us
  blocking collectives  52.4 us (55%)
  starting transfers between devices  24.1 us (25%)
  Pallas kernels  9.94 us (10%)
  waiting for transfers between devices  7.64 us (8%)
    all_gather x1, blocking collectives, body(): values = lax.all_gather(solved, HEIGHT, tiled=True)  29.5 us
    all_to_all x1, starting transfers between devices, body(): lax.all_to_all(sums, 'far', split_axis=0, concat_axis=0, tiled=True)  14.5 us
    all_gather x1, blocking collectives, body(): gathered = lax.all_gather(own, TEAMS)  14.3 us
    all_to_all x1, blocking collectives, body(): lax.all_to_all(corrections, TEAM, split_axis=0, concat_axis=0, tiled=True)  8.53 us
    all_to_all x1, waiting for transfers between devices, body(): lax.all_to_all(sums, 'far', split_axis=0, concat_axis=0, tiled=True)  7.53 us
    ppermute x1, starting transfers between devices, body(): low = lax.ppermute(rim, 'slab', [(i, i + 1) for i in range(slabs - 1)])  6.8 us
    ppermute x1, starting transfers between devices, body(): high = lax.ppermute(rim, 'slab', [(i + 1, i) for i in range(slabs - 1)])  2.78 us
    pallas_call x1, Pallas kernels, node_sums(): pl.pallas_call(functools.partial(sums_kernel, tiles=tiles, width=width),...  2.26 us
  transfers between devices with their start and end apart: 3, of which 2 were waited for; matrix products, arithmetic and copies ran while one was open for 0% of the time, Pallas kernels for 5%

profile of v12, /device:TPU:24, one launch (start us, length us, event | category | flops | bytes accessed | tf_op | source)
XLA Modules:
  0.0 94.2 jit_solution(12634751979929570264)
XLA Ops:
  0.0 0.9 pack.1
  0.9 14.3 %all-gather = f32[64,3456]{1,0:T(8,128)S(1)} all-gather(f32[8,3456]{1,0:T(8,128)S(1)} %pack.1), channel_id=2, replica_groups=mesh['section'=2,'far'=8,'near'=2,'core'=2,'slab'=8] {'near','section','..., dimensions={0}, use_global_device_ids=true | all-gather | bytes 995328 | tf_op jit(solution)/shard_map/all_gather | solution.py:382
  15.2 0.0 copy-start.1
  15.2 2.3 %node_sums.1 = f32[16,32,128]{2,1,0:T(8,128)} custom-call(s32[1]{0:T(128)} %bitcast.cls, s32[1]{0:T(128)} %bitcast.1.parity, f32[8,8,3456]{2,1,0:T(8,128)S(1)} %bitcast.7), custom_call_target="tpu_custom_call" | custom-call | tf_op jit(solution)/shard_map/node_sums/pallas_call | solution.py:167
  17.5 14.5 %all-to-all-start = ((f32[8,64,128]{2,1,0:T(8,128)}), f32[8,64,128]{2,1,0:T(8,128)S(1)}, u32[]{:S(2)}, u32[]{:S(2)}) async-start(f32[8,64,128]{2,1,0:T(8,128)} %bitcast.4), calls=%async_computation | async-start | bytes 524288 | tf_op jit(solution)/shard_map/all_to_all | solution.py:391
  32.0 0.0 copy-done.1
  32.0 0.0 copy-done
  32.1 1.2 %smooth_once.1 = (f32[16,8,128]{2,1,0:T(8,128)S(1)}, f32[2,8,128]{2,1,0:T(8,128)S(1)}) custom-call(s32[16]{0:T(128)} %kind.3, f32[16]{0:T(128)} %coeff.3, s32[2]{0:T(128)} %halo.1, f32[8,2048]{1,0:T(8,128)S(1)} %copy-done.1, f32[8,128,128]{2,1,0:T(8,128)S(1)} %copy-done), custom_call_target="tpu_custom_call" | custom-call | tf_op jit(solution)/shard_map/smooth_once/pallas_call | solution.py:273
  33.2 0.0 copy-start.2
  33.2 2.8 %collective-permute-start.1 = (f32[2,8,128]{2,1,0:T(8,128)S(1)}, f32[2,8,128]{2,1,0:T(8,128)S(1)}, u32[]{:S(2)}, u32[]{:S(2)}) collective-permute-start(f32[2,8,128]{2,1,0:T(8,128)S(1)} %get-tuple-element.11), channel_id=1, source_target_pairs={{1,0},{2,1},{3,2},{4,3},{5,4},{6,5},{7,6},{9,8},{10,9},{11,10},{12... | collective-permute-start | bytes 24584 | tf_op jit(solution)/shard_map/ppermute | solution.py:387
  36.0 6.8 %collective-permute-start = (f32[2,8,128]{2,1,0:T(8,128)S(1)}, f32[2,8,128]{2,1,0:T(8,128)S(1)}, u32[]{:S(2)}, u32[]{:S(2)}) collective-permute-start(f32[2,8,128]{2,1,0:T(8,128)S(1)} %get-tuple-element.11), channel_id=1, source_target_pairs={{0,1},{1,2},{2,3},{3,4},{4,5},{5,6},{6,7},{8,9},{9,10},{10,11},{11... | collective-permute-start | bytes 24584 | tf_op jit(solution)/shard_map/ppermute | solution.py:386
  42.8 1.2 %class_list.1.chosen = s32[2,137]{1,0:T(2,128)} custom-call(s32[1]{0:T(128)} %bitcast.cls, s32[1]{0:T(128)} %bitcast.1.parity, f32[8,8,3456]{2,1,0:T(8,128)S(1)} %bitcast.8), custom_call_target="tpu_custom_call" | custom-call | tf_op jit(solution)/shard_map/class_list/pallas_call | solution.py:188
  44.1 0.0 collective-permute-done.1.high
  44.1 0.1 collective-permute-done.low
  44.2 0.0 copy-done.2
  44.2 2.2 %smooth_again.1.smoothed = f32[16,8,128]{2,1,0:T(8,128)S(1)} custom-call(s32[16]{0:T(128)} %kind.3, f32[16]{0:T(128)} %coeff.3, s32[8,16]{1,0:T(8,128)} %cols.1, s32[8,16]{1,0:T(8,128)} %kinds.1, f32[8,16]{1,0:T(8,128)} %coeffs.1, f32[16,8,128]{2,1,0:T(8,128)S(1)} %get-tuple-element.10.smoothed, f32[2,8,128]{2,1,0:T(8,128)S(1)} %collective-permute-done.low, ...), custom_call_target="tpu_custom_call" | custom-call | tf_op jit(solution)/shard_map/smooth_again/pallas_call | solution.py:317
  46.4 7.5 %all-to-all-done = f32[8,64,128]{2,1,0:T(8,128)S(1)} async-done(((f32[8,64,128]{2,1,0:T(8,128)}), f32[8,64,128]{2,1,0:T(8,128)S(1)}, u32[]{:S(2)}, u32[]{:S(2)}) %all-to-all-start) | async-done | bytes 262176 | tf_op jit(solution)/shard_map/all_to_all | solution.py:391
  53.9 0.0 copy-done.3
  53.9 0.0 copy-done.4
  53.9 0.2 solve.1
  54.2 29.5 %all_gather.11.values = f32[32,32,128]{2,1,0:T(8,128)S(1)} all-gather(f32[2,32,128]{2,1,0:T(8,128)S(1)} %solve.1), channel_id=1, replica_groups=mesh['section'=2,'far'=8,'near'=2,'core'=2,'slab'=8] {'far','near'}, dimensions={0}, use_global_device_ids=true | all-gather | bytes 557056 | tf_op jit(solution)/shard_map/all_gather | solution.py:401
  83.7 1.3 %back.1 = f32[64,8,128]{2,1,0:T(8,128)S(1)} custom-call(s32[2,137]{1,0:T(2,128)} %class_list.1.chosen, f32[8,8,3456]{2,1,0:T(8,128)S(1)} %bitcast.9, f32[32,32,128]{2,1,0:T(8,128)S(1)} %all_gather.11.values), custom_call_target="tpu_custom_call" | custom-call | tf_op jit(solution)/shard_map/back/pallas_call | solution.py:246
  85.0 8.5 %all_to_all.10.pieces = f32[4,16,8,128]{3,2,1,0:T(8,128)S(1)} all-to-all(f32[4,16,8,128]{3,2,1,0:T(8,128)S(1)} %bitcast.10), channel_id=1, replica_groups=mesh['section'=2,'far'=8,'near'=2,'core'=2,'slab'=8] {'section','core'}, dimensions={0} | all-to-all | bytes 524288 | tf_op jit(solution)/shard_map/all_to_all | solution.py:403
  93.5 0.6 finish.1
  (3 shorter events, 0.0 us)
Async XLA Ops:
  15.2 16.8 %copy-start.1 = (f32[8,2048]{1,0:T(8,128)S(1)}, f32[8,2048]{1,0:T(8,128)}, u32[]{:S(2)}) copy-start(f32[8,2048]{1,0:T(8,128)} %residual.5) | copy-start | bytes 196612
  17.5 14.5 %copy-start = (f32[8,128,128]{2,1,0:T(8,128)S(1)}, f32[8,128,128]{2,1,0:T(8,128)}, u32[]{:S(2)}) copy-start(f32[8,128,128]{2,1,0:T(8,128)} %inverse.3) | copy-start | bytes 1572868
  17.5 36.4 %all-to-all-start = ((f32[8,64,128]{2,1,0:T(8,128)}), f32[8,64,128]{2,1,0:T(8,128)S(1)}, u32[]{:S(2)}, u32[]{:S(2)}) async-start(f32[8,64,128]{2,1,0:T(8,128)} %bitcast.4), calls=%async_computation | async-start | bytes 524288 | tf_op jit(solution)/shard_map/all_to_all | solution.py:391
  33.2 11.0 %copy-start.2 = (f32[8,128,128]{2,1,0:T(8,128)S(1)}, f32[8,128,128]{2,1,0:T(8,128)}, u32[]{:S(2)}) copy-start(f32[8,128,128]{2,1,0:T(8,128)} %coupling.1) | copy-start | bytes 1572868
  33.2 10.8 %collective-permute-start.1 = (f32[2,8,128]{2,1,0:T(8,128)S(1)}, f32[2,8,128]{2,1,0:T(8,128)S(1)}, u32[]{:S(2)}, u32[]{:S(2)}) collective-permute-start(f32[2,8,128]{2,1,0:T(8,128)S(1)} %get-tuple-element.11), channel_id=1, source_target_pairs={{1,0},{2,1},{3,2},{4,3},{5,4},{6,5},{7,6},{9,8},{10,9},{11,10},{12... | collective-permute-start | bytes 24584 | tf_op jit(solution)/shard_map/ppermute | solution.py:387
  36.0 8.2 %collective-permute-start = (f32[2,8,128]{2,1,0:T(8,128)S(1)}, f32[2,8,128]{2,1,0:T(8,128)S(1)}, u32[]{:S(2)}, u32[]{:S(2)}) collective-permute-start(f32[2,8,128]{2,1,0:T(8,128)S(1)} %get-tuple-element.11), channel_id=1, source_target_pairs={{0,1},{1,2},{2,3},{3,4},{4,5},{5,6},{6,7},{8,9},{9,10},{10,11},{11... | collective-permute-start | bytes 24584 | tf_op jit(solution)/shard_map/ppermute | solution.py:386
  44.2 9.7 %copy-start.3 = (f32[2,128,128]{2,1,0:T(8,128)S(1)}, f32[2,128,128]{2,1,0:T(8,128)}, u32[]{:S(2)}) copy-start(f32[2,128,128]{2,1,0:T(8,128)} %grad.1) | copy-start | bytes 393220
  44.2 9.7 %copy-start.4 = (f32[2,128,128]{2,1,0:T(8,128)S(1)}, f32[2,128,128]{2,1,0:T(8,128)}, u32[]{:S(2)}) copy-start(f32[2,128,128]{2,1,0:T(8,128)} %vec.1) | copy-start | bytes 393220

commit v13 on v12

--- a/solution.py
+++ b/solution.py
@@ -10,7 +10,7 @@
 DAMPING = 0.7
 CORES = 2
 NEAR = 2
-GROUP = 8
+GROUP = 16
 F32 = jnp.float32
 BF16 = jnp.bfloat16
 SMEM = pltpu.SMEM

time: 95.1 us -> 94.6 us (level)
  no operation moved by 1% of the time
where the time goes in v13:
time: 94.6 us; the launch traced here: 94 us
  blocking collectives  52.8 us (56%)
  starting transfers between devices  24.1 us (25%)
  Pallas kernels  9.54 us (10%)
  waiting for transfers between devices  7.41 us (8%)
    all_gather x1, blocking collectives, body(): values = lax.all_gather(solved, HEIGHT, tiled=True)  29.4 us
    all_to_all x1, starting transfers between devices, body(): lax.all_to_all(sums, 'far', split_axis=0, concat_axis=0, tiled=True)  14.5 us
    all_gather x1, blocking collectives, body(): gathered = lax.all_gather(own, TEAMS)  14.3 us
    all_to_all x1, blocking collectives, body(): lax.all_to_all(corrections, TEAM, split_axis=0, concat_axis=0, tiled=True)  9.15 us
    all_to_all x1, waiting for transfers between devices, body(): lax.all_to_all(sums, 'far', split_axis=0, concat_axis=0, tiled=True)  7.32 us
    ppermute x1, starting transfers between devices, body(): low = lax.ppermute(rim, 'slab', [(i, i + 1) for i in range(slabs - 1)])  6.01 us
    ppermute x1, starting transfers between devices, body(): high = lax.ppermute(rim, 'slab', [(i + 1, i) for i in range(slabs - 1)])  3.57 us
    pallas_call x1, Pallas kernels, node_sums(): pl.pallas_call(functools.partial(sums_kernel, tiles=tiles, width=width),...  2.15 us
  transfers between devices with their start and end apart: 3, of which 2 were waited for; matrix products, arithmetic and copies ran while one was open for 0% of the time, Pallas kernels for 5%

profile of v13, /device:TPU:24, one launch (start us, length us, event | category | flops | bytes accessed | tf_op | source)
XLA Modules:
  0.0 94.0 jit_solution(13009644938146110981)
XLA Ops:
  0.0 0.9 pack.1
  0.9 14.3 %all-gather = f32[64,3456]{1,0:T(8,128)S(1)} all-gather(f32[8,3456]{1,0:T(8,128)S(1)} %pack.1), channel_id=2, replica_groups=mesh['section'=2,'far'=8,'near'=2,'core'=2,'slab'=8] {'near','section','..., dimensions={0}, use_global_device_ids=true | all-gather | bytes 995328 | tf_op jit(solution)/shard_map/all_gather | solution.py:382
  15.2 0.0 copy-start.1
  15.2 2.2 %node_sums.1 = f32[16,32,128]{2,1,0:T(8,128)} custom-call(s32[1]{0:T(128)} %bitcast.cls, s32[1]{0:T(128)} %bitcast.1.parity, f32[8,8,3456]{2,1,0:T(8,128)S(1)} %bitcast.7), custom_call_target="tpu_custom_call" | custom-call | tf_op jit(solution)/shard_map/node_sums/pallas_call | solution.py:167
  17.4 14.5 %all-to-all-start = ((f32[8,64,128]{2,1,0:T(8,128)}), f32[8,64,128]{2,1,0:T(8,128)S(1)}, u32[]{:S(2)}, u32[]{:S(2)}) async-start(f32[8,64,128]{2,1,0:T(8,128)} %bitcast.4), calls=%async_computation | async-start | bytes 524288 | tf_op jit(solution)/shard_map/all_to_all | solution.py:391
  31.9 0.0 copy-done.1
  31.9 0.0 copy-done
  32.0 1.2 %smooth_once.1 = (f32[16,8,128]{2,1,0:T(8,128)S(1)}, f32[2,8,128]{2,1,0:T(8,128)S(1)}) custom-call(s32[16]{0:T(128)} %kind.3, f32[16]{0:T(128)} %coeff.3, s32[2]{0:T(128)} %halo.1, f32[8,2048]{1,0:T(8,128)S(1)} %copy-done.1, f32[8,128,128]{2,1,0:T(8,128)S(1)} %copy-done), custom_call_target="tpu_custom_call" | custom-call | tf_op jit(solution)/shard_map/smooth_once/pallas_call | solution.py:273
  33.1 0.0 copy-start.2
  33.1 3.6 %collective-permute-start.1 = (f32[2,8,128]{2,1,0:T(8,128)S(1)}, f32[2,8,128]{2,1,0:T(8,128)S(1)}, u32[]{:S(2)}, u32[]{:S(2)}) collective-permute-start(f32[2,8,128]{2,1,0:T(8,128)S(1)} %get-tuple-element.11), channel_id=1, source_target_pairs={{1,0},{2,1},{3,2},{4,3},{5,4},{6,5},{7,6},{9,8},{10,9},{11,10},{12... | collective-permute-start | bytes 24584 | tf_op jit(solution)/shard_map/ppermute | solution.py:387
  36.7 6.0 %collective-permute-start = (f32[2,8,128]{2,1,0:T(8,128)S(1)}, f32[2,8,128]{2,1,0:T(8,128)S(1)}, u32[]{:S(2)}, u32[]{:S(2)}) collective-permute-start(f32[2,8,128]{2,1,0:T(8,128)S(1)} %get-tuple-element.11), channel_id=1, source_target_pairs={{0,1},{1,2},{2,3},{3,4},{4,5},{5,6},{6,7},{8,9},{9,10},{10,11},{11... | collective-permute-start | bytes 24584 | tf_op jit(solution)/shard_map/ppermute | solution.py:386
  42.7 1.2 %class_list.1.chosen = s32[2,145]{1,0:T(2,128)} custom-call(s32[1]{0:T(128)} %bitcast.cls, s32[1]{0:T(128)} %bitcast.1.parity, f32[8,8,3456]{2,1,0:T(8,128)S(1)} %bitcast.8), custom_call_target="tpu_custom_call" | custom-call | tf_op jit(solution)/shard_map/class_list/pallas_call | solution.py:188
  44.0 0.0 collective-permute-done.1.high
  44.0 0.1 collective-permute-done.low
  44.1 0.0 copy-done.2
  44.1 2.2 %smooth_again.1.smoothed = f32[16,8,128]{2,1,0:T(8,128)S(1)} custom-call(s32[16]{0:T(128)} %kind.3, f32[16]{0:T(128)} %coeff.3, s32[8,16]{1,0:T(8,128)} %cols.1, s32[8,16]{1,0:T(8,128)} %kinds.1, f32[8,16]{1,0:T(8,128)} %coeffs.1, f32[16,8,128]{2,1,0:T(8,128)S(1)} %get-tuple-element.10.smoothed, f32[2,8,128]{2,1,0:T(8,128)S(1)} %collective-permute-done.low, ...), custom_call_target="tpu_custom_call" | custom-call | tf_op jit(solution)/shard_map/smooth_again/pallas_call | solution.py:317
  46.2 7.3 %all-to-all-done = f32[8,64,128]{2,1,0:T(8,128)S(1)} async-done(((f32[8,64,128]{2,1,0:T(8,128)}), f32[8,64,128]{2,1,0:T(8,128)S(1)}, u32[]{:S(2)}, u32[]{:S(2)}) %all-to-all-start) | async-done | bytes 262176 | tf_op jit(solution)/shard_map/all_to_all | solution.py:391
  53.6 0.0 copy-done.3
  53.6 0.0 copy-done.4
  53.6 0.2 solve.1
  53.8 29.4 %all_gather.11.values = f32[32,32,128]{2,1,0:T(8,128)S(1)} all-gather(f32[2,32,128]{2,1,0:T(8,128)S(1)} %solve.1), channel_id=1, replica_groups=mesh['section'=2,'far'=8,'near'=2,'core'=2,'slab'=8] {'far','near'}, dimensions={0}, use_global_device_ids=true | all-gather | bytes 557056 | tf_op jit(solution)/shard_map/all_gather | solution.py:401
  83.2 1.0 %back.1 = f32[64,8,128]{2,1,0:T(8,128)S(1)} custom-call(s32[2,145]{1,0:T(2,128)} %class_list.1.chosen, f32[8,8,3456]{2,1,0:T(8,128)S(1)} %bitcast.9, f32[32,32,128]{2,1,0:T(8,128)S(1)} %all_gather.11.values), custom_call_target="tpu_custom_call" | custom-call | tf_op jit(solution)/shard_map/back/pallas_call | solution.py:246
  84.2 9.1 %all_to_all.10.pieces = f32[4,16,8,128]{3,2,1,0:T(8,128)S(1)} all-to-all(f32[4,16,8,128]{3,2,1,0:T(8,128)S(1)} %bitcast.10), channel_id=1, replica_groups=mesh['section'=2,'far'=8,'near'=2,'core'=2,'slab'=8] {'section','core'}, dimensions={0} | all-to-all | bytes 524288 | tf_op jit(solution)/shard_map/all_to_all | solution.py:403
  93.4 0.6 finish.1
  (3 shorter events, 0.0 us)
Async XLA Ops:
  15.2 16.7 %copy-start.1 = (f32[8,2048]{1,0:T(8,128)S(1)}, f32[8,2048]{1,0:T(8,128)}, u32[]{:S(2)}) copy-start(f32[8,2048]{1,0:T(8,128)} %residual.5) | copy-start | bytes 196612
  17.4 14.5 %copy-start = (f32[8,128,128]{2,1,0:T(8,128)S(1)}, f32[8,128,128]{2,1,0:T(8,128)}, u32[]{:S(2)}) copy-start(f32[8,128,128]{2,1,0:T(8,128)} %inverse.3) | copy-start | bytes 1572868
  17.4 36.2 %all-to-all-start = ((f32[8,64,128]{2,1,0:T(8,128)}), f32[8,64,128]{2,1,0:T(8,128)S(1)}, u32[]{:S(2)}, u32[]{:S(2)}) async-start(f32[8,64,128]{2,1,0:T(8,128)} %bitcast.4), calls=%async_computation | async-start | bytes 524288 | tf_op jit(solution)/shard_map/all_to_all | solution.py:391
  33.1 11.0 %copy-start.2 = (f32[8,128,128]{2,1,0:T(8,128)S(1)}, f32[8,128,128]{2,1,0:T(8,128)}, u32[]{:S(2)}) copy-start(f32[8,128,128]{2,1,0:T(8,128)} %coupling.1) | copy-start | bytes 1572868
  33.1 10.9 %collective-permute-start.1 = (f32[2,8,128]{2,1,0:T(8,128)S(1)}, f32[2,8,128]{2,1,0:T(8,128)S(1)}, u32[]{:S(2)}, u32[]{:S(2)}) collective-permute-start(f32[2,8,128]{2,1,0:T(8,128)S(1)} %get-tuple-element.11), channel_id=1, source_target_pairs={{1,0},{2,1},{3,2},{4,3},{5,4},{6,5},{7,6},{9,8},{10,9},{11,10},{12... | collective-permute-start | bytes 24584 | tf_op jit(solution)/shard_map/ppermute | solution.py:387
  36.7 7.4 %collective-permute-start = (f32[2,8,128]{2,1,0:T(8,128)S(1)}, f32[2,8,128]{2,1,0:T(8,128)S(1)}, u32[]{:S(2)}, u32[]{:S(2)}) collective-permute-start(f32[2,8,128]{2,1,0:T(8,128)S(1)} %get-tuple-element.11), channel_id=1, source_target_pairs={{0,1},{1,2},{2,3},{3,4},{4,5},{5,6},{6,7},{8,9},{9,10},{10,11},{11... | collective-permute-start | bytes 24584 | tf_op jit(solution)/shard_map/ppermute | solution.py:386
  44.1 9.5 %copy-start.3 = (f32[2,128,128]{2,1,0:T(8,128)S(1)}, f32[2,128,128]{2,1,0:T(8,128)}, u32[]{:S(2)}) copy-start(f32[2,128,128]{2,1,0:T(8,128)} %grad.1) | copy-start | bytes 393220
  44.1 9.5 %copy-start.4 = (f32[2,128,128]{2,1,0:T(8,128)S(1)}, f32[2,128,128]{2,1,0:T(8,128)}, u32[]{:S(2)}) copy-start(f32[2,128,128]{2,1,0:T(8,128)} %vec.1) | copy-start | bytes 393220

commit v14 on v13

--- a/solution.py
+++ b/solution.py
@@ -10,7 +10,7 @@
 DAMPING = 0.7
 CORES = 2
 NEAR = 2
-GROUP = 16
+GROUP = 12
 F32 = jnp.float32
 BF16 = jnp.bfloat16
 SMEM = pltpu.SMEM

time: 94.6 us -> 95 us (level)
  waiting for transfers between devices: 7.41 us -> 6.4 us
    all_gather x1, blocking collectives: 29.4 us -> 30.6 us  [body(): values = lax.all_gather(solved, HEIGHT, tiled=True)]
    all_to_all x1, waiting for transfers between devices: 7.32 us -> 6.3 us  [body(): lax.all_to_all(sums, 'far', split_axis=0, concat_axis=0, tiled=True)]
where the time goes in v14:
time: 95 us; the launch traced here: 93.7 us
  blocking collectives  53.5 us (56%)
  starting transfers between devices  24.1 us (25%)
  Pallas kernels  9.56 us (10%)
  waiting for transfers between devices  6.4 us (7%)
    all_gather x1, blocking collectives, body(): values = lax.all_gather(solved, HEIGHT, tiled=True)  30.6 us
    all_to_all x1, starting transfers between devices, body(): lax.all_to_all(sums, 'far', split_axis=0, concat_axis=0, tiled=True)  14.5 us
    all_gather x1, blocking collectives, body(): gathered = lax.all_gather(own, TEAMS)  14.3 us
    all_to_all x1, blocking collectives, body(): lax.all_to_all(corrections, TEAM, split_axis=0, concat_axis=0, tiled=True)  8.51 us
    all_to_all x1, waiting for transfers between devices, body(): lax.all_to_all(sums, 'far', split_axis=0, concat_axis=0, tiled=True)  6.3 us
    ppermute x1, starting transfers between devices, body(): low = lax.ppermute(rim, 'slab', [(i, i + 1) for i in range(slabs - 1)])  6.18 us
    ppermute x1, starting transfers between devices, body(): high = lax.ppermute(rim, 'slab', [(i + 1, i) for i in range(slabs - 1)])  3.41 us
    pallas_call x1, Pallas kernels, smooth_again(): pl.pallas_call(again_kernel, out_shape=held((tiles, 8, width)), in_specs=...  2.14 us
  transfers between devices with their start and end apart: 3, of which 2 were waited for; matrix products, arithmetic and copies ran while one was open for 0% of the time, Pallas kernels for 5%

profile of v14, /device:TPU:24, one launch (start us, length us, event | category | flops | bytes accessed | tf_op | source)
XLA Modules:
  0.0 93.7 jit_solution(8114967067127548437)
XLA Ops:
  0.0 0.9 pack.1
  0.9 14.3 %all-gather = f32[64,3456]{1,0:T(8,128)S(1)} all-gather(f32[8,3456]{1,0:T(8,128)S(1)} %pack.1), channel_id=2, replica_groups=mesh['section'=2,'far'=8,'near'=2,'core'=2,'slab'=8] {'near','section','..., dimensions={0}, use_global_device_ids=true | all-gather | bytes 995328 | tf_op jit(solution)/shard_map/all_gather | solution.py:382
  15.2 0.0 copy-start.1
  15.2 2.0 %node_sums.1 = f32[16,32,128]{2,1,0:T(8,128)} custom-call(s32[1]{0:T(128)} %bitcast.cls, s32[1]{0:T(128)} %bitcast.1.parity, f32[8,8,3456]{2,1,0:T(8,128)S(1)} %bitcast.7), custom_call_target="tpu_custom_call" | custom-call | tf_op jit(solution)/shard_map/node_sums/pallas_call | solution.py:167
  17.2 14.5 %all-to-all-start = ((f32[8,64,128]{2,1,0:T(8,128)}), f32[8,64,128]{2,1,0:T(8,128)S(1)}, u32[]{:S(2)}, u32[]{:S(2)}) async-start(f32[8,64,128]{2,1,0:T(8,128)} %bitcast.4), calls=%async_computation | async-start | bytes 524288 | tf_op jit(solution)/shard_map/all_to_all | solution.py:391
  31.8 0.0 copy-done.1
  31.8 0.0 copy-done
  31.8 1.2 %smooth_once.1 = (f32[16,8,128]{2,1,0:T(8,128)S(1)}, f32[2,8,128]{2,1,0:T(8,128)S(1)}) custom-call(s32[16]{0:T(128)} %kind.3, f32[16]{0:T(128)} %coeff.3, s32[2]{0:T(128)} %halo.1, f32[8,2048]{1,0:T(8,128)S(1)} %copy-done.1, f32[8,128,128]{2,1,0:T(8,128)S(1)} %copy-done), custom_call_target="tpu_custom_call" | custom-call | tf_op jit(solution)/shard_map/smooth_once/pallas_call | solution.py:273
  33.0 0.0 copy-start.2
  33.0 3.4 %collective-permute-start.1 = (f32[2,8,128]{2,1,0:T(8,128)S(1)}, f32[2,8,128]{2,1,0:T(8,128)S(1)}, u32[]{:S(2)}, u32[]{:S(2)}) collective-permute-start(f32[2,8,128]{2,1,0:T(8,128)S(1)} %get-tuple-element.11), channel_id=1, source_target_pairs={{1,0},{2,1},{3,2},{4,3},{5,4},{6,5},{7,6},{9,8},{10,9},{11,10},{12... | collective-permute-start | bytes 24584 | tf_op jit(solution)/shard_map/ppermute | solution.py:387
  36.4 6.2 %collective-permute-start = (f32[2,8,128]{2,1,0:T(8,128)S(1)}, f32[2,8,128]{2,1,0:T(8,128)S(1)}, u32[]{:S(2)}, u32[]{:S(2)}) collective-permute-start(f32[2,8,128]{2,1,0:T(8,128)S(1)} %get-tuple-element.11), channel_id=1, source_target_pairs={{0,1},{1,2},{2,3},{3,4},{4,5},{5,6},{6,7},{8,9},{9,10},{10,11},{11... | collective-permute-start | bytes 24584 | tf_op jit(solution)/shard_map/ppermute | solution.py:386
  42.6 1.2 %class_list.1.chosen = s32[2,141]{1,0:T(2,128)} custom-call(s32[1]{0:T(128)} %bitcast.cls, s32[1]{0:T(128)} %bitcast.1.parity, f32[8,8,3456]{2,1,0:T(8,128)S(1)} %bitcast.8), custom_call_target="tpu_custom_call" | custom-call | tf_op jit(solution)/shard_map/class_list/pallas_call | solution.py:188
  43.8 0.0 collective-permute-done.1.high
  43.8 0.1 collective-permute-done.low
  43.9 0.0 copy-done.2
  43.9 2.1 %smooth_again.1.smoothed = f32[16,8,128]{2,1,0:T(8,128)S(1)} custom-call(s32[16]{0:T(128)} %kind.3, f32[16]{0:T(128)} %coeff.3, s32[8,16]{1,0:T(8,128)} %cols.1, s32[8,16]{1,0:T(8,128)} %kinds.1, f32[8,16]{1,0:T(8,128)} %coeffs.1, f32[16,8,128]{2,1,0:T(8,128)S(1)} %get-tuple-element.10.smoothed, f32[2,8,128]{2,1,0:T(8,128)S(1)} %collective-permute-done.low, ...), custom_call_target="tpu_custom_call" | custom-call | tf_op jit(solution)/shard_map/smooth_again/pallas_call | solution.py:317
  46.1 6.3 %all-to-all-done = f32[8,64,128]{2,1,0:T(8,128)S(1)} async-done(((f32[8,64,128]{2,1,0:T(8,128)}), f32[8,64,128]{2,1,0:T(8,128)S(1)}, u32[]{:S(2)}, u32[]{:S(2)}) %all-to-all-start) | async-done | bytes 262176 | tf_op jit(solution)/shard_map/all_to_all | solution.py:391
  52.4 0.0 copy-done.3
  52.4 0.0 copy-done.4
  52.4 0.2 solve.1
  52.6 30.6 %all_gather.11.values = f32[32,32,128]{2,1,0:T(8,128)S(1)} all-gather(f32[2,32,128]{2,1,0:T(8,128)S(1)} %solve.1), channel_id=1, replica_groups=mesh['section'=2,'far'=8,'near'=2,'core'=2,'slab'=8] {'far','near'}, dimensions={0}, use_global_device_ids=true | all-gather | bytes 557056 | tf_op jit(solution)/shard_map/all_gather | solution.py:401
  83.3 1.2 %back.1 = f32[64,8,128]{2,1,0:T(8,128)S(1)} custom-call(s32[2,141]{1,0:T(2,128)} %class_list.1.chosen, f32[8,8,3456]{2,1,0:T(8,128)S(1)} %bitcast.9, f32[32,32,128]{2,1,0:T(8,128)S(1)} %all_gather.11.values), custom_call_target="tpu_custom_call" | custom-call | tf_op jit(solution)/shard_map/back/pallas_call | solution.py:246
  84.5 8.5 %all_to_all.10.pieces = f32[4,16,8,128]{3,2,1,0:T(8,128)S(1)} all-to-all(f32[4,16,8,128]{3,2,1,0:T(8,128)S(1)} %bitcast.10), channel_id=1, replica_groups=mesh['section'=2,'far'=8,'near'=2,'core'=2,'slab'=8] {'section','core'}, dimensions={0} | all-to-all | bytes 524288 | tf_op jit(solution)/shard_map/all_to_all | solution.py:403
  93.0 0.6 finish.1
  (3 shorter events, 0.0 us)
Async XLA Ops:
  15.2 16.5 %copy-start.1 = (f32[8,2048]{1,0:T(8,128)S(1)}, f32[8,2048]{1,0:T(8,128)}, u32[]{:S(2)}) copy-start(f32[8,2048]{1,0:T(8,128)} %residual.5) | copy-start | bytes 196612
  17.2 14.5 %copy-start = (f32[8,128,128]{2,1,0:T(8,128)S(1)}, f32[8,128,128]{2,1,0:T(8,128)}, u32[]{:S(2)}) copy-start(f32[8,128,128]{2,1,0:T(8,128)} %inverse.3) | copy-start | bytes 1572868
  17.2 35.1 %all-to-all-start = ((f32[8,64,128]{2,1,0:T(8,128)}), f32[8,64,128]{2,1,0:T(8,128)S(1)}, u32[]{:S(2)}, u32[]{:S(2)}) async-start(f32[8,64,128]{2,1,0:T(8,128)} %bitcast.4), calls=%async_computation | async-start | bytes 524288 | tf_op jit(solution)/shard_map/all_to_all | solution.py:391
  33.0 11.0 %copy-start.2 = (f32[8,128,128]{2,1,0:T(8,128)S(1)}, f32[8,128,128]{2,1,0:T(8,128)}, u32[]{:S(2)}) copy-start(f32[8,128,128]{2,1,0:T(8,128)} %coupling.1) | copy-start | bytes 1572868
  33.0 10.8 %collective-permute-start.1 = (f32[2,8,128]{2,1,0:T(8,128)S(1)}, f32[2,8,128]{2,1,0:T(8,128)S(1)}, u32[]{:S(2)}, u32[]{:S(2)}) collective-permute-start(f32[2,8,128]{2,1,0:T(8,128)S(1)} %get-tuple-element.11), channel_id=1, source_target_pairs={{1,0},{2,1},{3,2},{4,3},{5,4},{6,5},{7,6},{9,8},{10,9},{11,10},{12... | collective-permute-start | bytes 24584 | tf_op jit(solution)/shard_map/ppermute | solution.py:387
  36.4 7.5 %collective-permute-start = (f32[2,8,128]{2,1,0:T(8,128)S(1)}, f32[2,8,128]{2,1,0:T(8,128)S(1)}, u32[]{:S(2)}, u32[]{:S(2)}) collective-permute-start(f32[2,8,128]{2,1,0:T(8,128)S(1)} %get-tuple-element.11), channel_id=1, source_target_pairs={{0,1},{1,2},{2,3},{3,4},{4,5},{5,6},{6,7},{8,9},{9,10},{10,11},{11... | collective-permute-start | bytes 24584 | tf_op jit(solution)/shard_map/ppermute | solution.py:386
  43.9 8.5 %copy-start.3 = (f32[2,128,128]{2,1,0:T(8,128)S(1)}, f32[2,128,128]{2,1,0:T(8,128)}, u32[]{:S(2)}) copy-start(f32[2,128,128]{2,1,0:T(8,128)} %grad.1) | copy-start | bytes 393220
  43.9 8.5 %copy-start.4 = (f32[2,128,128]{2,1,0:T(8,128)S(1)}, f32[2,128,128]{2,1,0:T(8,128)}, u32[]{:S(2)}) copy-start(f32[2,128,128]{2,1,0:T(8,128)} %vec.1) | copy-start | bytes 393220
